TPU v7x, 512 devices: a whole 4x8x8 slice. The times are simulated.
512 devices in a mesh: dp: 32 (over y_lo, z), mp: 16 (over x, y_hi, core).
Axes of the slice: x: 4, y: 8 (y_hi: 2, y_lo: 4; y = y_hi * 4 + y_lo), z: 8, core: 2. Of those that a mesh axis runs over, the one named last changes fastest.
Arguments:
- queries: bfloat16 [4096, 4096], P('dp', 'mp'), may hold values from -64 to 64
- database: bfloat16 [16384, 896], P('dp'), may hold values from -9 to 9
- key_weight: bfloat16 [896, 4096], P(None, 'mp'), may hold values from -1 to 2
- value_weight: bfloat16 [896, 4096], P(None, 'mp'), may hold values from -0.1875 to 0.1875
- out_weight: bfloat16 [4096, 8192], P('mp', 'dp'), may hold values from -0.1875 to 0.1875
- neighbours: int32 [64, 2], P('dp'), may hold values from 0 to 127, as said below
Outputs:
- mixed: bfloat16 [4096, 8192], P('dp', 'mp')
Inputs may be any that keep to these rules, and one draw needn't show every extreme that they name: neighbours[c, n] names block neighbours[c, n] % 4 of database shard neighbours[c, n] // 4; among the 4 neighbours of the spans 2 * i to 2 * i + 1, no two lie in the same shard.
All inputs are finite; a program needn't handle non-finite values.
Results may differ from a plain program's by a relative error of at most 0.018.
Values may be sent and summed in bfloat16 or wider, within the bound.
No kernel may reach another device: no remote copies, remote signals or barrier semaphores. Data moves between devices by JAX's collectives and lax.ppermute only.
A program may use at most 64 MiB of HBM per device.

v0:
```python
import math

import jax
import jax.numpy as jnp
from jax import lax
from jax.sharding import PartitionSpec as P

HEAD_DIM = 128
SPAN = 64
NEIGH = 2
NROW = 128
BLK_DEV = 4


def on_device(queries, database, key_weight, value_weight, out_weight, neighbours):
    shard_count = lax.axis_size("dp")
    span_count = neighbours.shape[0]
    inner_width = key_weight.shape[1]
    enc_width = database.shape[1]
    head_count = inner_width // HEAD_DIM
    flat_ids = neighbours.reshape(-1)
    shard_of = flat_ids // BLK_DEV
    local_of = flat_ids % BLK_DEV
    matches = shard_of[None, :] == jnp.arange(shard_count, dtype=jnp.int32)[:, None]
    wanted = jnp.sum(jnp.where(matches, local_of[None, :], 0), axis=1).reshape(shard_count, 1)
    requested = lax.all_to_all(wanted, "dp", split_axis=0, concat_axis=0, tiled=True)
    stored = database.reshape(BLK_DEV, NROW, enc_width)
    outgoing = stored[requested[:, 0]]
    arrived = lax.all_to_all(outgoing, "dp", split_axis=0, concat_axis=0, tiled=True)
    encoded_rows = arrived[shard_of].reshape(-1, enc_width)
    near_keys = jnp.dot(encoded_rows, key_weight, preferred_element_type=jnp.float32).astype(
        jnp.bfloat16
    )
    near_values = jnp.dot(encoded_rows, value_weight, preferred_element_type=jnp.float32).astype(
        jnp.bfloat16
    )
    key_blocks = near_keys.reshape(span_count, NEIGH * NROW, head_count, HEAD_DIM)
    value_blocks = near_values.reshape(span_count, NEIGH * NROW, head_count, HEAD_DIM)
    query_blocks = queries.reshape(span_count, SPAN, head_count, HEAD_DIM)
    scores = jnp.einsum(
        "cqhd,ckhd->chqk", query_blocks, key_blocks, preferred_element_type=jnp.float32
    )
    scores = scores / math.sqrt(HEAD_DIM)
    weights = jax.nn.softmax(scores, axis=-1).astype(jnp.bfloat16)
    attended = jnp.einsum(
        "chqk,ckhd->cqhd", weights, value_blocks, preferred_element_type=jnp.float32
    )
    attended = attended.astype(jnp.bfloat16).reshape(span_count * SPAN, inner_width)
    partial_terms = jnp.dot(
        attended,
        lax.all_gather(out_weight, "dp", axis=1, tiled=True),
        preferred_element_type=jnp.float32,
    )
    return lax.psum_scatter(
        partial_terms.astype(jnp.bfloat16), "mp", scatter_dimension=1, tiled=True
    )


def solution(mesh):
    in_specs = (
        P("dp", "mp"),
        P("dp", None),
        P(None, "mp"),
        P(None, "mp"),
        P("mp", "dp"),
        P("dp", None),
    )
    out_specs = P("dp", "mp")
    return jax.shard_map(
        on_device, mesh=mesh, in_specs=in_specs, out_specs=out_specs, check_vma=False
    )
```

profile of v0, /device:TPU:8, one launch (start us, length us, event | category | flops | bytes accessed | tf_op | source)
XLA Modules:
  0.0 458.7 jit_solution(4644224904882574688)
XLA Ops:
  6.5 0.0 copy-start
  6.5 0.8 reshape.185
  7.4 0.1 select_reduce_fusion
  7.5 0.1 copy.24
  7.6 22.7 %all_to_all.17 = s32[32,1,1]{2,1,0:T(1,128)S(1)} all-to-all(s32[32,1,1]{2,1,0:T(1,128)S(1)} %copy.24), channel_id=1, replica_groups=mesh['dp'=32,'mp'=16] {'dp'}, dimensions={0} | all-to-all | bytes 256 | tf_op jit(solution)/shard_map/all_to_all | solution.py:26
  30.2 0.7 reduce
  30.9 0.0 copy-done
  30.9 4.4 gather_fusion
  35.3 0.0 copy-start.4
  35.3 0.0 copy-start.1
  35.3 0.0 copy-start.2
  35.3 6.1 %all-to-all-start.1 = ((bf16[32,128,896]{2,1,0:T(8,128)(2,1)}), bf16[32,128,896]{2,1,0:T(8,128)(2,1)}, u32[]{:S(2)}, u32[]{:S(2)}) async-start(bf16[32,128,896]{2,1,0:T(8,128)(2,1)} %gather_fusion), calls=%async_computation.1 | async-start | bytes 14680064 | tf_op jit(solution)/shard_map/all_to_all | solution.py:29
  41.5 0.0 copy-start.3
  41.5 0.0 all-gather.2.cloned.1.call-start
  41.5 0.7 all-gather.2.cloned.1.call-update
  42.2 0.0 reduce-scatter.2.cloned.1.call-start
  42.3 0.0 copy-done.4
  42.3 0.1 reshape.186
  42.4 0.0 copy-done.1
  42.4 223.8 %all-to-all-done.1 = bf16[32,128,896]{2,1,0:T(8,128)(2,1)} async-done(((bf16[32,128,896]{2,1,0:T(8,128)(2,1)}), bf16[32,128,896]{2,1,0:T(8,128)(2,1)}, u32[]{:S(2)}, u32[]{:S(2)}) %all-to-all-start.1) | async-done | bytes 7340064 | tf_op jit(solution)/shard_map/all_to_all | solution.py:29
  266.2 3.8 gather_fusion.1
  270.0 0.0 copy-done.2
  270.0 0.4 convolution_convert_fusion.1
  270.4 0.1 reshape.189
  270.5 0.0 copy-done.3
  270.5 0.4 convolution_convert_fusion.2
  271.0 0.1 reshape.188
  271.0 0.2 fusion.2
  271.2 0.2 fusion.14
  271.4 0.5 fusion.4
  272.0 0.1 copy.28
  272.0 68.9 %all-gather.2.cloned.1.call-done = bf16[256,8192]{1,0:T(8,128)(2,1)} async-done(((bf16[256,256]{1,0:T(8,128)(2,1)}), bf16[256,8192]{1,0:T(8,128)(2,1)}) %all-gather.2.cloned.1.call-update) | async-done | bytes 4194320 | tf_op jit(solution)/shard_map/all_gather | solution.py:51
  341.0 4.3 convolution_convert_fusion
  345.2 0.0 reduce-scatter.2.cloned.1.call-update
  345.2 106.6 %reduce-scatter.2.cloned.1.call-done = bf16[128,512]{1,0:T(8,128)(2,1)} async-done(((bf16[128,8192]{1,0:T(8,128)(2,1)}), bf16[128,512]{1,0:T(8,128)(2,1)}) %reduce-scatter.2.cloned.1.call-update) | async-done | bytes 131088 | tf_op jit(solution)/shard_map/reduce_scatter | solution.py:54
  (6 shorter events, 0.1 us)
Async XLA Ops:
  6.5 24.4 %copy-start = (bf16[512,896]{1,0:T(8,128)(2,1)S(1)}, bf16[512,896]{1,0:T(8,128)(2,1)}, u32[]{:S(2)}) copy-start(bf16[512,896]{1,0:T(8,128)(2,1)} %param.7) | copy-start | bytes 2752516
  35.3 6.9 %copy-start.4 = (s32[2,2]{1,0:T(2,128)S(1)}, s32[2,2]{1,0:T(2,128)}, u32[]{:S(2)}) copy-start(s32[2,2]{1,0:T(2,128)} %param.11) | copy-start | bytes 52
  35.3 7.0 %copy-start.1 = (bf16[128,256]{1,0:T(8,128)(2,1)S(1)}, bf16[128,256]{1,0:T(8,128)(2,1)}, u32[]{:S(2)}) copy-start(bf16[128,256]{1,0:T(8,128)(2,1)} %param.6) | copy-start | bytes 196612
  35.3 234.6 %copy-start.2 = (bf16[896,256]{1,0:T(8,128)(2,1)S(1)}, bf16[896,256]{1,0:T(8,128)(2,1)}, u32[]{:S(2)}) copy-start(bf16[896,256]{1,0:T(8,128)(2,1)} %param.8) | copy-start | bytes 1376260
  35.3 230.9 %all-to-all-start.1 = ((bf16[32,128,896]{2,1,0:T(8,128)(2,1)}), bf16[32,128,896]{2,1,0:T(8,128)(2,1)}, u32[]{:S(2)}, u32[]{:S(2)}) async-start(bf16[32,128,896]{2,1,0:T(8,128)(2,1)} %gather_fusion), calls=%async_computation.1 | async-start | bytes 14680064 | tf_op jit(solution)/shard_map/all_to_all | solution.py:29
  41.5 229.0 %copy-start.3 = (bf16[896,256]{1,0:T(8,128)(2,1)S(1)}, bf16[896,256]{1,0:T(8,128)(2,1)}, u32[]{:S(2)}) copy-start(bf16[896,256]{1,0:T(8,128)(2,1)} %param.9) | copy-start | bytes 1376260
  41.5 299.5 %all-gather.2.cloned.1.call-start = ((), (), s32[]{:S(2)}) async-start(), calls=%async_computation.3 | async-start | bytes 4325376 | tf_op jit(solution)/shard_map/all_gather | solution.py:51
  42.2 409.6 %reduce-scatter.2.cloned.1.call-start = ((), (), s32[]{:S(2)}) async-start(), calls=%async_computation.4 | async-start | bytes 2228224 | tf_op jit(solution)/shard_map/reduce_scatter | solution.py:54
Sparse Core Ops, SparseCore 0:
  44.3 296.5 all-gather.1
  345.8 106.0 reduce-scatter.1
where the time goes:
time: 460 us; the launch traced here: 459 us
  waiting for transfers between devices  400 us (87%)
  blocking collectives  22.7 us (5%)
  between operations  13.5 us (3%)
  local copies, waits for them, and re-layouts  9.45 us (2%)
  starting transfers between devices  6.21 us (1%)
  matrix products  5.85 us (1%)
    all_to_all x1, waiting for transfers between devices, on_device(): lax.all_to_all(outgoing, 'dp', split_axis=0, concat_axis=0, tiled=True)  224 us
    reduce_scatter x1, waiting for transfers between devices, on_device(): lax.psum_scatter(partial_terms.astype(jnp.bfloat16), 'mp', scatter_dimens...  107 us
    all_gather x1, waiting for transfers between devices, on_device(): lax.all_gather(out_weight, 'dp', axis=1, tiled=True)  68.9 us
    all_to_all x1, blocking collectives, on_device(): lax.all_to_all(wanted, 'dp', split_axis=0, concat_axis=0, tiled=True)  22.7 us
  transfers between devices with their start and end apart: 3, of which 3 were waited for; matrix products, arithmetic and copies ran while one was open for 1% of the time, Pallas kernels for 0%

commit v1 on v0

v1 whole, which is shorter than its diff:
```python
import math

import jax
import jax.numpy as jnp
from jax import lax
from jax.sharding import PartitionSpec as P

HEAD_DIM = 128
SPAN = 64
NEIGH = 2
NROW = 128
BLK_DEV = 4


def weight_blocks(out_weight):
    dp_count = lax.axis_size("dp")
    mp_count = lax.axis_size("mp")
    ratio = dp_count // mp_count
    moves = []
    for d in range(dp_count):
        for m in range(mp_count):
            target = ((d % ratio) * mp_count + m) * mp_count + d // ratio
            moves.append((d * mp_count + m, target))
    return lax.ppermute(out_weight, ("dp", "mp"), moves)


def weight_columns(moved):
    gathered = lax.all_gather(moved, "dp", axis=0, tiled=True)
    mp_count = lax.axis_size("mp")
    return gathered.reshape(-1, mp_count * moved.shape[0], moved.shape[1])


def near_rows(database, neighbours):
    dp_count = lax.axis_size("dp")
    mp_count = lax.axis_size("mp")
    own_shard = lax.axis_index("dp")
    part = lax.axis_index("mp")
    part_rows = NROW // mp_count
    enc_width = database.shape[1]
    per_owner = neighbours.size
    ids = lax.all_gather(neighbours, "dp", axis=0, tiled=True).reshape(dp_count, per_owner)
    mine = ids // BLK_DEV == own_shard
    wanted = jnp.sum(jnp.where(mine, ids % BLK_DEV, 0), axis=1).reshape(dp_count, 1, 1)
    stored = lax.dynamic_slice(
        database.reshape(BLK_DEV, NROW, enc_width),
        (0, part * part_rows, 0),
        (BLK_DEV, part_rows, enc_width),
    )
    outgoing = stored[0][None]
    for block in range(1, BLK_DEV):
        outgoing = jnp.where(wanted == block, stored[block][None], outgoing)
    outgoing = jnp.broadcast_to(outgoing, (dp_count, part_rows, enc_width))
    arrived = lax.all_to_all(outgoing, "dp", split_axis=0, concat_axis=0, tiled=True)
    shard_of = neighbours.reshape(-1) // BLK_DEV
    chosen = [
        lax.dynamic_slice(arrived, (shard_of[j], 0, 0), (1, part_rows, enc_width))
        for j in range(per_owner)
    ]
    chosen = jnp.concatenate(chosen, axis=0)
    gathered = lax.all_gather(chosen, "mp", axis=0)
    gathered = gathered.reshape(mp_count, per_owner // NEIGH, NEIGH * part_rows, enc_width)
    return gathered.transpose(1, 0, 2, 3).reshape(-1, enc_width)


def on_device(queries, database, key_weight, value_weight, out_weight, neighbours):
    span_count = neighbours.shape[0]
    inner_width = key_weight.shape[1]
    head_count = inner_width // HEAD_DIM
    moved = weight_blocks(out_weight)
    database, moved = lax.optimization_barrier((database, moved))
    columns = weight_columns(moved)
    encoded_rows = near_rows(database, neighbours)
    near_keys = jnp.dot(encoded_rows, key_weight, preferred_element_type=jnp.float32).astype(
        jnp.bfloat16
    )
    near_values = jnp.dot(encoded_rows, value_weight, preferred_element_type=jnp.float32).astype(
        jnp.bfloat16
    )
    key_blocks = near_keys.reshape(span_count, NEIGH * NROW, head_count, HEAD_DIM)
    value_blocks = near_values.reshape(span_count, NEIGH * NROW, head_count, HEAD_DIM)
    query_blocks = queries.reshape(span_count, SPAN, head_count, HEAD_DIM)
    scores = jnp.einsum(
        "cqhd,ckhd->chqk", query_blocks, key_blocks, preferred_element_type=jnp.float32
    )
    scores = scores / math.sqrt(HEAD_DIM)
    weights = jax.nn.softmax(scores, axis=-1).astype(jnp.bfloat16)
    attended = jnp.einsum(
        "chqk,ckhd->cqhd", weights, value_blocks, preferred_element_type=jnp.float32
    )
    attended = attended.astype(jnp.bfloat16).reshape(span_count * SPAN, inner_width)
    attended, columns = lax.optimization_barrier((attended, columns))
    attended = lax.all_gather(attended, "mp", axis=1, tiled=True)
    parts = [
        jnp.dot(attended, columns[k], preferred_element_type=jnp.float32)
        for k in range(columns.shape[0])
    ]
    return jnp.concatenate(parts, axis=1).astype(jnp.bfloat16)


def solution(mesh):
    in_specs = (
        P("dp", "mp"),
        P("dp", None),
        P(None, "mp"),
        P(None, "mp"),
        P("mp", "dp"),
        P("dp", None),
    )
    out_specs = P("dp", "mp")
    return jax.shard_map(
        on_device, mesh=mesh, in_specs=in_specs, out_specs=out_specs, check_vma=False
    )
```

time: 460 us -> 279 us (0.61)
  the two profiles are of different devices: /device:TPU:8 before, /device:TPU:1 now
where the time goes in v1:
time: 279 us; the launch traced here: 278 us
  blocking collectives  140 us (50%)
  waiting for transfers between devices  94.4 us (34%)
  between operations  20.8 us (7%)
  starting transfers between devices  9.44 us (3%)
  matrix products  6.31 us (2%)
  local copies, waits for them, and re-layouts  4.8 us (2%)
    all_gather x1, blocking collectives, near_rows(): lax.all_gather(neighbours, 'dp', axis=0, tiled=True)  79.7 us
    all_gather x1, waiting for transfers between devices, on_device(): attended = lax.all_gather(attended, 'mp', axis=1, tiled=True)  77.1 us
    all_gather x1, blocking collectives, near_rows(): gathered = lax.all_gather(chosen, 'mp', axis=0)  60.6 us
    ppermute x1, waiting for transfers between devices, weight_blocks(): return lax.ppermute(out_weight, ('dp', 'mp'), moves)  13.6 us
  transfers between devices with their start and end apart: 4, of which 4 were waited for; matrix products, arithmetic and copies ran while one was open for 3% of the time, Pallas kernels for 0%

profile of v1, /device:TPU:1, one launch (start us, length us, event | category | flops | bytes accessed | tf_op | source)
XLA Modules:
  0.0 278.1 jit_solution(13490782136744343003)
XLA Ops:
  6.5 0.0 copy-start
  6.5 0.0 copy-start.2
  6.5 0.0 all-gather.5.cloned.1.call-start
  6.5 5.5 %collective-permute-start = (bf16[256,256]{1,0:T(8,128)(2,1)}, bf16[256,256]{1,0:T(8,128)(2,1)S(1)}, u32[]{:S(2)}, u32[]{:S(2)}) collective-permute-start(bf16[256,256]{1,0:T(8,128)(2,1)} %param.10), channel_id=1, source_target_pairs={{0,0},{1,16},{2,32},{3,48},{4,64},{5,80},{6,96},{7,112},{8,128},{9... | collective-permute-start | bytes 393224 | tf_op jit(solution)/shard_map/ppermute | solution.py:24
  12.1 13.6 %collective-permute-done = bf16[256,256]{1,0:T(8,128)(2,1)S(1)} collective-permute-done((bf16[256,256]{1,0:T(8,128)(2,1)}, bf16[256,256]{1,0:T(8,128)(2,1)S(1)}, u32[]{:S(2)}, u32[]{:S(2)}) %collective-permute-start) | collective-permute-done | bytes 131104 | tf_op jit(solution)/shard_map/ppermute | solution.py:24
  25.7 0.0 copy-start.1
  25.7 0.7 copy-done.1
  26.3 0.0 all-gather.5.cloned.1.call-update
  26.4 79.7 %all-gather.1 = s32[32,2,2]{2,1,0:T(2,128)S(1)} all-gather(s32[1,2,2]{2,1,0:T(2,128)} %bitcast.54), channel_id=1, replica_groups=mesh['dp'=32,'mp'=16] {'dp'}, dimensions={0}, use_global_device_ids=true | all-gather | bytes 528 | tf_op jit(solution)/shard_map/all_gather | solution.py:41
  106.0 0.1 copy.28
  106.1 0.1 reduce_sum.26
  106.3 0.1 reduce_sum.27
  106.4 0.8 dynamic-slice_bitcast_fusion.3
  107.2 1.0 select_select_fusion
  108.1 3.9 %all-to-all-start = ((bf16[32,8,896]{2,1,0:T(8,128)(2,1)}), bf16[32,8,896]{2,1,0:T(8,128)(2,1)S(1)}, u32[]{:S(2)}, u32[]{:S(2)}) async-start(bf16[32,8,896]{2,1,0:T(8,128)(2,1)} %select_select_fusion), calls=%async_computation | async-start | bytes 917504 | tf_op jit(solution)/shard_map/all_to_all | solution.py:53
  112.0 0.0 all-gather.7.cloned.1.call-start
  112.1 0.8 reshape.45
  112.9 0.7 fusion.23
  118.4 0.9 reshape.50
  121.6 2.2 all-to-all-done
  123.9 60.6 %all-gather = bf16[64,8,896]{2,1,0:T(8,128)(2,1)S(1)} all-gather(bf16[4,8,896]{2,1,0:T(8,128)(2,1)S(1)} %pad_maximum_fusion.1), channel_id=2, replica_groups=mesh['dp'=32,'mp'=16] {'mp'}, dimensions={0}, use_global_device_ids=true | all-gather | bytes 974848 | tf_op jit(solution)/shard_map/all_gather | solution.py:60
  184.5 0.1 copy.23
  184.6 0.0 copy-done
  184.6 0.4 convolution_convert_fusion
  185.0 0.1 reshape.49
  185.1 0.0 copy-done.2
  185.1 0.4 convolution_convert_fusion.1
  185.5 0.1 reshape.48
  185.6 0.2 fusion.8
  185.8 0.2 fusion.24
  186.0 0.5 fusion.16
  186.5 0.1 copy.27
  186.6 0.6 copy.37
  187.3 1.4 all-gather.5.cloned.1.call-done
  188.7 0.0 all-gather.7.cloned.1.call-update
  188.7 77.1 %all-gather.7.cloned.1.call-done = bf16[128,4096]{1,0:T(8,128)(2,1)} async-done(((bf16[128,256]{1,0:T(8,128)(2,1)}), bf16[128,4096]{1,0:T(8,128)(2,1)}) %all-gather.7.cloned.1.call-update) | async-done | bytes 1048592 | tf_op jit(solution)/shard_map/all_gather | solution.py:92
  265.8 2.4 fusion.10
  268.2 2.4 fusion.13
  270.5 0.7 pad_maximum_fusion
  (5 shorter events, 0.1 us)
Async XLA Ops:
  6.5 178.0 %copy-start = (bf16[896,256]{1,0:T(8,128)(2,1)S(1)}, bf16[896,256]{1,0:T(8,128)(2,1)}, u32[]{:S(2)}) copy-start(bf16[896,256]{1,0:T(8,128)(2,1)} %param.8) | copy-start | bytes 1376260
  6.5 178.6 %copy-start.2 = (bf16[896,256]{1,0:T(8,128)(2,1)S(1)}, bf16[896,256]{1,0:T(8,128)(2,1)}, u32[]{:S(2)}) copy-start(bf16[896,256]{1,0:T(8,128)(2,1)} %param.9) | copy-start | bytes 1376260
  6.5 182.1 %all-gather.5.cloned.1.call-start = ((), (), s32[]{:S(2)}) async-start(), calls=%async_computation.1 | async-start | bytes 4325376 | tf_op jit(solution)/shard_map/all_gather | solution.py:28
  6.5 19.1 %collective-permute-start = (bf16[256,256]{1,0:T(8,128)(2,1)}, bf16[256,256]{1,0:T(8,128)(2,1)S(1)}, u32[]{:S(2)}, u32[]{:S(2)}) collective-permute-start(bf16[256,256]{1,0:T(8,128)(2,1)} %param.10), channel_id=1, source_target_pairs={{0,0},{1,16},{2,32},{3,48},{4,64},{5,80},{6,96},{7,112},{8,128},{9... | collective-permute-start | bytes 393224 | tf_op jit(solution)/shard_map/ppermute | solution.py:24
  25.7 0.7 copy-start.1
  108.1 15.7 %all-to-all-start = ((bf16[32,8,896]{2,1,0:T(8,128)(2,1)}), bf16[32,8,896]{2,1,0:T(8,128)(2,1)S(1)}, u32[]{:S(2)}, u32[]{:S(2)}) async-start(bf16[32,8,896]{2,1,0:T(8,128)(2,1)} %select_select_fusion), calls=%async_computation | async-start | bytes 917504 | tf_op jit(solution)/shard_map/all_to_all | solution.py:53
  112.0 153.8 %all-gather.7.cloned.1.call-start = ((), (), s32[]{:S(2)}) async-start(), calls=%async_computation.2 | async-start | bytes 1114112 | tf_op jit(solution)/shard_map/all_gather | solution.py:92
Sparse Core Ops, SparseCore 0:
  26.5 162.1 all-gather.4
  191.8 73.9 all-gather.6

commit v2 on v1

--- a/solution.py
+++ b/solution.py
@@ -30,17 +30,25 @@
     return gathered.reshape(-1, mp_count * moved.shape[0], moved.shape[1])
 
 
+def copies_to_all(block, axis):
+    count = lax.axis_size(axis)
+    copies = jnp.broadcast_to(block[None], (count, *block.shape))
+    return lax.all_to_all(copies, axis, split_axis=0, concat_axis=0, tiled=True)
+
+
 def near_rows(database, neighbours):
     dp_count = lax.axis_size("dp")
     mp_count = lax.axis_size("mp")
-    own_shard = lax.axis_index("dp")
     part = lax.axis_index("mp")
     part_rows = NROW // mp_count
     enc_width = database.shape[1]
     per_owner = neighbours.size
-    ids = lax.all_gather(neighbours, "dp", axis=0, tiled=True).reshape(dp_count, per_owner)
-    mine = ids // BLK_DEV == own_shard
-    wanted = jnp.sum(jnp.where(mine, ids % BLK_DEV, 0), axis=1).reshape(dp_count, 1, 1)
+    flat_ids = neighbours.reshape(1, per_owner)
+    shard_ids = jnp.arange(dp_count, dtype=jnp.int32)[:, None]
+    asked = jnp.sum(jnp.where(flat_ids // BLK_DEV == shard_ids, flat_ids % BLK_DEV, 0), axis=1)
+    wanted = lax.all_to_all(
+        asked.reshape(dp_count, 1), "dp", split_axis=0, concat_axis=0, tiled=True
+    ).reshape(dp_count, 1, 1)
     stored = lax.dynamic_slice(
         database.reshape(BLK_DEV, NROW, enc_width),
         (0, part * part_rows, 0),
@@ -57,7 +65,7 @@
         for j in range(per_owner)
     ]
     chosen = jnp.concatenate(chosen, axis=0)
-    gathered = lax.all_gather(chosen, "mp", axis=0)
+    gathered = copies_to_all(chosen, "mp")
     gathered = gathered.reshape(mp_count, per_owner // NEIGH, NEIGH * part_rows, enc_width)
     return gathered.transpose(1, 0, 2, 3).reshape(-1, enc_width)
 
@@ -88,8 +96,7 @@
         "chqk,ckhd->cqhd", weights, value_blocks, preferred_element_type=jnp.float32
     )
     attended = attended.astype(jnp.bfloat16).reshape(span_count * SPAN, inner_width)
-    attended, columns = lax.optimization_barrier((attended, columns))
-    attended = lax.all_gather(attended, "mp", axis=1, tiled=True)
+    attended = copies_to_all(attended, "mp").transpose(1, 0, 2).reshape(span_count * SPAN, -1)
     parts = [
         jnp.dot(attended, columns[k], preferred_element_type=jnp.float32)
         for k in range(columns.shape[0])

time: 279 us -> 233 us (0.84)
  the two profiles are of different devices: /device:TPU:1 before, /device:TPU:66 now
where the time goes in v2:
time: 233 us; the launch traced here: 232 us
  waiting for transfers between devices  114 us (49%)
  starting transfers between devices  49.7 us (21%)
  blocking collectives  33.2 us (14%)
  between operations  21 us (9%)
  matrix products  5.92 us (3%)
  local copies, waits for them, and re-layouts  5.22 us (2%)
  other arithmetic  3.77 us (2%)
    all_gather x1, waiting for transfers between devices, weight_columns(): gathered = lax.all_gather(moved, 'dp', axis=0, tiled=True)  73.4 us
    all_to_all x1, blocking collectives, copies_to_all(): return lax.all_to_all(copies, axis, split_axis=0, concat_axis=0, tiled=True)  33.2 us
    all_to_all x1, starting transfers between devices, near_rows(): lax.all_to_all(asked.reshape(dp_count, 1), 'dp', split_axis=0, concat_axi...  28.5 us
    all_to_all x1, waiting for transfers between devices, copies_to_all(): return lax.all_to_all(copies, axis, split_axis=0, concat_axis=0, tiled=True)  20 us
    ppermute x1, starting transfers between devices, weight_blocks(): return lax.ppermute(out_weight, ('dp', 'mp'), moves)  11.2 us
    all_to_all x1, waiting for transfers between devices, near_rows(): lax.all_to_all(asked.reshape(dp_count, 1), 'dp', split_axis=0, concat_axi...  8.94 us
    all_to_all x1, waiting for transfers between devices, near_rows(): lax.all_to_all(outgoing, 'dp', split_axis=0, concat_axis=0, tiled=True)  5.93 us
    ppermute x1, waiting for transfers between devices, weight_blocks(): return lax.ppermute(out_weight, ('dp', 'mp'), moves)  5.38 us
  transfers between devices with their start and end apart: 5, of which 5 were waited for; matrix products, arithmetic and copies ran while one was open for 4% of the time, Pallas kernels for 0%

profile of v2, /device:TPU:66, one launch (start us, length us, event | category | flops | bytes accessed | tf_op | source)
XLA Modules:
  0.0 232.5 jit_solution(11024761245459335510)
XLA Ops:
  6.5 0.0 copy-start
  6.5 0.0 copy-start.2
  6.5 0.0 all-gather.2.cloned.1.call-start
  6.5 11.2 %collective-permute-start = (bf16[256,256]{1,0:T(8,128)(2,1)}, bf16[256,256]{1,0:T(8,128)(2,1)S(1)}, u32[]{:S(2)}, u32[]{:S(2)}) collective-permute-start(bf16[256,256]{1,0:T(8,128)(2,1)} %param.10), channel_id=1, source_target_pairs={{0,0},{1,16},{2,32},{3,48},{4,64},{5,80},{6,96},{7,112},{8,128},{9... | collective-permute-start | bytes 393224 | tf_op jit(solution)/shard_map/ppermute | solution.py:24
  17.8 5.4 %collective-permute-done = bf16[256,256]{1,0:T(8,128)(2,1)S(1)} collective-permute-done((bf16[256,256]{1,0:T(8,128)(2,1)}, bf16[256,256]{1,0:T(8,128)(2,1)S(1)}, u32[]{:S(2)}, u32[]{:S(2)}) %collective-permute-start) | collective-permute-done | bytes 131104 | tf_op jit(solution)/shard_map/ppermute | solution.py:24
  23.2 0.0 copy-start.1
  23.2 0.7 copy-done.1
  23.8 0.0 all-gather.2.cloned.1.call-update
  23.8 0.8 reshape.138
  24.6 0.1 select_reduce_fusion
  24.7 0.7 copy.35
  25.4 28.5 %all-to-all-start = ((s32[32,1,1]{2,1,0:T(1,128)}), s32[32,1,1]{2,1,0:T(1,128)S(1)}, u32[]{:S(2)}, u32[]{:S(2)}) async-start(s32[32,1,1]{2,1,0:T(1,128)} %copy.35), calls=%async_computation | async-start | bytes 32768 | tf_op jit(solution)/shard_map/all_to_all | solution.py:49
  53.9 8.9 %all-to-all-done = s32[32,1,1]{2,1,0:T(1,128)S(1)} async-done(((s32[32,1,1]{2,1,0:T(1,128)}), s32[32,1,1]{2,1,0:T(1,128)S(1)}, u32[]{:S(2)}, u32[]{:S(2)}) %all-to-all-start) | async-done | bytes 160 | tf_op jit(solution)/shard_map/all_to_all | solution.py:49
  62.8 1.8 compare_reduce_fusion.2
  64.6 0.8 dynamic-slice_bitcast_fusion.3
  65.4 1.0 select_select_fusion
  66.4 0.0 copy-start.3
  66.4 5.1 %all-to-all-start.1 = ((bf16[32,8,896]{2,1,0:T(8,128)(2,1)}), bf16[32,8,896]{2,1,0:T(8,128)(2,1)S(1)}, u32[]{:S(2)}, u32[]{:S(2)}) async-start(bf16[32,8,896]{2,1,0:T(8,128)(2,1)} %select_select_fusion), calls=%async_computation.1 | async-start | bytes 917504 | tf_op jit(solution)/shard_map/all_to_all | solution.py:61
  71.6 0.7 fusion.20
  79.7 5.9 %all-to-all-done.1 = bf16[32,8,896]{2,1,0:T(8,128)(2,1)S(1)} async-done(((bf16[32,8,896]{2,1,0:T(8,128)(2,1)}), bf16[32,8,896]{2,1,0:T(8,128)(2,1)S(1)}, u32[]{:S(2)}, u32[]{:S(2)}) %all-to-all-start.1) | async-done | bytes 458784 | tf_op jit(solution)/shard_map/all_to_all | solution.py:61
  85.7 1.0 broadcast_in_dim.108
  86.7 4.9 %all-to-all-start.2 = ((bf16[16,4,8,896]{3,2,1,0:T(8,128)(2,1)}), bf16[16,4,8,896]{3,2,1,0:T(8,128)(2,1)S(1)}, u32[]{:S(2)}, u32[]{:S(2)}) async-start(bf16[16,4,8,896]{3,2,1,0:T(8,128)(2,1)} %broadcast_in_dim.108), calls=%async_computation.2 | async-start | bytes 1835008 | tf_op jit(solution)/shard_map/all_to_all | solution.py:36
  91.6 0.0 copy-done.2
  91.6 20.0 %all-to-all-done.2 = bf16[16,4,8,896]{3,2,1,0:T(8,128)(2,1)S(1)} async-done(((bf16[16,4,8,896]{3,2,1,0:T(8,128)(2,1)}), bf16[16,4,8,896]{3,2,1,0:T(8,128)(2,1)S(1)}, u32[]{:S(2)}, u32[]{:S(2)}) %all-to-all-start.2) | async-done | bytes 917536 | tf_op jit(solution)/shard_map/all_to_all | solution.py:36
  111.6 0.1 copy.36
  111.6 0.0 copy-done
  111.7 0.4 convolution_convert_fusion
  112.1 0.1 reshape.143
  112.2 0.0 copy-done.3
  112.2 0.4 convolution_convert_fusion.1
  112.6 0.1 reshape.142
  112.7 0.2 fusion.6
  112.9 0.2 fusion.21
  113.1 0.5 fusion.14
  113.6 0.1 copy.42
  113.8 0.1 reshape.146
  113.9 0.2 broadcast_in_dim.110
  114.1 33.2 %all_to_all.24 = bf16[16,128,256]{1,2,0:T(8,128)(2,1)S(1)} all-to-all(bf16[16,128,256]{1,2,0:T(8,128)(2,1)S(1)} %broadcast_in_dim.110), channel_id=1, replica_groups=mesh['dp'=32,'mp'=16] {'mp'}, dimensions={0} | all-to-all | bytes 2097152 | tf_op jit(solution)/shard_map/all_to_all | solution.py:36
  147.3 73.4 %all-gather.2.cloned.1.call-done = bf16[8192,256]{1,0:T(8,128)(2,1)} async-done(((bf16[256,256]{1,0:T(8,128)(2,1)}), bf16[8192,256]{1,0:T(8,128)(2,1)}) %all-gather.2.cloned.1.call-update) | async-done | bytes 4194320 | tf_op jit(solution)/shard_map/all_gather | solution.py:28
  220.6 2.2 fusion.8
  222.8 2.2 fusion.11
  225.0 0.7 pad_maximum_fusion
  (4 shorter events, 0.1 us)
Async XLA Ops:
  6.5 105.1 %copy-start = (bf16[896,256]{1,0:T(8,128)(2,1)S(1)}, bf16[896,256]{1,0:T(8,128)(2,1)}, u32[]{:S(2)}) copy-start(bf16[896,256]{1,0:T(8,128)(2,1)} %param.8) | copy-start | bytes 1376260
  6.5 85.0 %copy-start.2 = (bf16[128,256]{1,0:T(8,128)(2,1)S(1)}, bf16[128,256]{1,0:T(8,128)(2,1)}, u32[]{:S(2)}) copy-start(bf16[128,256]{1,0:T(8,128)(2,1)} %param.6) | copy-start | bytes 196612
  6.5 214.1 %all-gather.2.cloned.1.call-start = ((), (), s32[]{:S(2)}) async-start(), calls=%async_computation.4 | async-start | bytes 4325376 | tf_op jit(solution)/shard_map/all_gather | solution.py:28
  6.5 16.6 %collective-permute-start = (bf16[256,256]{1,0:T(8,128)(2,1)}, bf16[256,256]{1,0:T(8,128)(2,1)S(1)}, u32[]{:S(2)}, u32[]{:S(2)}) collective-permute-start(bf16[256,256]{1,0:T(8,128)(2,1)} %param.10), channel_id=1, source_target_pairs={{0,0},{1,16},{2,32},{3,48},{4,64},{5,80},{6,96},{7,112},{8,128},{9... | collective-permute-start | bytes 393224 | tf_op jit(solution)/shard_map/ppermute | solution.py:24
  23.2 0.7 copy-start.1
  25.4 37.4 %all-to-all-start = ((s32[32,1,1]{2,1,0:T(1,128)}), s32[32,1,1]{2,1,0:T(1,128)S(1)}, u32[]{:S(2)}, u32[]{:S(2)}) async-start(s32[32,1,1]{2,1,0:T(1,128)} %copy.35), calls=%async_computation | async-start | bytes 32768 | tf_op jit(solution)/shard_map/all_to_all | solution.py:49
  66.4 45.8 %copy-start.3 = (bf16[896,256]{1,0:T(8,128)(2,1)S(1)}, bf16[896,256]{1,0:T(8,128)(2,1)}, u32[]{:S(2)}) copy-start(bf16[896,256]{1,0:T(8,128)(2,1)} %param.9) | copy-start | bytes 1376260
  66.4 19.3 %all-to-all-start.1 = ((bf16[32,8,896]{2,1,0:T(8,128)(2,1)}), bf16[32,8,896]{2,1,0:T(8,128)(2,1)S(1)}, u32[]{:S(2)}, u32[]{:S(2)}) async-start(bf16[32,8,896]{2,1,0:T(8,128)(2,1)} %select_select_fusion), calls=%async_computation.1 | async-start | bytes 917504 | tf_op jit(solution)/shard_map/all_to_all | solution.py:61
  86.7 24.9 %all-to-all-start.2 = ((bf16[16,4,8,896]{3,2,1,0:T(8,128)(2,1)}), bf16[16,4,8,896]{3,2,1,0:T(8,128)(2,1)S(1)}, u32[]{:S(2)}, u32[]{:S(2)}) async-start(bf16[16,4,8,896]{3,2,1,0:T(8,128)(2,1)} %broadcast_in_dim.108), calls=%async_computation.2 | async-start | bytes 1835008 | tf_op jit(solution)/shard_map/all_to_all | solution.py:36
Sparse Core Ops, SparseCore 0:
  24.0 196.6 all-gather.1

commit v3 on v2

--- a/solution.py
+++ b/solution.py
@@ -12,21 +12,35 @@
 BLK_DEV = 4
 
 
+NEAR_DP = 8
+
+
 def weight_blocks(out_weight):
     dp_count = lax.axis_size("dp")
     mp_count = lax.axis_size("mp")
     ratio = dp_count // mp_count
+    far_count = dp_count // NEAR_DP
     moves = []
     for d in range(dp_count):
         for m in range(mp_count):
-            target = ((d % ratio) * mp_count + m) * mp_count + d // ratio
-            moves.append((d * mp_count + m, target))
+            order = (d % ratio) * mp_count + m
+            place = (order % far_count) * NEAR_DP + order // far_count
+            moves.append((d * mp_count + m, place * mp_count + d // ratio))
     return lax.ppermute(out_weight, ("dp", "mp"), moves)
 
 
 def weight_columns(moved):
-    gathered = lax.all_gather(moved, "dp", axis=0, tiled=True)
+    dp_count = lax.axis_size("dp")
     mp_count = lax.axis_size("mp")
+    far_groups = [list(range(z, dp_count, NEAR_DP)) for z in range(NEAR_DP)]
+    near_groups = [list(range(y, y + NEAR_DP)) for y in range(0, dp_count, NEAR_DP)]
+    far_count = dp_count // NEAR_DP
+    copies = jnp.broadcast_to(moved[None], (far_count, *moved.shape))
+    piece = lax.all_to_all(
+        copies, "dp", split_axis=0, concat_axis=0, axis_index_groups=far_groups, tiled=True
+    )
+    piece = piece.reshape(-1, moved.shape[1])
+    gathered = lax.all_gather(piece, "dp", axis=0, axis_index_groups=near_groups, tiled=True)
     return gathered.reshape(-1, mp_count * moved.shape[0], moved.shape[1])
 
 
@@ -36,7 +50,7 @@
     return lax.all_to_all(copies, axis, split_axis=0, concat_axis=0, tiled=True)
 
 
-def near_rows(database, neighbours):
+def rows_to_send(database, neighbours):
     dp_count = lax.axis_size("dp")
     mp_count = lax.axis_size("mp")
     part = lax.axis_index("mp")
@@ -57,7 +71,13 @@
     outgoing = stored[0][None]
     for block in range(1, BLK_DEV):
         outgoing = jnp.where(wanted == block, stored[block][None], outgoing)
-    outgoing = jnp.broadcast_to(outgoing, (dp_count, part_rows, enc_width))
+    return jnp.broadcast_to(outgoing, (dp_count, part_rows, enc_width))
+
+
+def near_rows(outgoing, neighbours):
+    mp_count = lax.axis_size("mp")
+    dp_count, part_rows, enc_width = outgoing.shape
+    per_owner = neighbours.size
     arrived = lax.all_to_all(outgoing, "dp", split_axis=0, concat_axis=0, tiled=True)
     shard_of = neighbours.reshape(-1) // BLK_DEV
     chosen = [
@@ -75,9 +95,10 @@
     inner_width = key_weight.shape[1]
     head_count = inner_width // HEAD_DIM
     moved = weight_blocks(out_weight)
-    database, moved = lax.optimization_barrier((database, moved))
+    outgoing = rows_to_send(database, neighbours)
+    outgoing, moved = lax.optimization_barrier((outgoing, moved))
     columns = weight_columns(moved)
-    encoded_rows = near_rows(database, neighbours)
+    encoded_rows = near_rows(outgoing, neighbours)
     near_keys = jnp.dot(encoded_rows, key_weight, preferred_element_type=jnp.float32).astype(
         jnp.bfloat16
     )

time: 233 us -> 170 us (0.73)
  the two profiles are of different devices: /device:TPU:66 before, /device:TPU:8 now
where the time goes in v3:
time: 170 us; the launch traced here: 169 us
  blocking collectives  55.8 us (33%)
  waiting for transfers between devices  39.4 us (23%)
  starting transfers between devices  38 us (22%)
  between operations  21.3 us (13%)
  matrix products  5.93 us (3%)
  local copies, waits for them, and re-layouts  4.67 us (3%)
  other arithmetic  3.78 us (2%)
    all_to_all x1, blocking collectives, copies_to_all(): return lax.all_to_all(copies, axis, split_axis=0, concat_axis=0, tiled=True)  34.2 us
    all_to_all x1, waiting for transfers between devices, copies_to_all(): return lax.all_to_all(copies, axis, split_axis=0, concat_axis=0, tiled=True)  27.3 us
    all_to_all x1, blocking collectives, weight_columns(): lax.all_to_all(copies, 'dp', split_axis=0, concat_axis=0, axis_index_grou...  21.5 us
    all_to_all x1, starting transfers between devices, near_rows(): lax.all_to_all(outgoing, 'dp', split_axis=0, concat_axis=0, tiled=True)  14.7 us
    all_to_all x1, starting transfers between devices, rows_to_send(): lax.all_to_all(asked.reshape(dp_count, 1), 'dp', split_axis=0, concat_axi...  14 us
    all_to_all x1, waiting for transfers between devices, near_rows(): lax.all_to_all(outgoing, 'dp', split_axis=0, concat_axis=0, tiled=True)  7.24 us
    all_to_all x1, starting transfers between devices, copies_to_all(): return lax.all_to_all(copies, axis, split_axis=0, concat_axis=0, tiled=True)  6.18 us
    all_to_all x1, waiting for transfers between devices, rows_to_send(): lax.all_to_all(asked.reshape(dp_count, 1), 'dp', split_axis=0, concat_axi...  4.91 us
  transfers between devices with their start and end apart: 5, of which 3 were waited for; matrix products, arithmetic and copies ran while one was open for 5% of the time, Pallas kernels for 0%

profile of v3, /device:TPU:8, one launch (start us, length us, event | category | flops | bytes accessed | tf_op | source)
XLA Modules:
  0.0 168.9 jit_solution(5154104102438354735)
XLA Ops:
  6.5 0.0 copy-start
  6.5 0.0 copy-start.1
  6.5 0.8 reshape.142
  7.4 0.1 select_reduce_fusion
  7.5 0.7 copy.35
  8.2 14.0 %all-to-all-start = ((s32[32,1,1]{2,1,0:T(1,128)}), s32[32,1,1]{2,1,0:T(1,128)S(1)}, u32[]{:S(2)}, u32[]{:S(2)}) async-start(s32[32,1,1]{2,1,0:T(1,128)} %copy.35), calls=%async_computation | async-start | bytes 32768 | tf_op jit(solution)/shard_map/all_to_all | solution.py:63
  22.1 0.0 all-gather.2.cloned.1.call-start
  22.2 3.1 %collective-permute-start = (bf16[256,256]{1,0:T(8,128)(2,1)}, bf16[256,256]{1,0:T(8,128)(2,1)S(1)}, u32[]{:S(2)}, u32[]{:S(2)}) collective-permute-start(bf16[256,256]{1,0:T(8,128)(2,1)} %param.10), channel_id=1, source_target_pairs={{0,0},{1,128},{2,256},{3,384},{4,16},{5,144},{6,272},{7,400},{8,32... | collective-permute-start | bytes 393224 | tf_op jit(solution)/shard_map/ppermute | solution.py:29
  25.3 0.8 dynamic-slice_bitcast_fusion.3
  26.0 4.9 %all-to-all-done = s32[32,1,1]{2,1,0:T(1,128)S(1)} async-done(((s32[32,1,1]{2,1,0:T(1,128)}), s32[32,1,1]{2,1,0:T(1,128)S(1)}, u32[]{:S(2)}, u32[]{:S(2)}) %all-to-all-start) | async-done | bytes 160 | tf_op jit(solution)/shard_map/all_to_all | solution.py:63
  31.0 1.8 %compare_reduce_fusion.2 = (pred[32]{0:T(512)(128)(4,1)S(1)}, pred[32]{0:T(512)(128)(4,1)S(1)}, pred[32]{0:T(512)(128)(4,1)S(1)}) fusion(s32[32,1,1]{2,1,0:T(1,128)S(1)} %all-to-all-done), kind=kLoop, calls=%fused_computation.24 | loop fusion | flops 96 | bytes 224 | tf_op jit(solution)/shard_map/eq | solution.py:73
  32.8 1.0 select_select_fusion
  33.8 0.0 collective-permute-done
  33.8 21.5 %all_to_all.29 = bf16[4,256,256]{2,1,0:T(8,128)(2,1)} all-to-all(bf16[4,256,256]{2,1,0:T(8,128)(2,1)S(1)} %broadcast_in_dim.117), channel_id=1, replica_groups={{0,128,256,384},{16,144,272,400},{32,160,288,416},{48,176,304,432},{64,..., dimensions={0} | all-to-all | bytes 1048576 | tf_op jit(solution)/shard_map/all_to_all | solution.py:39
  55.3 0.0 all-gather.2.cloned.1.call-update
  55.3 0.0 copy-start.2
  55.4 14.7 %all-to-all-start.1 = ((bf16[32,8,896]{2,1,0:T(8,128)(2,1)}), bf16[32,8,896]{2,1,0:T(8,128)(2,1)S(1)}, u32[]{:S(2)}, u32[]{:S(2)}) async-start(bf16[32,8,896]{2,1,0:T(8,128)(2,1)} %select_select_fusion), calls=%async_computation.1 | async-start | bytes 917504 | tf_op jit(solution)/shard_map/all_to_all | solution.py:81
  70.1 0.7 fusion.20
  78.5 7.2 %all-to-all-done.1 = bf16[32,8,896]{2,1,0:T(8,128)(2,1)S(1)} async-done(((bf16[32,8,896]{2,1,0:T(8,128)(2,1)}), bf16[32,8,896]{2,1,0:T(8,128)(2,1)S(1)}, u32[]{:S(2)}, u32[]{:S(2)}) %all-to-all-start.1) | async-done | bytes 458784 | tf_op jit(solution)/shard_map/all_to_all | solution.py:81
  85.8 1.0 broadcast_in_dim.114
  86.8 6.2 %all-to-all-start.2 = ((bf16[16,4,8,896]{3,2,1,0:T(8,128)(2,1)}), bf16[16,4,8,896]{3,2,1,0:T(8,128)(2,1)S(1)}, u32[]{:S(2)}, u32[]{:S(2)}) async-start(bf16[16,4,8,896]{3,2,1,0:T(8,128)(2,1)} %broadcast_in_dim.114), calls=%async_computation.2 | async-start | bytes 1835008 | tf_op jit(solution)/shard_map/all_to_all | solution.py:50
  93.0 0.0 copy-done.1
  93.0 27.3 %all-to-all-done.2 = bf16[16,4,8,896]{3,2,1,0:T(8,128)(2,1)S(1)} async-done(((bf16[16,4,8,896]{3,2,1,0:T(8,128)(2,1)}), bf16[16,4,8,896]{3,2,1,0:T(8,128)(2,1)S(1)}, u32[]{:S(2)}, u32[]{:S(2)}) %all-to-all-start.2) | async-done | bytes 917536 | tf_op jit(solution)/shard_map/all_to_all | solution.py:50
  120.3 0.1 copy.36
  120.3 0.0 copy-done
  120.4 0.4 convolution_convert_fusion
  120.8 0.1 reshape.147
  120.9 0.0 copy-done.2
  120.9 0.4 convolution_convert_fusion.1
  121.3 0.1 reshape.146
  121.4 0.2 fusion.6
  121.6 0.2 fusion.21
  121.8 0.5 fusion.14
  122.3 0.1 copy.42
  122.5 0.1 reshape.151
  122.6 0.2 broadcast_in_dim.116
  122.8 34.2 %all_to_all.30 = bf16[16,128,256]{1,2,0:T(8,128)(2,1)S(1)} all-to-all(bf16[16,128,256]{1,2,0:T(8,128)(2,1)S(1)} %broadcast_in_dim.116), channel_id=1, replica_groups=mesh['dp'=32,'mp'=16] {'mp'}, dimensions={0} | all-to-all | bytes 2097152 | tf_op jit(solution)/shard_map/all_to_all | solution.py:50
  157.0 0.0 all-gather.2.cloned.1.call-done
  157.0 2.2 %fusion.8 = bf16[128,256]{1,0:T(8,128)(2,1)S(1)} fusion(bf16[128,4096]{0,1:T(8,128)(2,1)S(1)} %bitcast.38, bf16[8192,256]{1,0:T(8,128)(2,1)} %all-gather.2.cloned.1.call-done), kind=kOutput, calls=%fused_computation.11 | convolution fusion | flops 268468224 | bytes 3211264 | tf_op jit(solution)/shard_map/dot_general | solution.py:122
  159.2 2.2 %fusion.11 = bf16[128,256]{1,0:T(8,128)(2,1)S(1)} fusion(bf16[128,4096]{0,1:T(8,128)(2,1)S(1)} %bitcast.39, bf16[8192,256]{1,0:T(8,128)(2,1)} %all-gather.2.cloned.1.call-done), kind=kOutput, calls=%fused_computation.12 | convolution fusion | flops 268468224 | bytes 3211264 | tf_op jit(solution)/shard_map/dot_general | solution.py:122
  161.4 0.7 pad_maximum_fusion
  (5 shorter events, 0.1 us)
Async XLA Ops:
  6.5 113.8 %copy-start = (bf16[896,256]{1,0:T(8,128)(2,1)S(1)}, bf16[896,256]{1,0:T(8,128)(2,1)}, u32[]{:S(2)}) copy-start(bf16[896,256]{1,0:T(8,128)(2,1)} %param.8) | copy-start | bytes 1376260
  6.5 86.4 %copy-start.1 = (bf16[128,256]{1,0:T(8,128)(2,1)S(1)}, bf16[128,256]{1,0:T(8,128)(2,1)}, u32[]{:S(2)}) copy-start(bf16[128,256]{1,0:T(8,128)(2,1)} %param.6) | copy-start | bytes 196612
  8.2 22.8 %all-to-all-start = ((s32[32,1,1]{2,1,0:T(1,128)}), s32[32,1,1]{2,1,0:T(1,128)S(1)}, u32[]{:S(2)}, u32[]{:S(2)}) async-start(s32[32,1,1]{2,1,0:T(1,128)} %copy.35), calls=%async_computation | async-start | bytes 32768 | tf_op jit(solution)/shard_map/all_to_all | solution.py:63
  22.1 134.9 %all-gather.2.cloned.1.call-start = ((), (), s32[]{:S(2)}) async-start(), calls=%async_computation.5 | async-start | bytes 4718592 | tf_op jit(solution)/shard_map/all_gather | solution.py:43
  22.2 11.6 %collective-permute-start = (bf16[256,256]{1,0:T(8,128)(2,1)}, bf16[256,256]{1,0:T(8,128)(2,1)S(1)}, u32[]{:S(2)}, u32[]{:S(2)}) collective-permute-start(bf16[256,256]{1,0:T(8,128)(2,1)} %param.10), channel_id=1, source_target_pairs={{0,0},{1,128},{2,256},{3,384},{4,16},{5,144},{6,272},{7,400},{8,32... | collective-permute-start | bytes 393224 | tf_op jit(solution)/shard_map/ppermute | solution.py:29
  55.3 65.5 %copy-start.2 = (bf16[896,256]{1,0:T(8,128)(2,1)S(1)}, bf16[896,256]{1,0:T(8,128)(2,1)}, u32[]{:S(2)}) copy-start(bf16[896,256]{1,0:T(8,128)(2,1)} %param.9) | copy-start | bytes 1376260
  55.4 30.4 %all-to-all-start.1 = ((bf16[32,8,896]{2,1,0:T(8,128)(2,1)}), bf16[32,8,896]{2,1,0:T(8,128)(2,1)S(1)}, u32[]{:S(2)}, u32[]{:S(2)}) async-start(bf16[32,8,896]{2,1,0:T(8,128)(2,1)} %select_select_fusion), calls=%async_computation.1 | async-start | bytes 917504 | tf_op jit(solution)/shard_map/all_to_all | solution.py:81
  86.8 33.5 %all-to-all-start.2 = ((bf16[16,4,8,896]{3,2,1,0:T(8,128)(2,1)}), bf16[16,4,8,896]{3,2,1,0:T(8,128)(2,1)S(1)}, u32[]{:S(2)}, u32[]{:S(2)}) async-start(bf16[16,4,8,896]{3,2,1,0:T(8,128)(2,1)} %broadcast_in_dim.114), calls=%async_computation.2 | async-start | bytes 1835008 | tf_op jit(solution)/shard_map/all_to_all | solution.py:50
Sparse Core Ops, SparseCore 0:
  55.5 67.9 all-gather.1

commit v4 on v2

--- a/solution.py
+++ b/solution.py
@@ -10,33 +10,68 @@
 NEIGH = 2
 NROW = 128
 BLK_DEV = 4
+NEAR_DP = 8
+FAR_MP = 2
 
 
 def weight_blocks(out_weight):
     dp_count = lax.axis_size("dp")
     mp_count = lax.axis_size("mp")
     ratio = dp_count // mp_count
+    far_count = dp_count // NEAR_DP
     moves = []
     for d in range(dp_count):
         for m in range(mp_count):
-            target = ((d % ratio) * mp_count + m) * mp_count + d // ratio
-            moves.append((d * mp_count + m, target))
+            column = d // ratio
+            other_half = (m ^ column) // FAR_MP % 2
+            member = m // (2 * FAR_MP) * FAR_MP + m % FAR_MP
+            order = (other_half * ratio + d % ratio) * (mp_count // 2) + member
+            place = (order % far_count) * NEAR_DP + order // far_count
+            moves.append((d * mp_count + m, place * mp_count + column))
     return lax.ppermute(out_weight, ("dp", "mp"), moves)
 
 
-def weight_columns(moved):
-    gathered = lax.all_gather(moved, "dp", axis=0, tiled=True)
-    mp_count = lax.axis_size("mp")
-    return gathered.reshape(-1, mp_count * moved.shape[0], moved.shape[1])
+def far_piece(moved):
+    dp_count = lax.axis_size("dp")
+    far_count = dp_count // NEAR_DP
+    far = lax.axis_index("dp") // NEAR_DP
+    piece = jnp.zeros((far_count, *moved.shape), moved.dtype)
+    for step in range(far_count):
+        block = moved
+        if step:
+            block = lax.ppermute(
+                moved, "dp", [(d, d ^ (step * NEAR_DP)) for d in range(dp_count)]
+            )
+        piece = lax.dynamic_update_slice(piece, block[None], (far ^ step, 0, 0))
+    return piece.reshape(-1, moved.shape[1])
 
 
-def copies_to_all(block, axis):
-    count = lax.axis_size(axis)
-    copies = jnp.broadcast_to(block[None], (count, *block.shape))
-    return lax.all_to_all(copies, axis, split_axis=0, concat_axis=0, tiled=True)
+def near_gather(piece):
+    dp_count = lax.axis_size("dp")
+    near_groups = [list(range(y, y + NEAR_DP)) for y in range(0, dp_count, NEAR_DP)]
+    return lax.all_gather(piece, "dp", axis=0, axis_index_groups=near_groups, tiled=True)
 
 
-def near_rows(database, neighbours):
+def copies_to_half(block):
+    mp_count = lax.axis_size("mp")
+    groups = [
+        [m for m in range(mp_count) if m // FAR_MP % 2 == half] for half in range(2)
+    ]
+    copies = jnp.broadcast_to(block[None], (mp_count // 2, *block.shape))
+    return lax.all_to_all(
+        copies, "mp", split_axis=0, concat_axis=0, axis_index_groups=groups, tiled=True
+    )
+
+
+def copies_to_all(block):
+    mp_count = lax.axis_size("mp")
+    other = lax.ppermute(block, "mp", [(m, m ^ FAR_MP) for m in range(mp_count)])
+    own_half = copies_to_half(block)
+    other, own_half = lax.optimization_barrier((other, own_half))
+    return own_half, copies_to_half(other)
+
+
+def rows_to_send(database, neighbours, moved):
     dp_count = lax.axis_size("dp")
     mp_count = lax.axis_size("mp")
     part = lax.axis_index("mp")
@@ -58,15 +93,23 @@
     for block in range(1, BLK_DEV):
         outgoing = jnp.where(wanted == block, stored[block][None], outgoing)
     outgoing = jnp.broadcast_to(outgoing, (dp_count, part_rows, enc_width))
-    arrived = lax.all_to_all(outgoing, "dp", split_axis=0, concat_axis=0, tiled=True)
+    return lax.optimization_barrier((outgoing, moved))
+
+
+def near_rows(arrived, neighbours):
+    part_rows, enc_width = arrived.shape[1:]
+    per_owner = neighbours.size
     shard_of = neighbours.reshape(-1) // BLK_DEV
     chosen = [
         lax.dynamic_slice(arrived, (shard_of[j], 0, 0), (1, part_rows, enc_width))
         for j in range(per_owner)
     ]
     chosen = jnp.concatenate(chosen, axis=0)
-    gathered = copies_to_all(chosen, "mp")
-    gathered = gathered.reshape(mp_count, per_owner // NEIGH, NEIGH * part_rows, enc_width)
+    halves = [
+        half.reshape(-1, per_owner // NEIGH, NEIGH * part_rows, enc_width)
+        for half in copies_to_all(chosen)
+    ]
+    gathered = jnp.concatenate(halves, axis=0)
     return gathered.transpose(1, 0, 2, 3).reshape(-1, enc_width)
 
 
@@ -74,10 +117,14 @@
     span_count = neighbours.shape[0]
     inner_width = key_weight.shape[1]
     head_count = inner_width // HEAD_DIM
+    tokens = span_count * SPAN
     moved = weight_blocks(out_weight)
-    database, moved = lax.optimization_barrier((database, moved))
-    columns = weight_columns(moved)
-    encoded_rows = near_rows(database, neighbours)
+    outgoing, moved = rows_to_send(database, neighbours, moved)
+    arrived = lax.all_to_all(outgoing, "dp", split_axis=0, concat_axis=0, tiled=True)
+    piece = far_piece(moved)
+    arrived, piece = lax.optimization_barrier((arrived, piece))
+    columns = near_gather(piece)
+    encoded_rows = near_rows(arrived, neighbours)
     near_keys = jnp.dot(encoded_rows, key_weight, preferred_element_type=jnp.float32).astype(
         jnp.bfloat16
     )
@@ -95,11 +142,16 @@
     attended = jnp.einsum(
         "chqk,ckhd->cqhd", weights, value_blocks, preferred_element_type=jnp.float32
     )
-    attended = attended.astype(jnp.bfloat16).reshape(span_count * SPAN, inner_width)
-    attended = copies_to_all(attended, "mp").transpose(1, 0, 2).reshape(span_count * SPAN, -1)
+    attended = attended.astype(jnp.bfloat16).reshape(tokens, inner_width)
+    own_half, other_half = copies_to_all(attended)
+    own_half = own_half.transpose(1, 0, 2).reshape(tokens, -1)
+    other_half = other_half.transpose(1, 0, 2).reshape(tokens, -1)
+    ratio = lax.axis_size("dp") // lax.axis_size("mp")
+    columns = columns.reshape(2, ratio, own_half.shape[1], -1)
     parts = [
-        jnp.dot(attended, columns[k], preferred_element_type=jnp.float32)
-        for k in range(columns.shape[0])
+        jnp.dot(own_half, columns[0, k], preferred_element_type=jnp.float32)
+        + jnp.dot(other_half, columns[1, k], preferred_element_type=jnp.float32)
+        for k in range(ratio)
     ]
     return jnp.concatenate(parts, axis=1).astype(jnp.bfloat16)
 

time: 233 us -> 170 us (0.73)
  the two profiles are of different devices: /device:TPU:66 before, /device:TPU:1 now
where the time goes in v4:
time: 170 us; the launch traced here: 169 us
  starting transfers between devices  74.1 us (44%)
  waiting for transfers between devices  40.1 us (24%)
  between operations  21.4 us (13%)
  blocking collectives  15.8 us (9%)
  matrix products  7.92 us (5%)
  local copies, waits for them, and re-layouts  6.23 us (4%)
  other arithmetic  3.87 us (2%)
    all_to_all x1, starting transfers between devices, on_device(): lax.all_to_all(outgoing, 'dp', split_axis=0, concat_axis=0, tiled=True)  22.3 us
    all_to_all x3, starting transfers between devices, copies_to_half(): lax.all_to_all(copies, 'mp', split_axis=0, concat_axis=0, axis_index_grou...  18.1 us
    all_to_all x1, blocking collectives, copies_to_half(): lax.all_to_all(copies, 'mp', split_axis=0, concat_axis=0, axis_index_grou...  15.8 us
    ppermute x2, waiting for transfers between devices, copies_to_all(): lax.ppermute(block, 'mp', [(m, m ^ FAR_MP) for m in range(mp_count)])  14.8 us
    all_to_all x1, starting transfers between devices, rows_to_send(): lax.all_to_all(asked.reshape(dp_count, 1), 'dp', split_axis=0, concat_axi...  14.3 us
    all_to_all x1, waiting for transfers between devices, on_device(): lax.all_to_all(outgoing, 'dp', split_axis=0, concat_axis=0, tiled=True)  12.6 us
    ppermute x3, starting transfers between devices, far_piece(): lax.ppermute(moved, 'dp', [(d, d ^ step * NEAR_DP) for d in range(dp_coun...  11.2 us
    all_to_all x3, waiting for transfers between devices, copies_to_half(): lax.all_to_all(copies, 'mp', split_axis=0, concat_axis=0, axis_index_grou...  8.77 us
  transfers between devices with their start and end apart: 12, of which 5 were waited for; matrix products, arithmetic and copies ran while one was open for 6% of the time, Pallas kernels for 0%

profile of v4, /device:TPU:1, one launch (start us, length us, event | category | flops | bytes accessed | tf_op | source)
XLA Modules:
  0.0 169.4 jit_solution(10050165261585669139)
XLA Ops:
  6.5 0.8 reshape.150
  7.4 0.1 select_reduce_fusion
  7.5 0.7 copy.39
  8.2 14.3 %all-to-all-start = ((s32[32,1,1]{2,1,0:T(1,128)}), s32[32,1,1]{2,1,0:T(1,128)S(1)}, u32[]{:S(2)}, u32[]{:S(2)}) async-start(s32[32,1,1]{2,1,0:T(1,128)} %copy.39), calls=%async_computation | async-start | bytes 32768 | tf_op jit(solution)/shard_map/all_to_all | solution.py:84
  22.5 4.3 %collective-permute-start = (bf16[256,256]{1,0:T(8,128)(2,1)}, bf16[256,256]{1,0:T(8,128)(2,1)S(1)}, u32[]{:S(2)}, u32[]{:S(2)}) collective-permute-start(bf16[256,256]{1,0:T(8,128)(2,1)} %param.10), channel_id=1, source_target_pairs={{0,0},{1,128},{2,64},{3,192},{4,256},{5,384},{6,320},{7,448},{8,16... | collective-permute-start | bytes 393224 | tf_op jit(solution)/shard_map/ppermute | solution.py:31
  26.8 0.8 dynamic-slice_bitcast_fusion.3
  27.5 3.8 %all-to-all-done = s32[32,1,1]{2,1,0:T(1,128)S(1)} async-done(((s32[32,1,1]{2,1,0:T(1,128)}), s32[32,1,1]{2,1,0:T(1,128)S(1)}, u32[]{:S(2)}, u32[]{:S(2)}) %all-to-all-start) | async-done | bytes 160 | tf_op jit(solution)/shard_map/all_to_all | solution.py:84
  31.4 1.8 %compare_reduce_fusion.2 = (pred[32]{0:T(512)(128)(4,1)S(1)}, pred[32]{0:T(512)(128)(4,1)S(1)}, pred[32]{0:T(512)(128)(4,1)S(1)}) fusion(s32[32,1,1]{2,1,0:T(1,128)S(1)} %all-to-all-done), kind=kLoop, calls=%fused_computation.34 | loop fusion | flops 96 | bytes 224 | tf_op jit(solution)/shard_map/eq | solution.py:94
  33.2 1.0 select_select_fusion
  34.2 2.2 %collective-permute-start.1 = (bf16[256,256]{1,0:T(8,128)(2,1)S(1)}, bf16[256,256]{1,0:T(8,128)(2,1)S(1)}, u32[]{:S(2)}, u32[]{:S(2)}) collective-permute-start(bf16[256,256]{1,0:T(8,128)(2,1)S(1)} %collective-permute-done), channel_id=1, source_target_pairs={{0,128},{16,144},{32,160},{48,176},{64,192},{80,208},{96,224},{112... | collective-permute-start | bytes 393224 | tf_op jit(solution)/shard_map/ppermute | solution.py:42
  36.3 6.0 %collective-permute-start.2 = (bf16[256,256]{1,0:T(8,128)(2,1)S(1)}, bf16[256,256]{1,0:T(8,128)(2,1)S(1)}, u32[]{:S(2)}, u32[]{:S(2)}) collective-permute-start(bf16[256,256]{1,0:T(8,128)(2,1)S(1)} %collective-permute-done), channel_id=1, source_target_pairs={{0,256},{16,272},{32,288},{48,304},{64,320},{80,336},{96,352},{112... | collective-permute-start | bytes 393224 | tf_op jit(solution)/shard_map/ppermute | solution.py:42
  42.3 3.1 %collective-permute-start.3 = (bf16[256,256]{1,0:T(8,128)(2,1)S(1)}, bf16[256,256]{1,0:T(8,128)(2,1)S(1)}, u32[]{:S(2)}, u32[]{:S(2)}) collective-permute-start(bf16[256,256]{1,0:T(8,128)(2,1)S(1)} %collective-permute-done), channel_id=1, source_target_pairs={{0,384},{16,400},{32,416},{48,432},{64,448},{80,464},{96,480},{112... | collective-permute-start | bytes 393224 | tf_op jit(solution)/shard_map/ppermute | solution.py:42
  45.4 22.3 %all-to-all-start.1 = ((bf16[32,8,896]{2,1,0:T(8,128)(2,1)}), bf16[32,8,896]{2,1,0:T(8,128)(2,1)S(1)}, u32[]{:S(2)}, u32[]{:S(2)}) async-start(bf16[32,8,896]{2,1,0:T(8,128)(2,1)} %select_select_fusion), calls=%async_computation.1 | async-start | bytes 917504 | tf_op jit(solution)/shard_map/all_to_all | solution.py:123
  67.8 0.0 all-gather.2.cloned.1.call-start
  68.0 12.6 %all-to-all-done.1 = bf16[32,8,896]{2,1,0:T(8,128)(2,1)S(1)} async-done(((bf16[32,8,896]{2,1,0:T(8,128)(2,1)}), bf16[32,8,896]{2,1,0:T(8,128)(2,1)S(1)}, u32[]{:S(2)}, u32[]{:S(2)}) %all-to-all-start.1) | async-done | bytes 458784 | tf_op jit(solution)/shard_map/all_to_all | solution.py:123
  80.7 0.0 all-gather.2.cloned.1.call-update
  80.7 0.7 fusion.14
  89.1 0.8 broadcast_in_dim.138
  89.9 7.8 %all-to-all-start.2 = ((bf16[8,4,8,896]{3,2,1,0:T(8,128)(2,1)}), bf16[8,4,8,896]{3,2,1,0:T(8,128)(2,1)S(1)}, u32[]{:S(2)}, u32[]{:S(2)}) async-start(bf16[8,4,8,896]{3,2,1,0:T(8,128)(2,1)} %broadcast_in_dim.138), calls=%async_computation.2 | async-start | bytes 917504 | tf_op jit(solution)/shard_map/all_to_all | solution.py:61
  97.7 1.9 %collective-permute-start.4 = (bf16[4,8,896]{2,1,0:T(8,128)(2,1)S(1)}, bf16[4,8,896]{2,1,0:T(8,128)(2,1)S(1)}, u32[]{:S(2)}, u32[]{:S(2)}) collective-permute-start(bf16[4,8,896]{2,1,0:T(8,128)(2,1)S(1)} %pad_maximum_fusion.1), channel_id=1, source_target_pairs={{0,2},{1,3},{2,0},{3,1},{4,6},{5,7},{6,4},{7,5},{8,10},{9,11},{10,... | collective-permute-start | bytes 172040 | tf_op jit(solution)/shard_map/ppermute | solution.py:68
  99.6 7.3 %collective-permute-done.4 = bf16[4,8,896]{2,1,0:T(8,128)(2,1)S(1)} collective-permute-done((bf16[4,8,896]{2,1,0:T(8,128)(2,1)S(1)}, bf16[4,8,896]{2,1,0:T(8,128)(2,1)S(1)}, u32[]{:S(2)}, u32[]{:S(2)}) %collective-permute-start.4) | collective-permute-done | bytes 57376 | tf_op jit(solution)/shard_map/ppermute | solution.py:68
  106.9 0.8 broadcast_in_dim.139
  107.7 6.0 %all-to-all-start.3 = ((bf16[8,4,8,896]{3,2,1,0:T(8,128)(2,1)}), bf16[8,4,8,896]{3,2,1,0:T(8,128)(2,1)S(1)}, u32[]{:S(2)}, u32[]{:S(2)}) async-start(bf16[8,4,8,896]{3,2,1,0:T(8,128)(2,1)} %broadcast_in_dim.139), calls=%async_computation.3 | async-start | bytes 917504 | tf_op jit(solution)/shard_map/all_to_all | solution.py:61
  113.8 8.8 %all-to-all-done.3 = bf16[8,4,8,896]{3,2,1,0:T(8,128)(2,1)S(1)} async-done(((bf16[8,4,8,896]{3,2,1,0:T(8,128)(2,1)}), bf16[8,4,8,896]{3,2,1,0:T(8,128)(2,1)S(1)}, u32[]{:S(2)}, u32[]{:S(2)}) %all-to-all-start.3) | async-done | bytes 458784 | tf_op jit(solution)/shard_map/all_to_all | solution.py:61
  122.5 0.1 maximum_bitcast_fusion
  122.6 0.1 copy.40
  122.7 0.4 convolution_convert_fusion
  123.2 0.1 reshape.157
  123.2 0.4 convolution_convert_fusion.1
  123.7 0.1 reshape.156
  123.7 0.2 fusion.2
  124.0 0.2 fusion.15
  124.2 0.5 fusion.6
  124.7 0.1 copy.44
  124.8 0.1 copy.45
  124.9 0.9 broadcast_in_dim.140
  125.8 4.3 %all-to-all-start.4 = ((bf16[8,128,256]{1,2,0:T(8,128)(2,1)}), bf16[8,128,256]{1,2,0:T(8,128)(2,1)S(1)}, u32[]{:S(2)}, u32[]{:S(2)}) async-start(bf16[8,128,256]{1,2,0:T(8,128)(2,1)} %broadcast_in_dim.140), calls=%async_computation.4 | async-start | bytes 1048576 | tf_op jit(solution)/shard_map/all_to_all | solution.py:61
  130.0 1.9 %collective-permute-start.5 = (bf16[128,256]{1,0:T(8,128)(2,1)S(1)}, bf16[128,256]{1,0:T(8,128)(2,1)S(1)}, u32[]{:S(2)}, u32[]{:S(2)}) collective-permute-start(bf16[128,256]{1,0:T(8,128)(2,1)S(1)} %bitcast.80), channel_id=1, source_target_pairs={{0,2},{1,3},{2,0},{3,1},{4,6},{5,7},{6,4},{7,5},{8,10},{9,11},{10,... | collective-permute-start | bytes 196616 | tf_op jit(solution)/shard_map/ppermute | solution.py:68
  131.9 7.6 %collective-permute-done.5 = bf16[128,256]{1,0:T(8,128)(2,1)S(1)} collective-permute-done((bf16[128,256]{1,0:T(8,128)(2,1)S(1)}, bf16[128,256]{1,0:T(8,128)(2,1)S(1)}, u32[]{:S(2)}, u32[]{:S(2)}) %collective-permute-start.5) | collective-permute-done | bytes 65568 | tf_op jit(solution)/shard_map/ppermute | solution.py:68
  139.5 0.0 all-to-all-done.4
  139.5 0.1 copy.46
  139.6 0.1 broadcast_in_dim.141
  139.7 15.8 %all_to_all.34 = bf16[8,128,256]{1,2,0:T(8,128)(2,1)S(1)} all-to-all(bf16[8,128,256]{1,2,0:T(8,128)(2,1)S(1)} %broadcast_in_dim.141), channel_id=1, replica_groups={{0,1,4,5,8,9,12,13},{2,3,6,7,10,11,14,15},{16,17,20,21,24,25,28,29},{18..., dimensions={0} | all-to-all | bytes 1048576 | tf_op jit(solution)/shard_map/all_to_all | solution.py:61
  155.6 1.6 fusion.8
  157.1 1.6 fusion.7
  158.7 1.6 fusion.4
  160.3 1.6 fusion.5
  161.9 0.7 pad_maximum_fusion
  (24 shorter events, 0.2 us)
Async XLA Ops:
  6.5 116.2 %copy-start = (bf16[896,256]{1,0:T(8,128)(2,1)S(1)}, bf16[896,256]{1,0:T(8,128)(2,1)}, u32[]{:S(2)}) copy-start(bf16[896,256]{1,0:T(8,128)(2,1)} %param.8) | copy-start | bytes 1376260
  6.5 107.2 %copy-start.2 = (bf16[128,256]{1,0:T(8,128)(2,1)S(1)}, bf16[128,256]{1,0:T(8,128)(2,1)}, u32[]{:S(2)}) copy-start(bf16[128,256]{1,0:T(8,128)(2,1)} %param.6) | copy-start | bytes 196612
  8.2 23.2 %all-to-all-start = ((s32[32,1,1]{2,1,0:T(1,128)}), s32[32,1,1]{2,1,0:T(1,128)S(1)}, u32[]{:S(2)}, u32[]{:S(2)}) async-start(s32[32,1,1]{2,1,0:T(1,128)} %copy.39), calls=%async_computation | async-start | bytes 32768 | tf_op jit(solution)/shard_map/all_to_all | solution.py:84
  22.5 11.7 %collective-permute-start = (bf16[256,256]{1,0:T(8,128)(2,1)}, bf16[256,256]{1,0:T(8,128)(2,1)S(1)}, u32[]{:S(2)}, u32[]{:S(2)}) collective-permute-start(bf16[256,256]{1,0:T(8,128)(2,1)} %param.10), channel_id=1, source_target_pairs={{0,0},{1,128},{2,64},{3,192},{4,256},{5,384},{6,320},{7,448},{8,16... | collective-permute-start | bytes 393224 | tf_op jit(solution)/shard_map/ppermute | solution.py:31
  34.2 33.7 %collective-permute-start.1 = (bf16[256,256]{1,0:T(8,128)(2,1)S(1)}, bf16[256,256]{1,0:T(8,128)(2,1)S(1)}, u32[]{:S(2)}, u32[]{:S(2)}) collective-permute-start(bf16[256,256]{1,0:T(8,128)(2,1)S(1)} %collective-permute-done), channel_id=1, source_target_pairs={{0,128},{16,144},{32,160},{48,176},{64,192},{80,208},{96,224},{112... | collective-permute-start | bytes 393224 | tf_op jit(solution)/shard_map/ppermute | solution.py:42
  36.3 31.6 %collective-permute-start.2 = (bf16[256,256]{1,0:T(8,128)(2,1)S(1)}, bf16[256,256]{1,0:T(8,128)(2,1)S(1)}, u32[]{:S(2)}, u32[]{:S(2)}) collective-permute-start(bf16[256,256]{1,0:T(8,128)(2,1)S(1)} %collective-permute-done), channel_id=1, source_target_pairs={{0,256},{16,272},{32,288},{48,304},{64,320},{80,336},{96,352},{112... | collective-permute-start | bytes 393224 | tf_op jit(solution)/shard_map/ppermute | solution.py:42
  42.3 25.6 %collective-permute-start.3 = (bf16[256,256]{1,0:T(8,128)(2,1)S(1)}, bf16[256,256]{1,0:T(8,128)(2,1)S(1)}, u32[]{:S(2)}, u32[]{:S(2)}) collective-permute-start(bf16[256,256]{1,0:T(8,128)(2,1)S(1)} %collective-permute-done), channel_id=1, source_target_pairs={{0,384},{16,400},{32,416},{48,432},{64,448},{80,464},{96,480},{112... | collective-permute-start | bytes 393224 | tf_op jit(solution)/shard_map/ppermute | solution.py:42
  45.4 35.2 %all-to-all-start.1 = ((bf16[32,8,896]{2,1,0:T(8,128)(2,1)}), bf16[32,8,896]{2,1,0:T(8,128)(2,1)S(1)}, u32[]{:S(2)}, u32[]{:S(2)}) async-start(bf16[32,8,896]{2,1,0:T(8,128)(2,1)} %select_select_fusion), calls=%async_computation.1 | async-start | bytes 917504 | tf_op jit(solution)/shard_map/all_to_all | solution.py:123
  67.8 87.8 %all-gather.2.cloned.1.call-start = ((), (), s32[]{:S(2)}) async-start(), calls=%async_computation.6 | async-start | bytes 4718592 | tf_op jit(solution)/shard_map/all_gather | solution.py:52
  68.0 12.7 %copy-start.1 = (bf16[4,256,256]{2,1,0:T(8,128)(2,1)}, bf16[4,256,256]{2,1,0:T(8,128)(2,1)S(1)}, u32[]{:S(2)}) copy-start(bf16[4,256,256]{2,1,0:T(8,128)(2,1)S(1)} %bitcast_dynamic-update-slice_fusion) | copy-start | bytes 1572868
  89.9 33.3 %copy-start.3 = (bf16[896,256]{1,0:T(8,128)(2,1)S(1)}, bf16[896,256]{1,0:T(8,128)(2,1)}, u32[]{:S(2)}) copy-start(bf16[896,256]{1,0:T(8,128)(2,1)} %param.9) | copy-start | bytes 1376260
  89.9 16.9 %all-to-all-start.2 = ((bf16[8,4,8,896]{3,2,1,0:T(8,128)(2,1)}), bf16[8,4,8,896]{3,2,1,0:T(8,128)(2,1)S(1)}, u32[]{:S(2)}, u32[]{:S(2)}) async-start(bf16[8,4,8,896]{3,2,1,0:T(8,128)(2,1)} %broadcast_in_dim.138), calls=%async_computation.2 | async-start | bytes 917504 | tf_op jit(solution)/shard_map/all_to_all | solution.py:61
  97.7 9.2 %collective-permute-start.4 = (bf16[4,8,896]{2,1,0:T(8,128)(2,1)S(1)}, bf16[4,8,896]{2,1,0:T(8,128)(2,1)S(1)}, u32[]{:S(2)}, u32[]{:S(2)}) collective-permute-start(bf16[4,8,896]{2,1,0:T(8,128)(2,1)S(1)} %pad_maximum_fusion.1), channel_id=1, source_target_pairs={{0,2},{1,3},{2,0},{3,1},{4,6},{5,7},{6,4},{7,5},{8,10},{9,11},{10,... | collective-permute-start | bytes 172040 | tf_op jit(solution)/shard_map/ppermute | solution.py:68
  107.7 14.8 %all-to-all-start.3 = ((bf16[8,4,8,896]{3,2,1,0:T(8,128)(2,1)}), bf16[8,4,8,896]{3,2,1,0:T(8,128)(2,1)S(1)}, u32[]{:S(2)}, u32[]{:S(2)}) async-start(bf16[8,4,8,896]{3,2,1,0:T(8,128)(2,1)} %broadcast_in_dim.139), calls=%async_computation.3 | async-start | bytes 917504 | tf_op jit(solution)/shard_map/all_to_all | solution.py:61
  125.8 13.8 %all-to-all-start.4 = ((bf16[8,128,256]{1,2,0:T(8,128)(2,1)}), bf16[8,128,256]{1,2,0:T(8,128)(2,1)S(1)}, u32[]{:S(2)}, u32[]{:S(2)}) async-start(bf16[8,128,256]{1,2,0:T(8,128)(2,1)} %broadcast_in_dim.140), calls=%async_computation.4 | async-start | bytes 1048576 | tf_op jit(solution)/shard_map/all_to_all | solution.py:61
  130.0 9.5 %collective-permute-start.5 = (bf16[128,256]{1,0:T(8,128)(2,1)S(1)}, bf16[128,256]{1,0:T(8,128)(2,1)S(1)}, u32[]{:S(2)}, u32[]{:S(2)}) collective-permute-start(bf16[128,256]{1,0:T(8,128)(2,1)S(1)} %bitcast.80), channel_id=1, source_target_pairs={{0,2},{1,3},{2,0},{3,1},{4,6},{5,7},{6,4},{7,5},{8,10},{9,11},{10,... | collective-permute-start | bytes 196616 | tf_op jit(solution)/shard_map/ppermute | solution.py:68
Sparse Core Ops, SparseCore 0:
  80.8 54.3 all-gather.1

commit v5 on v2

--- a/solution.py
+++ b/solution.py
@@ -12,22 +12,36 @@
 BLK_DEV = 4
 
 
+NEAR_DP = 8
+
+
 def weight_blocks(out_weight):
     dp_count = lax.axis_size("dp")
     mp_count = lax.axis_size("mp")
     ratio = dp_count // mp_count
+    far_count = dp_count // NEAR_DP
     moves = []
     for d in range(dp_count):
         for m in range(mp_count):
-            target = ((d % ratio) * mp_count + m) * mp_count + d // ratio
-            moves.append((d * mp_count + m, target))
+            order = (d % ratio) * mp_count + m
+            place = (order % far_count) * NEAR_DP + order // far_count
+            moves.append((d * mp_count + m, place * mp_count + d // ratio))
     return lax.ppermute(out_weight, ("dp", "mp"), moves)
 
 
-def weight_columns(moved):
-    gathered = lax.all_gather(moved, "dp", axis=0, tiled=True)
-    mp_count = lax.axis_size("mp")
-    return gathered.reshape(-1, mp_count * moved.shape[0], moved.shape[1])
+def to_far(block):
+    dp_count = lax.axis_size("dp")
+    groups = [list(range(z, dp_count, NEAR_DP)) for z in range(NEAR_DP)]
+    copies = jnp.broadcast_to(block[None], (dp_count // NEAR_DP, *block.shape))
+    return lax.all_to_all(
+        copies, "dp", split_axis=0, concat_axis=0, axis_index_groups=groups, tiled=True
+    )
+
+
+def to_near(piece):
+    dp_count = lax.axis_size("dp")
+    groups = [list(range(y, y + NEAR_DP)) for y in range(0, dp_count, NEAR_DP)]
+    return lax.all_gather(piece, "dp", axis=0, axis_index_groups=groups, tiled=True)
 
 
 def copies_to_all(block, axis):
@@ -36,37 +50,31 @@
     return lax.all_to_all(copies, axis, split_axis=0, concat_axis=0, tiled=True)
 
 
-def near_rows(database, neighbours):
-    dp_count = lax.axis_size("dp")
+def own_part(database):
     mp_count = lax.axis_size("mp")
-    part = lax.axis_index("mp")
     part_rows = NROW // mp_count
     enc_width = database.shape[1]
-    per_owner = neighbours.size
-    flat_ids = neighbours.reshape(1, per_owner)
-    shard_ids = jnp.arange(dp_count, dtype=jnp.int32)[:, None]
-    asked = jnp.sum(jnp.where(flat_ids // BLK_DEV == shard_ids, flat_ids % BLK_DEV, 0), axis=1)
-    wanted = lax.all_to_all(
-        asked.reshape(dp_count, 1), "dp", split_axis=0, concat_axis=0, tiled=True
-    ).reshape(dp_count, 1, 1)
-    stored = lax.dynamic_slice(
+    return lax.dynamic_slice(
         database.reshape(BLK_DEV, NROW, enc_width),
-        (0, part * part_rows, 0),
+        (0, lax.axis_index("mp") * part_rows, 0),
         (BLK_DEV, part_rows, enc_width),
     )
-    outgoing = stored[0][None]
-    for block in range(1, BLK_DEV):
-        outgoing = jnp.where(wanted == block, stored[block][None], outgoing)
-    outgoing = jnp.broadcast_to(outgoing, (dp_count, part_rows, enc_width))
-    arrived = lax.all_to_all(outgoing, "dp", split_axis=0, concat_axis=0, tiled=True)
-    shard_of = neighbours.reshape(-1) // BLK_DEV
+
+
+def near_rows(stored, neighbours):
+    far_count, part_rows, enc_width = stored.shape[1], stored.shape[3], stored.shape[4]
+    per_owner = neighbours.size
+    ids = neighbours.reshape(-1)
+    shard_of = ids // BLK_DEV
+    place = (shard_of % NEAR_DP * far_count + shard_of // NEAR_DP) * BLK_DEV + ids % BLK_DEV
+    stored = stored.reshape(-1, part_rows, enc_width)
     chosen = [
-        lax.dynamic_slice(arrived, (shard_of[j], 0, 0), (1, part_rows, enc_width))
+        lax.dynamic_slice(stored, (place[j], 0, 0), (1, part_rows, enc_width))
         for j in range(per_owner)
     ]
     chosen = jnp.concatenate(chosen, axis=0)
     gathered = copies_to_all(chosen, "mp")
-    gathered = gathered.reshape(mp_count, per_owner // NEIGH, NEIGH * part_rows, enc_width)
+    gathered = gathered.reshape(-1, per_owner // NEIGH, NEIGH * part_rows, enc_width)
     return gathered.transpose(1, 0, 2, 3).reshape(-1, enc_width)
 
 
@@ -74,10 +82,14 @@
     span_count = neighbours.shape[0]
     inner_width = key_weight.shape[1]
     head_count = inner_width // HEAD_DIM
+    mp_count = lax.axis_size("mp")
     moved = weight_blocks(out_weight)
-    database, moved = lax.optimization_barrier((database, moved))
-    columns = weight_columns(moved)
-    encoded_rows = near_rows(database, neighbours)
+    part = to_far(own_part(database))
+    stored = to_near(part[None])
+    _, moved = lax.optimization_barrier((part, moved))
+    piece = to_far(moved).reshape(-1, moved.shape[1])
+    columns = to_near(piece).reshape(-1, mp_count * moved.shape[0], moved.shape[1])
+    encoded_rows = near_rows(stored, neighbours)
     near_keys = jnp.dot(encoded_rows, key_weight, preferred_element_type=jnp.float32).astype(
         jnp.bfloat16
     )

time: 233 us -> 156 us (0.67)
  the two profiles are of different devices: /device:TPU:66 before, /device:TPU:8 now
where the time goes in v5:
time: 156 us; the launch traced here: 155 us
  blocking collectives  71.2 us (46%)
  waiting for transfers between devices  39.4 us (25%)
  between operations  21.3 us (14%)
  starting transfers between devices  10.9 us (7%)
  matrix products  6.95 us (4%)
  local copies, waits for them, and re-layouts  4.42 us (3%)
    all_to_all x2, blocking collectives, to_far(): lax.all_to_all(copies, 'dp', split_axis=0, concat_axis=0, axis_index_grou...  39 us
    all_to_all x1, blocking collectives, copies_to_all(): return lax.all_to_all(copies, axis, split_axis=0, concat_axis=0, tiled=True)  32.2 us
    all_to_all x1, waiting for transfers between devices, copies_to_all(): return lax.all_to_all(copies, axis, split_axis=0, concat_axis=0, tiled=True)  28.8 us
    all_to_all x1, starting transfers between devices, copies_to_all(): return lax.all_to_all(copies, axis, split_axis=0, concat_axis=0, tiled=True)  8.96 us
    all_gather x2, waiting for transfers between devices, to_near(): lax.all_gather(piece, 'dp', axis=0, axis_index_groups=groups, tiled=True)  6.03 us
    ppermute x1, waiting for transfers between devices, weight_blocks(): return lax.ppermute(out_weight, ('dp', 'mp'), moves)  4.57 us
    dot_general x2, matrix products, on_device(): jnp.dot(attended, columns[k], preferred_element_type=jnp.float32)  4.33 us
  transfers between devices with their start and end apart: 4, of which 3 were waited for; matrix products, arithmetic and copies ran while one was open for 4% of the time, Pallas kernels for 0%

profile of v5, /device:TPU:8, one launch (start us, length us, event | category | flops | bytes accessed | tf_op | source)
XLA Modules:
  0.0 155.0 jit_solution(16045284924116387645)
XLA Ops:
  6.5 0.0 copy-start
  6.5 0.0 copy-start.3
  6.5 0.0 all-gather.6.cloned.1.call-start
  6.5 1.2 copy-done
  7.7 14.8 %all_to_all.20 = bf16[4,4,8,896]{3,2,1,0:T(8,128)(2,1)} all-to-all(bf16[4,4,8,896]{3,2,1,0:T(8,128)(2,1)S(1)} %broadcast_in_dim.12), channel_id=1, replica_groups={{0,128,256,384},{16,144,272,400},{32,160,288,416},{48,176,304,432},{64,..., dimensions={0} | all-to-all | bytes 458752 | tf_op jit(solution)/shard_map/all_to_all | solution.py:36
  22.6 0.0 all-gather.6.cloned.1.call-update
  22.6 0.0 all-gather.4.cloned.1.call-start
  22.7 1.9 %collective-permute-start = (bf16[256,256]{1,0:T(8,128)(2,1)}, bf16[256,256]{1,0:T(8,128)(2,1)S(1)}, u32[]{:S(2)}, u32[]{:S(2)}) collective-permute-start(bf16[256,256]{1,0:T(8,128)(2,1)} %param.10), channel_id=1, source_target_pairs={{0,0},{1,128},{2,256},{3,384},{4,16},{5,144},{6,272},{7,400},{8,32... | collective-permute-start | bytes 393224 | tf_op jit(solution)/shard_map/ppermute | solution.py:29
  24.6 4.6 %collective-permute-done = bf16[256,256]{1,0:T(8,128)(2,1)S(1)} collective-permute-done((bf16[256,256]{1,0:T(8,128)(2,1)}, bf16[256,256]{1,0:T(8,128)(2,1)S(1)}, u32[]{:S(2)}, u32[]{:S(2)}) %collective-permute-start) | collective-permute-done | bytes 131104 | tf_op jit(solution)/shard_map/ppermute | solution.py:29
  29.2 0.0 copy-start.1
  29.2 24.2 %all_to_all.21 = bf16[4,256,256]{2,1,0:T(8,128)(2,1)} all-to-all(bf16[4,256,256]{2,1,0:T(8,128)(2,1)S(1)} %broadcast_in_dim.17), channel_id=1, replica_groups={{0,128,256,384},{16,144,272,400},{32,160,288,416},{48,176,304,432},{64,..., dimensions={0} | all-to-all | bytes 1048576 | tf_op jit(solution)/shard_map/all_to_all | solution.py:36
  53.4 0.0 all-gather.4.cloned.1.call-update
  53.4 0.0 copy-done.3
  53.4 0.1 reshape.43
  53.5 0.7 fusion.23
  61.9 6.0 %all-gather.6.cloned.1.call-done = bf16[32,4,8,896]{3,2,1,0:T(8,128)(2,1)} async-done(((bf16[4,4,8,896]{3,2,1,0:T(8,128)(2,1)}), bf16[32,4,8,896]{3,2,1,0:T(8,128)(2,1)}) %all-gather.6.cloned.1.call-update) | async-done | bytes 1835024 | tf_op jit(solution)/shard_map/all_gather | solution.py:44
  67.9 0.8 constant_dynamic-slice_fusion.3
  68.7 1.0 broadcast_in_dim.14
  69.7 0.0 copy-start.2
  69.7 9.0 %all-to-all-start.1 = ((bf16[16,4,8,896]{3,2,1,0:T(8,128)(2,1)}), bf16[16,4,8,896]{3,2,1,0:T(8,128)(2,1)S(1)}, u32[]{:S(2)}, u32[]{:S(2)}) async-start(bf16[16,4,8,896]{3,2,1,0:T(8,128)(2,1)} %broadcast_in_dim.14), calls=%async_computation.1 | async-start | bytes 1835008 | tf_op jit(solution)/shard_map/all_to_all | solution.py:50
  78.7 0.0 copy-done.1
  78.7 28.8 %all-to-all-done.1 = bf16[16,4,8,896]{3,2,1,0:T(8,128)(2,1)S(1)} async-done(((bf16[16,4,8,896]{3,2,1,0:T(8,128)(2,1)}), bf16[16,4,8,896]{3,2,1,0:T(8,128)(2,1)S(1)}, u32[]{:S(2)}, u32[]{:S(2)}) %all-to-all-start.1) | async-done | bytes 917536 | tf_op jit(solution)/shard_map/all_to_all | solution.py:50
  107.5 0.1 copy.21
  107.6 0.0 copy-done.2
  107.6 0.4 convolution_convert_fusion
  108.0 0.1 reshape.47
  108.1 1.5 convolution_convert_fusion.1
  109.6 0.1 reshape.46
  109.6 0.2 fusion.6
  109.8 0.2 fusion.24
  110.1 0.5 fusion.14
  110.6 0.1 copy.27
  110.7 0.1 reshape.53
  110.8 0.2 broadcast_in_dim.16
  111.0 32.2 %all_to_all.22 = bf16[16,128,256]{1,2,0:T(8,128)(2,1)S(1)} all-to-all(bf16[16,128,256]{1,2,0:T(8,128)(2,1)S(1)} %broadcast_in_dim.16), channel_id=1, replica_groups=mesh['dp'=32,'mp'=16] {'mp'}, dimensions={0} | all-to-all | bytes 2097152 | tf_op jit(solution)/shard_map/all_to_all | solution.py:50
  143.2 0.0 all-gather.4.cloned.1.call-done
  143.2 2.2 %fusion.8 = bf16[128,256]{1,0:T(8,128)(2,1)S(1)} fusion(bf16[128,4096]{0,1:T(8,128)(2,1)S(1)} %bitcast.31, bf16[8192,256]{1,0:T(8,128)(2,1)} %all-gather.4.cloned.1.call-done), kind=kOutput, calls=%fused_computation.11 | convolution fusion | flops 268468224 | bytes 3211264 | tf_op jit(solution)/shard_map/dot_general | solution.py:113
  145.4 2.2 %fusion.11 = bf16[128,256]{1,0:T(8,128)(2,1)S(1)} fusion(bf16[128,4096]{0,1:T(8,128)(2,1)S(1)} %bitcast.32, bf16[8192,256]{1,0:T(8,128)(2,1)} %all-gather.4.cloned.1.call-done), kind=kOutput, calls=%fused_computation.12 | convolution fusion | flops 268468224 | bytes 3211264 | tf_op jit(solution)/shard_map/dot_general | solution.py:113
  147.5 0.7 pad_maximum_fusion
  (6 shorter events, 0.1 us)
Async XLA Ops:
  6.5 1.2 copy-start
  6.5 46.9 %copy-start.3 = (s32[2,2]{1,0:T(2,128)S(1)}, s32[2,2]{1,0:T(2,128)}, u32[]{:S(2)}) copy-start(s32[2,2]{1,0:T(2,128)} %param.11) | copy-start | bytes 52
  6.5 61.4 %all-gather.6.cloned.1.call-start = ((), (), s32[]{:S(2)}) async-start(), calls=%async_computation.5 | async-start | bytes 2064384 | tf_op jit(solution)/shard_map/all_gather | solution.py:44
  22.6 120.6 %all-gather.4.cloned.1.call-start = ((), (), s32[]{:S(2)}) async-start(), calls=%async_computation.4 | async-start | bytes 4718592 | tf_op jit(solution)/shard_map/all_gather | solution.py:44
  22.7 6.5 %collective-permute-start = (bf16[256,256]{1,0:T(8,128)(2,1)}, bf16[256,256]{1,0:T(8,128)(2,1)S(1)}, u32[]{:S(2)}, u32[]{:S(2)}) collective-permute-start(bf16[256,256]{1,0:T(8,128)(2,1)} %param.10), channel_id=1, source_target_pairs={{0,0},{1,128},{2,256},{3,384},{4,16},{5,144},{6,272},{7,400},{8,32... | collective-permute-start | bytes 393224 | tf_op jit(solution)/shard_map/ppermute | solution.py:29
  29.2 49.5 %copy-start.1 = (bf16[128,256]{1,0:T(8,128)(2,1)S(1)}, bf16[128,256]{1,0:T(8,128)(2,1)}, u32[]{:S(2)}) copy-start(bf16[128,256]{1,0:T(8,128)(2,1)} %param.6) | copy-start | bytes 196612
  69.7 37.9 %copy-start.2 = (bf16[896,256]{1,0:T(8,128)(2,1)S(1)}, bf16[896,256]{1,0:T(8,128)(2,1)}, u32[]{:S(2)}) copy-start(bf16[896,256]{1,0:T(8,128)(2,1)} %param.8) | copy-start | bytes 1376260
  69.7 37.8 %all-to-all-start.1 = ((bf16[16,4,8,896]{3,2,1,0:T(8,128)(2,1)}), bf16[16,4,8,896]{3,2,1,0:T(8,128)(2,1)S(1)}, u32[]{:S(2)}, u32[]{:S(2)}) async-start(bf16[16,4,8,896]{3,2,1,0:T(8,128)(2,1)} %broadcast_in_dim.14), calls=%async_computation.1 | async-start | bytes 1835008 | tf_op jit(solution)/shard_map/all_to_all | solution.py:50
Sparse Core Ops, SparseCore 0:
  22.7 45.1 all-gather.5
  70.0 58.3 all-gather.3

commit v6 on v0

v6 whole, which is shorter than its diff:
```python
import math

import jax
import jax.numpy as jnp
from jax import lax
from jax.experimental import pallas as pl
from jax.experimental.pallas import tpu as pltpu
from jax.sharding import PartitionSpec as P

HEAD_DIM = 128
SPAN = 64
NEIGH = 2
NROW = 128
BLK_DEV = 4


NEAR_DP = 8


def far_piece(out_weight):
    dp_count = lax.axis_size("dp")
    mp_count = lax.axis_size("mp")
    ratio = dp_count // mp_count
    far_count = dp_count // NEAR_DP
    blocks = []
    for step in range(far_count):
        moves = []
        for d in range(dp_count):
            for m in range(mp_count):
                order = (d % ratio) * mp_count + m
                place = (order % far_count ^ step) * NEAR_DP + order // far_count
                moves.append((d * mp_count + m, place * mp_count + d // ratio))
        blocks.append(lax.ppermute(out_weight, ("dp", "mp"), moves))
    return blocks


def in_order(blocks):
    far = lax.axis_index("dp") // NEAR_DP
    piece = jnp.zeros((len(blocks), *blocks[0].shape), blocks[0].dtype)
    for step, block in enumerate(blocks):
        piece = lax.dynamic_update_slice(piece, block[None], (far ^ step, 0, 0))
    return piece.reshape(-1, blocks[0].shape[1])


def near_gather(piece):
    dp_count = lax.axis_size("dp")
    groups = [list(range(y, y + NEAR_DP)) for y in range(0, dp_count, NEAR_DP)]
    return lax.all_gather(piece, "dp", axis=0, axis_index_groups=groups, tiled=True)


def pick(indices, blocks, copies):
    def body(indices_ref, blocks_ref, out_ref):
        for j in range(indices.shape[0]):
            block = blocks_ref[indices_ref[j]]
            for c in range(copies):
                out_ref[c, j] = block

    return pl.pallas_call(
        body,
        out_shape=jax.ShapeDtypeStruct((copies, *indices.shape, *blocks.shape[1:]), blocks.dtype),
        in_specs=[
            pl.BlockSpec(memory_space=pltpu.SMEM),
            pl.BlockSpec(memory_space=pltpu.VMEM),
        ],
        out_specs=pl.BlockSpec(memory_space=pltpu.VMEM),
        name="pick",
    )(indices, blocks)


def rows_to_send(database, neighbours):
    dp_count = lax.axis_size("dp")
    part_rows = NROW // lax.axis_size("mp")
    enc_width = database.shape[1]
    flat_ids = neighbours.reshape(1, -1)
    shard_ids = jnp.arange(dp_count, dtype=jnp.int32)[:, None]
    asked = jnp.sum(jnp.where(flat_ids // BLK_DEV == shard_ids, flat_ids % BLK_DEV, 0), axis=1)
    wanted = lax.all_to_all(
        asked.reshape(dp_count, 1), "dp", split_axis=0, concat_axis=0, tiled=True
    ).reshape(dp_count)
    stored = lax.dynamic_slice(
        database.reshape(BLK_DEV, NROW, enc_width),
        (0, lax.axis_index("mp") * part_rows, 0),
        (BLK_DEV, part_rows, enc_width),
    )
    return pick(wanted, stored, 1)[0]


def near_rows(arrived, neighbours):
    mp_count = lax.axis_size("mp")
    part_rows, enc_width = arrived.shape[1:]
    per_owner = neighbours.size
    copies = pick(neighbours.reshape(-1) // BLK_DEV, arrived, mp_count)
    gathered = lax.all_to_all(copies, "mp", split_axis=0, concat_axis=0, tiled=True)
    gathered = gathered.reshape(mp_count, per_owner // NEIGH, NEIGH * part_rows, enc_width)
    return gathered.transpose(1, 0, 2, 3).reshape(-1, enc_width)


def copies_to_all(block, axis):
    count = lax.axis_size(axis)
    copies = jnp.broadcast_to(block[None], (count, *block.shape))
    return lax.all_to_all(copies, axis, split_axis=0, concat_axis=0, tiled=True)


def on_device(queries, database, key_weight, value_weight, out_weight, neighbours):
    span_count = neighbours.shape[0]
    inner_width = key_weight.shape[1]
    head_count = inner_width // HEAD_DIM
    blocks = far_piece(out_weight)
    outgoing = rows_to_send(database, neighbours)
    arrived = lax.all_to_all(outgoing, "dp", split_axis=0, concat_axis=0, tiled=True)
    arrived, blocks = lax.optimization_barrier((arrived, blocks))
    columns = near_gather(in_order(blocks)).reshape(
        -1, lax.axis_size("mp") * out_weight.shape[0], out_weight.shape[1]
    )
    encoded_rows = near_rows(arrived, neighbours)
    near_keys = jnp.dot(encoded_rows, key_weight, preferred_element_type=jnp.float32).astype(
        jnp.bfloat16
    )
    near_values = jnp.dot(encoded_rows, value_weight, preferred_element_type=jnp.float32).astype(
        jnp.bfloat16
    )
    key_blocks = near_keys.reshape(span_count, NEIGH * NROW, head_count, HEAD_DIM)
    value_blocks = near_values.reshape(span_count, NEIGH * NROW, head_count, HEAD_DIM)
    query_blocks = queries.reshape(span_count, SPAN, head_count, HEAD_DIM)
    scores = jnp.einsum(
        "cqhd,ckhd->chqk", query_blocks, key_blocks, preferred_element_type=jnp.float32
    )
    scores = scores / math.sqrt(HEAD_DIM)
    weights = jax.nn.softmax(scores, axis=-1).astype(jnp.bfloat16)
    attended = jnp.einsum(
        "chqk,ckhd->cqhd", weights, value_blocks, preferred_element_type=jnp.float32
    )
    attended = attended.astype(jnp.bfloat16).reshape(span_count * SPAN, inner_width)
    attended = copies_to_all(attended, "mp").transpose(1, 0, 2).reshape(span_count * SPAN, -1)
    parts = [
        jnp.dot(attended, columns[k], preferred_element_type=jnp.float32)
        for k in range(columns.shape[0])
    ]
    return jnp.concatenate(parts, axis=1).astype(jnp.bfloat16)


def solution(mesh):
    in_specs = (
        P("dp", "mp"),
        P("dp", None),
        P(None, "mp"),
        P(None, "mp"),
        P("mp", "dp"),
        P("dp", None),
    )
    out_specs = P("dp", "mp")
    return jax.shard_map(
        on_device, mesh=mesh, in_specs=in_specs, out_specs=out_specs, check_vma=False
    )
```

time: 460 us -> 181 us (0.39)
  the two profiles are of different devices: /device:TPU:8 before, /device:TPU:137 now
where the time goes in v6:
time: 181 us; the launch traced here: 180 us
  starting transfers between devices  68.6 us (38%)
  waiting for transfers between devices  46.8 us (26%)
  blocking collectives  34.5 us (19%)
  between operations  13.7 us (8%)
  matrix products  6.98 us (4%)
  local copies, waits for them, and re-layouts  3.75 us (2%)
  Pallas kernels  3.66 us (2%)
  other arithmetic  2.21 us (1%)
    all_to_all x1, blocking collectives, copies_to_all(): return lax.all_to_all(copies, axis, split_axis=0, concat_axis=0, tiled=True)  34.5 us
    all_to_all x1, starting transfers between devices, near_rows(): lax.all_to_all(copies, 'mp', split_axis=0, concat_axis=0, tiled=True)  28.6 us
    all_to_all x1, waiting for transfers between devices, near_rows(): lax.all_to_all(copies, 'mp', split_axis=0, concat_axis=0, tiled=True)  28 us
    ppermute x4, starting transfers between devices, far_piece(): blocks.append(lax.ppermute(out_weight, ('dp', 'mp'), moves))  21.8 us
    ppermute x4, waiting for transfers between devices, far_piece(): blocks.append(lax.ppermute(out_weight, ('dp', 'mp'), moves))  13.1 us
    all_to_all x1, starting transfers between devices, rows_to_send(): lax.all_to_all(asked.reshape(dp_count, 1), 'dp', split_axis=0, concat_axi...  11.6 us
    all_to_all x1, starting transfers between devices, on_device(): lax.all_to_all(outgoing, 'dp', split_axis=0, concat_axis=0, tiled=True)  6.65 us
    all_to_all x1, waiting for transfers between devices, rows_to_send(): lax.all_to_all(asked.reshape(dp_count, 1), 'dp', split_axis=0, concat_axi...  5.64 us
  transfers between devices with their start and end apart: 8, of which 4 were waited for; matrix products, arithmetic and copies ran while one was open for 2% of the time, Pallas kernels for 1%

profile of v6, /device:TPU:137, one launch (start us, length us, event | category | flops | bytes accessed | tf_op | source)
XLA Modules:
  0.0 180.2 jit_solution(12238115521508621817)
XLA Ops:
  6.5 0.0 copy-start
  6.5 0.0 copy-start.3
  6.5 0.8 reshape.131
  7.4 0.0 copy-start.4
  7.4 0.1 select_reduce_fusion
  7.5 0.7 copy.30
  8.2 11.6 %all-to-all-start = ((s32[32,1,1]{2,1,0:T(1,128)}), s32[32,1,1]{2,1,0:T(1,128)S(1)}, u32[]{:S(2)}, u32[]{:S(2)}) async-start(s32[32,1,1]{2,1,0:T(1,128)} %copy.30), calls=%async_computation | async-start | bytes 32768 | tf_op jit(solution)/shard_map/all_to_all | solution.py:77
  19.8 0.0 copy-done
  19.8 0.6 constant_dynamic-slice_fusion.blocks_ref
  20.4 5.6 %all-to-all-done = s32[32,1,1]{2,1,0:T(1,128)S(1)} async-done(((s32[32,1,1]{2,1,0:T(1,128)}), s32[32,1,1]{2,1,0:T(1,128)S(1)}, u32[]{:S(2)}, u32[]{:S(2)}) %all-to-all-start) | async-done | bytes 160 | tf_op jit(solution)/shard_map/all_to_all | solution.py:77
  26.1 1.2 reduce.indices_ref
  27.3 1.6 pick.2
  28.9 6.6 %all-to-all-start.1 = ((bf16[32,8,896]{2,1,0:T(8,128)(2,1)}), bf16[32,8,896]{2,1,0:T(8,128)(2,1)S(1)}, u32[]{:S(2)}, u32[]{:S(2)}) async-start(bf16[32,8,896]{2,1,0:T(8,128)(2,1)} %bitcast.36), calls=%async_computation.1 | async-start | bytes 917504 | tf_op jit(solution)/shard_map/all_to_all | solution.py:110
  35.6 0.0 all-gather.2.cloned.1.call-start
  35.6 3.1 %collective-permute-start = (bf16[256,256]{1,0:T(8,128)(2,1)}, bf16[256,256]{1,0:T(8,128)(2,1)S(1)}, u32[]{:S(2)}, u32[]{:S(2)}) collective-permute-start(bf16[256,256]{1,0:T(8,128)(2,1)} %param.10), channel_id=1, source_target_pairs={{0,0},{1,128},{2,256},{3,384},{4,16},{5,144},{6,272},{7,400},{8,32... | collective-permute-start | bytes 393224 | tf_op jit(solution)/shard_map/ppermute | solution.py:33
  38.8 6.2 %collective-permute-start.1 = (bf16[256,256]{1,0:T(8,128)(2,1)}, bf16[256,256]{1,0:T(8,128)(2,1)S(1)}, u32[]{:S(2)}, u32[]{:S(2)}) collective-permute-start(bf16[256,256]{1,0:T(8,128)(2,1)} %param.10), channel_id=1, source_target_pairs={{0,128},{1,0},{2,384},{3,256},{4,144},{5,16},{6,400},{7,272},{8,16... | collective-permute-start | bytes 393224 | tf_op jit(solution)/shard_map/ppermute | solution.py:33
  45.0 7.0 %collective-permute-start.2 = (bf16[256,256]{1,0:T(8,128)(2,1)}, bf16[256,256]{1,0:T(8,128)(2,1)S(1)}, u32[]{:S(2)}, u32[]{:S(2)}) collective-permute-start(bf16[256,256]{1,0:T(8,128)(2,1)} %param.10), channel_id=1, source_target_pairs={{0,256},{1,384},{2,0},{3,128},{4,272},{5,400},{6,16},{7,144},{8,28... | collective-permute-start | bytes 393224 | tf_op jit(solution)/shard_map/ppermute | solution.py:33
  52.0 5.5 %collective-permute-start.3 = (bf16[256,256]{1,0:T(8,128)(2,1)}, bf16[256,256]{1,0:T(8,128)(2,1)S(1)}, u32[]{:S(2)}, u32[]{:S(2)}) collective-permute-start(bf16[256,256]{1,0:T(8,128)(2,1)} %param.10), channel_id=1, source_target_pairs={{0,384},{1,256},{2,128},{3,0},{4,400},{5,272},{6,144},{7,16},{8,41... | collective-permute-start | bytes 393224 | tf_op jit(solution)/shard_map/ppermute | solution.py:33
  57.5 0.0 collective-permute-done
  57.5 0.0 collective-permute-done.1
  57.5 11.0 %collective-permute-done.2 = bf16[256,256]{1,0:T(8,128)(2,1)S(1)} collective-permute-done((bf16[256,256]{1,0:T(8,128)(2,1)}, bf16[256,256]{1,0:T(8,128)(2,1)S(1)}, u32[]{:S(2)}, u32[]{:S(2)}) %collective-permute-start.2) | collective-permute-done | bytes 131104 | tf_op jit(solution)/shard_map/ppermute | solution.py:33
  68.5 2.2 %collective-permute-done.3 = bf16[256,256]{1,0:T(8,128)(2,1)S(1)} collective-permute-done((bf16[256,256]{1,0:T(8,128)(2,1)}, bf16[256,256]{1,0:T(8,128)(2,1)S(1)}, u32[]{:S(2)}, u32[]{:S(2)}) %collective-permute-start.3) | collective-permute-done | bytes 131104 | tf_op jit(solution)/shard_map/ppermute | solution.py:33
  70.7 0.0 all-to-all-done.1.blocks_ref
  70.8 0.0 copy-start.1
  70.8 0.8 copy-done.1
  71.6 0.0 all-gather.2.cloned.1.call-update
  71.6 0.0 copy-done.4
  71.7 0.0 copy-done.2
  71.7 2.0 %pick.3 = bf16[16,4,8,896]{3,2,1,0:T(8,128)(2,1)} custom-call(s32[4]{0:T(128)} %copy-done.4, bf16[32,8,896]{2,1,0:T(8,128)(2,1)} %copy-done.2), custom_call_target="tpu_custom_call" | custom-call | tf_op jit(solution)/shard_map/pick/pallas_call | solution.py:58
  73.7 28.6 %all-to-all-start.2 = ((bf16[16,4,8,896]{3,2,1,0:T(8,128)(2,1)}), bf16[16,4,8,896]{3,2,1,0:T(8,128)(2,1)S(1)}, u32[]{:S(2)}, u32[]{:S(2)}) async-start(bf16[16,4,8,896]{3,2,1,0:T(8,128)(2,1)} %pick.3), calls=%async_computation.2 | async-start | bytes 1835008 | tf_op jit(solution)/shard_map/all_to_all | solution.py:93
  102.3 0.0 copy-done.3
  102.3 28.0 %all-to-all-done.2 = bf16[16,4,8,896]{3,2,1,0:T(8,128)(2,1)S(1)} async-done(((bf16[16,4,8,896]{3,2,1,0:T(8,128)(2,1)}), bf16[16,4,8,896]{3,2,1,0:T(8,128)(2,1)S(1)}, u32[]{:S(2)}, u32[]{:S(2)}) %all-to-all-start.2) | async-done | bytes 917536 | tf_op jit(solution)/shard_map/all_to_all | solution.py:93
  130.3 0.1 copy.31
  130.4 0.0 copy-done.5
  130.4 0.4 convolution_convert_fusion.1
  130.8 0.1 reshape.136
  130.9 1.5 convolution_convert_fusion
  132.3 0.1 reshape.137
  132.4 0.2 fusion.6
  132.6 0.2 fusion.20
  132.8 0.5 fusion.14
  133.4 0.1 copy.37
  133.5 0.1 reshape.141
  133.6 0.2 broadcast_in_dim.40
  133.8 34.5 %all_to_all.24 = bf16[16,128,256]{1,2,0:T(8,128)(2,1)S(1)} all-to-all(bf16[16,128,256]{1,2,0:T(8,128)(2,1)S(1)} %broadcast_in_dim.40), channel_id=1, replica_groups=mesh['dp'=32,'mp'=16] {'mp'}, dimensions={0} | all-to-all | bytes 2097152 | tf_op jit(solution)/shard_map/all_to_all | solution.py:101
  168.3 2.2 %fusion.11 = bf16[128,256]{1,0:T(8,128)(2,1)S(1)} fusion(bf16[128,4096]{0,1:T(8,128)(2,1)S(1)} %bitcast.37, bf16[8192,256]{1,0:T(8,128)(2,1)} %all-gather.2.cloned.1.call-done), kind=kOutput, calls=%fused_computation.12 | convolution fusion | flops 268468224 | bytes 3211264 | tf_op jit(solution)/shard_map/dot_general | solution.py:136
  170.5 2.2 %fusion.8 = bf16[128,256]{1,0:T(8,128)(2,1)S(1)} fusion(bf16[128,4096]{0,1:T(8,128)(2,1)S(1)} %bitcast.38, bf16[8192,256]{1,0:T(8,128)(2,1)} %all-gather.2.cloned.1.call-done), kind=kOutput, calls=%fused_computation.11 | convolution fusion | flops 268468224 | bytes 3211264 | tf_op jit(solution)/shard_map/dot_general | solution.py:136
  172.7 0.7 pad_maximum_fusion
  (10 shorter events, 0.1 us)
Async XLA Ops:
  6.5 13.2 %copy-start = (bf16[512,896]{1,0:T(8,128)(2,1)S(1)}, bf16[512,896]{1,0:T(8,128)(2,1)}, u32[]{:S(2)}) copy-start(bf16[512,896]{1,0:T(8,128)(2,1)} %param.7) | copy-start | bytes 2752516
  6.5 95.7 %copy-start.3 = (bf16[128,256]{1,0:T(8,128)(2,1)S(1)}, bf16[128,256]{1,0:T(8,128)(2,1)}, u32[]{:S(2)}) copy-start(bf16[128,256]{1,0:T(8,128)(2,1)} %param.6) | copy-start | bytes 196612
  7.4 64.2 %copy-start.4 = (s32[4]{0:T(128)}, s32[4]{0:T(128)S(1)}, u32[]{:S(2)}) copy-start(s32[4]{0:T(128)S(1)} %get-tuple-element.16.indices_ref) | copy-start | bytes 52
  8.2 17.9 %all-to-all-start = ((s32[32,1,1]{2,1,0:T(1,128)}), s32[32,1,1]{2,1,0:T(1,128)S(1)}, u32[]{:S(2)}, u32[]{:S(2)}) async-start(s32[32,1,1]{2,1,0:T(1,128)} %copy.30), calls=%async_computation | async-start | bytes 32768 | tf_op jit(solution)/shard_map/all_to_all | solution.py:77
  28.9 101.4 %copy-start.5 = (bf16[896,256]{1,0:T(8,128)(2,1)S(1)}, bf16[896,256]{1,0:T(8,128)(2,1)}, u32[]{:S(2)}) copy-start(bf16[896,256]{1,0:T(8,128)(2,1)} %param.9) | copy-start | bytes 1376260
  28.9 41.7 %all-to-all-start.1 = ((bf16[32,8,896]{2,1,0:T(8,128)(2,1)}), bf16[32,8,896]{2,1,0:T(8,128)(2,1)S(1)}, u32[]{:S(2)}, u32[]{:S(2)}) async-start(bf16[32,8,896]{2,1,0:T(8,128)(2,1)} %bitcast.36), calls=%async_computation.1 | async-start | bytes 917504 | tf_op jit(solution)/shard_map/all_to_all | solution.py:110
  35.6 132.7 %all-gather.2.cloned.1.call-start = ((), (), s32[]{:S(2)}) async-start(), calls=%async_computation.4 | async-start | bytes 4718592 | tf_op jit(solution)/shard_map/all_gather | solution.py:48
  35.6 21.9 %collective-permute-start = (bf16[256,256]{1,0:T(8,128)(2,1)}, bf16[256,256]{1,0:T(8,128)(2,1)S(1)}, u32[]{:S(2)}, u32[]{:S(2)}) collective-permute-start(bf16[256,256]{1,0:T(8,128)(2,1)} %param.10), channel_id=1, source_target_pairs={{0,0},{1,128},{2,256},{3,384},{4,16},{5,144},{6,272},{7,400},{8,32... | collective-permute-start | bytes 393224 | tf_op jit(solution)/shard_map/ppermute | solution.py:33
  38.8 18.8 %collective-permute-start.1 = (bf16[256,256]{1,0:T(8,128)(2,1)}, bf16[256,256]{1,0:T(8,128)(2,1)S(1)}, u32[]{:S(2)}, u32[]{:S(2)}) collective-permute-start(bf16[256,256]{1,0:T(8,128)(2,1)} %param.10), channel_id=1, source_target_pairs={{0,128},{1,0},{2,384},{3,256},{4,144},{5,16},{6,400},{7,272},{8,16... | collective-permute-start | bytes 393224 | tf_op jit(solution)/shard_map/ppermute | solution.py:33
  45.0 23.5 %collective-permute-start.2 = (bf16[256,256]{1,0:T(8,128)(2,1)}, bf16[256,256]{1,0:T(8,128)(2,1)S(1)}, u32[]{:S(2)}, u32[]{:S(2)}) collective-permute-start(bf16[256,256]{1,0:T(8,128)(2,1)} %param.10), channel_id=1, source_target_pairs={{0,256},{1,384},{2,0},{3,128},{4,272},{5,400},{6,16},{7,144},{8,28... | collective-permute-start | bytes 393224 | tf_op jit(solution)/shard_map/ppermute | solution.py:33
  52.0 18.7 %collective-permute-start.3 = (bf16[256,256]{1,0:T(8,128)(2,1)}, bf16[256,256]{1,0:T(8,128)(2,1)S(1)}, u32[]{:S(2)}, u32[]{:S(2)}) collective-permute-start(bf16[256,256]{1,0:T(8,128)(2,1)} %param.10), channel_id=1, source_target_pairs={{0,384},{1,256},{2,128},{3,0},{4,400},{5,272},{6,144},{7,16},{8,41... | collective-permute-start | bytes 393224 | tf_op jit(solution)/shard_map/ppermute | solution.py:33
  70.7 1.0 copy-start.2
  70.8 0.8 copy-start.1
  73.7 56.6 %all-to-all-start.2 = ((bf16[16,4,8,896]{3,2,1,0:T(8,128)(2,1)}), bf16[16,4,8,896]{3,2,1,0:T(8,128)(2,1)S(1)}, u32[]{:S(2)}, u32[]{:S(2)}) async-start(bf16[16,4,8,896]{3,2,1,0:T(8,128)(2,1)} %pick.3), calls=%async_computation.2 | async-start | bytes 1835008 | tf_op jit(solution)/shard_map/all_to_all | solution.py:93
Sparse Core Ops, SparseCore 0:
  71.8 76.0 all-gather.1

commit v7 on v6

--- a/solution.py
+++ b/solution.py
@@ -15,37 +15,81 @@
 
 
 NEAR_DP = 8
+LOCAL_MP = 4
 
 
-def far_piece(out_weight):
+def weight_block(out_weight):
     dp_count = lax.axis_size("dp")
     mp_count = lax.axis_size("mp")
-    ratio = dp_count // mp_count
-    far_count = dp_count // NEAR_DP
-    blocks = []
-    for step in range(far_count):
-        moves = []
-        for d in range(dp_count):
-            for m in range(mp_count):
-                order = (d % ratio) * mp_count + m
-                place = (order % far_count ^ step) * NEAR_DP + order // far_count
-                moves.append((d * mp_count + m, place * mp_count + d // ratio))
-        blocks.append(lax.ppermute(out_weight, ("dp", "mp"), moves))
-    return blocks
+    moves = []
+    for d in range(dp_count):
+        for m in range(mp_count):
+            near = d % NEAR_DP
+            local = m % LOCAL_MP
+            ratio = NEAR_DP // LOCAL_MP
+            to_near = near % ratio * LOCAL_MP + local
+            to_local = near // ratio
+            target = (d - near + to_near) * mp_count + m - local + to_local
+            moves.append((d * mp_count + m, target))
+    return lax.ppermute(out_weight, ("dp", "mp"), moves)
 
 
-def in_order(blocks):
-    far = lax.axis_index("dp") // NEAR_DP
-    piece = jnp.zeros((len(blocks), *blocks[0].shape), blocks[0].dtype)
-    for step, block in enumerate(blocks):
-        piece = lax.dynamic_update_slice(piece, block[None], (far ^ step, 0, 0))
-    return piece.reshape(-1, blocks[0].shape[1])
+def far_blocks(moved):
+    dp_count = lax.axis_size("dp")
+    blocks = [moved]
+    for step in range(1, dp_count // NEAR_DP):
+        pairs = [(d, d ^ (step * NEAR_DP)) for d in range(dp_count)]
+        blocks.append(lax.ppermute(moved, "dp", pairs))
+    return jnp.stack(blocks)
 
 
 def near_gather(piece):
     dp_count = lax.axis_size("dp")
     groups = [list(range(y, y + NEAR_DP)) for y in range(0, dp_count, NEAR_DP)]
-    return lax.all_gather(piece, "dp", axis=0, axis_index_groups=groups, tiled=True)
+    return lax.all_gather(piece, "dp", axis=0, axis_index_groups=groups)
+
+
+def exchange(blocks, groups):
+    return lax.all_to_all(
+        blocks, "mp", split_axis=0, concat_axis=0, axis_index_groups=groups, tiled=True
+    )
+
+
+def partial_products(attended, columns):
+    part_count, local_count, far_count, row_count, width = columns.shape
+    tokens = attended.shape[1]
+    far = (lax.axis_index("dp") // NEAR_DP).astype(jnp.int32).reshape(1)
+
+    def body(far_ref, attended_ref, columns_ref, out_ref):
+        total = jnp.zeros((tokens, width), jnp.float32)
+        for local in range(local_count):
+            total += jnp.dot(
+                attended_ref[local], columns_ref[0, local, 0], preferred_element_type=jnp.float32
+            )
+        out_ref[0] = total.astype(out_ref.dtype)
+
+    return pl.pallas_call(
+        body,
+        out_shape=jax.ShapeDtypeStruct((far_count, tokens, part_count * width), attended.dtype),
+        grid_spec=pltpu.PrefetchScalarGridSpec(
+            num_scalar_prefetch=1,
+            grid=(far_count, part_count),
+            in_specs=[
+                pl.BlockSpec(attended.shape, lambda i, j, far_ref: (0, 0, 0)),
+                pl.BlockSpec(
+                    (1, local_count, 1, row_count, width),
+                    lambda i, j, far_ref: (j, 0, i ^ far_ref[0], 0, 0),
+                ),
+            ],
+            out_specs=pl.BlockSpec((1, tokens, width), lambda i, j, far_ref: (i, 0, j)),
+        ),
+        cost_estimate=pl.CostEstimate(
+            flops=2 * tokens * columns.size,
+            bytes_accessed=2 * columns.size,
+            transcendentals=0,
+        ),
+        name="partial_products",
+    )(far, attended, columns)
 
 
 def pick(indices, blocks, copies):
@@ -67,7 +111,7 @@
     )(indices, blocks)
 
 
-def rows_to_send(database, neighbours):
+def rows_to_send(database, neighbours, piece):
     dp_count = lax.axis_size("dp")
     part_rows = NROW // lax.axis_size("mp")
     enc_width = database.shape[1]
@@ -82,7 +126,8 @@
         (0, lax.axis_index("mp") * part_rows, 0),
         (BLK_DEV, part_rows, enc_width),
     )
-    return pick(wanted, stored, 1)[0]
+    wanted, piece = lax.optimization_barrier((wanted, piece))
+    return pick(wanted, stored, 1)[0], piece
 
 
 def near_rows(arrived, neighbours):
@@ -95,23 +140,16 @@
     return gathered.transpose(1, 0, 2, 3).reshape(-1, enc_width)
 
 
-def copies_to_all(block, axis):
-    count = lax.axis_size(axis)
-    copies = jnp.broadcast_to(block[None], (count, *block.shape))
-    return lax.all_to_all(copies, axis, split_axis=0, concat_axis=0, tiled=True)
-
-
 def on_device(queries, database, key_weight, value_weight, out_weight, neighbours):
     span_count = neighbours.shape[0]
     inner_width = key_weight.shape[1]
     head_count = inner_width // HEAD_DIM
-    blocks = far_piece(out_weight)
-    outgoing = rows_to_send(database, neighbours)
+    mp_count = lax.axis_size("mp")
+    piece = far_blocks(weight_block(out_weight))
+    outgoing, piece = rows_to_send(database, neighbours, piece)
+    columns = near_gather(piece)
+    columns = columns.reshape(-1, LOCAL_MP, *columns.shape[1:])
     arrived = lax.all_to_all(outgoing, "dp", split_axis=0, concat_axis=0, tiled=True)
-    arrived, blocks = lax.optimization_barrier((arrived, blocks))
-    columns = near_gather(in_order(blocks)).reshape(
-        -1, lax.axis_size("mp") * out_weight.shape[0], out_weight.shape[1]
-    )
     encoded_rows = near_rows(arrived, neighbours)
     near_keys = jnp.dot(encoded_rows, key_weight, preferred_element_type=jnp.float32).astype(
         jnp.bfloat16
@@ -131,12 +169,12 @@
         "chqk,ckhd->cqhd", weights, value_blocks, preferred_element_type=jnp.float32
     )
     attended = attended.astype(jnp.bfloat16).reshape(span_count * SPAN, inner_width)
-    attended = copies_to_all(attended, "mp").transpose(1, 0, 2).reshape(span_count * SPAN, -1)
-    parts = [
-        jnp.dot(attended, columns[k], preferred_element_type=jnp.float32)
-        for k in range(columns.shape[0])
-    ]
-    return jnp.concatenate(parts, axis=1).astype(jnp.bfloat16)
+    copies = jnp.broadcast_to(attended[None], (LOCAL_MP, *attended.shape))
+    local_groups = [list(range(m, m + LOCAL_MP)) for m in range(0, mp_count, LOCAL_MP)]
+    ring_groups = [list(range(r, mp_count, LOCAL_MP)) for r in range(LOCAL_MP)]
+    partials = partial_products(exchange(copies, local_groups), columns)
+    partials = exchange(partials, ring_groups).astype(jnp.float32)
+    return jnp.sum(partials, axis=0).astype(jnp.bfloat16)
 
 
 def solution(mesh):

time: 181 us -> 167 us (0.923)
  the two profiles are of different devices: /device:TPU:137 before, /device:TPU:8 now
where the time goes in v7:
time: 167 us; the launch traced here: 166 us
  blocking collectives  67.9 us (41%)
  waiting for transfers between devices  41.3 us (25%)
  starting transfers between devices  23.8 us (14%)
  between operations  13.6 us (8%)
  Pallas kernels  10.3 us (6%)
  local copies, waits for them, and re-layouts  3.22 us (2%)
  other arithmetic  3.13 us (2%)
  matrix products  2.61 us (2%)
    all_to_all x1, blocking collectives, rows_to_send(): lax.all_to_all(asked.reshape(dp_count, 1), 'dp', split_axis=0, concat_axi...  35.4 us
    all_to_all x1, waiting for transfers between devices, near_rows(): lax.all_to_all(copies, 'mp', split_axis=0, concat_axis=0, tiled=True)  28.9 us
    all_to_all x1, blocking collectives, on_device(): lax.all_to_all(outgoing, 'dp', split_axis=0, concat_axis=0, tiled=True)  19.1 us
    all_to_all x1, blocking collectives, exchange(): lax.all_to_all(blocks, 'mp', split_axis=0, concat_axis=0, axis_index_grou...  13.4 us
    ppermute x3, starting transfers between devices, far_blocks(): blocks.append(lax.ppermute(moved, 'dp', pairs))  13 us
    all_to_all x1, waiting for transfers between devices, exchange(): lax.all_to_all(blocks, 'mp', split_axis=0, concat_axis=0, axis_index_grou...  12.5 us
    pallas_call x1, Pallas kernels, partial_products(): pl.pallas_call(body, out_shape=jax.ShapeDtypeStruct((far_count, tokens, p...  6.63 us
    all_to_all x1, starting transfers between devices, near_rows(): lax.all_to_all(copies, 'mp', split_axis=0, concat_axis=0, tiled=True)  5.72 us
  transfers between devices with their start and end apart: 7, of which 2 were waited for; matrix products, arithmetic and copies ran while one was open for 4% of the time, Pallas kernels for 2%

profile of v7, /device:TPU:8, one launch (start us, length us, event | category | flops | bytes accessed | tf_op | source)
XLA Modules:
  0.0 165.9 jit_solution(10908551033818842963)
XLA Ops:
  6.5 0.0 copy-start
  6.5 0.0 copy-start.2
  6.5 0.0 all-gather.3.cloned.1.call-start
  6.5 1.7 %collective-permute-start = (bf16[256,256]{1,0:T(8,128)(2,1)}, bf16[256,256]{1,0:T(8,128)(2,1)S(1)}, u32[]{:S(2)}, u32[]{:S(2)}) collective-permute-start(bf16[256,256]{1,0:T(8,128)(2,1)} %param.10), channel_id=1, source_target_pairs={{0,0},{1,16},{2,32},{3,48},{4,4},{5,20},{6,36},{7,52},{8,8},{9,24}... | collective-permute-start | bytes 393224 | tf_op jit(solution)/shard_map/ppermute | solution.py:34
  8.2 0.8 reshape.127
  9.0 0.0 collective-permute-done
  9.0 7.7 %collective-permute-start.1 = (bf16[256,256]{1,0:T(8,128)(2,1)S(1)}, bf16[256,256]{1,0:T(8,128)(2,1)S(1)}, u32[]{:S(2)}, u32[]{:S(2)}) collective-permute-start(bf16[256,256]{1,0:T(8,128)(2,1)S(1)} %collective-permute-done), channel_id=1, source_target_pairs={{0,128},{16,144},{32,160},{48,176},{64,192},{80,208},{96,224},{112... | collective-permute-start | bytes 393224 | tf_op jit(solution)/shard_map/ppermute | solution.py:42
  16.7 1.9 %collective-permute-start.2 = (bf16[256,256]{1,0:T(8,128)(2,1)S(1)}, bf16[256,256]{1,0:T(8,128)(2,1)S(1)}, u32[]{:S(2)}, u32[]{:S(2)}) collective-permute-start(bf16[256,256]{1,0:T(8,128)(2,1)S(1)} %collective-permute-done), channel_id=1, source_target_pairs={{0,256},{16,272},{32,288},{48,304},{64,320},{80,336},{96,352},{112... | collective-permute-start | bytes 393224 | tf_op jit(solution)/shard_map/ppermute | solution.py:42
  18.6 3.4 %collective-permute-start.3 = (bf16[256,256]{1,0:T(8,128)(2,1)S(1)}, bf16[256,256]{1,0:T(8,128)(2,1)S(1)}, u32[]{:S(2)}, u32[]{:S(2)}) collective-permute-start(bf16[256,256]{1,0:T(8,128)(2,1)S(1)} %collective-permute-done), channel_id=1, source_target_pairs={{0,384},{16,400},{32,416},{48,432},{64,448},{80,464},{96,480},{112... | collective-permute-start | bytes 393224 | tf_op jit(solution)/shard_map/ppermute | solution.py:42
  22.0 0.0 copy-start.3
  22.0 0.1 select_reduce_fusion
  22.1 0.1 copy.27
  22.2 0.0 copy-start.4
  22.2 35.4 %all_to_all.29 = s32[32,1,1]{2,1,0:T(1,128)S(1)} all-to-all(s32[32,1,1]{2,1,0:T(1,128)S(1)} %copy.27), channel_id=1, replica_groups=mesh['dp'=32,'mp'=16] {'dp'}, dimensions={0} | all-to-all | bytes 256 | tf_op jit(solution)/shard_map/all_to_all | solution.py:121
  57.6 1.2 reduce.1.indices_ref
  58.8 0.0 collective-permute-done.1
  58.8 0.0 collective-permute-done.2
  58.8 0.0 collective-permute-done.3
  58.9 0.9 pad_maximum_fusion
  59.7 0.0 all-gather.3.cloned.1.call-update
  59.7 0.0 copy-done
  59.7 0.6 constant_dynamic-slice_fusion.blocks_ref
  60.4 1.6 pick.2
  62.0 19.1 %all_to_all.30.blocks_ref = bf16[32,8,896]{2,1,0:T(8,128)(2,1)} all-to-all(bf16[32,8,896]{2,1,0:T(8,128)(2,1)} %bitcast.31), channel_id=1, replica_groups=mesh['dp'=32,'mp'=16] {'dp'}, dimensions={0} | all-to-all | bytes 917504 | tf_op jit(solution)/shard_map/all_to_all | solution.py:152
  81.2 0.0 copy-done.3
  81.2 2.0 %pick.3 = bf16[16,4,8,896]{3,2,1,0:T(8,128)(2,1)} custom-call(s32[4]{0:T(128)} %copy-done.3, bf16[32,8,896]{2,1,0:T(8,128)(2,1)} %all_to_all.30.blocks_ref), custom_call_target="tpu_custom_call" | custom-call | tf_op jit(solution)/shard_map/pick/pallas_call | solution.py:102
  83.2 5.7 %all-to-all-start.2 = ((bf16[16,4,8,896]{3,2,1,0:T(8,128)(2,1)}), bf16[16,4,8,896]{3,2,1,0:T(8,128)(2,1)S(1)}, u32[]{:S(2)}, u32[]{:S(2)}) async-start(bf16[16,4,8,896]{3,2,1,0:T(8,128)(2,1)} %pick.3), calls=%async_computation.2 | async-start | bytes 1835008 | tf_op jit(solution)/shard_map/all_to_all | solution.py:138
  88.9 0.0 copy-done.2
  89.0 28.9 %all-to-all-done.2 = bf16[16,4,8,896]{3,2,1,0:T(8,128)(2,1)S(1)} async-done(((bf16[16,4,8,896]{3,2,1,0:T(8,128)(2,1)}), bf16[16,4,8,896]{3,2,1,0:T(8,128)(2,1)S(1)}, u32[]{:S(2)}, u32[]{:S(2)}) %all-to-all-start.2) | async-done | bytes 917536 | tf_op jit(solution)/shard_map/all_to_all | solution.py:138
  117.8 0.1 copy.28
  117.9 0.0 copy-done.4
  117.9 0.4 convolution_convert_fusion
  118.3 0.1 reshape.133
  118.4 1.5 convolution_convert_fusion.1
  119.9 0.1 reshape.132
  119.9 0.2 fusion.2
  120.2 0.2 fusion.10
  120.4 0.5 fusion.4
  120.9 0.1 copy.32
  121.0 0.7 broadcast_in_dim.25
  121.7 3.4 %all-to-all-start.3 = ((bf16[4,128,256]{2,1,0:T(8,128)(2,1)}), bf16[4,128,256]{2,1,0:T(8,128)(2,1)S(1)}, u32[]{:S(2)}, u32[]{:S(2)}) async-start(bf16[4,128,256]{2,1,0:T(8,128)(2,1)} %broadcast_in_dim.25), calls=%async_computation.3 | async-start | bytes 524288 | tf_op jit(solution)/shard_map/all_to_all | solution.py:53
  125.1 12.5 %all-to-all-done.3.attended_ref = bf16[4,128,256]{2,1,0:T(8,128)(2,1)S(1)} async-done(((bf16[4,128,256]{2,1,0:T(8,128)(2,1)}), bf16[4,128,256]{2,1,0:T(8,128)(2,1)S(1)}, u32[]{:S(2)}, u32[]{:S(2)}) %all-to-all-start.3) | async-done | bytes 262176 | tf_op jit(solution)/shard_map/all_to_all | solution.py:53
  137.6 0.0 copy-start.1
  137.6 0.0 all-gather.3.cloned.1.call-done
  137.6 0.7 copy-done.1
  138.3 6.6 %partial_products.1 = bf16[4,128,512]{2,1,0:T(8,128)(2,1)} custom-call(s32[1]{0:T(128)} %bitcast.far_ref, bf16[4,128,256]{2,1,0:T(8,128)(2,1)} %copy-done.1, bf16[2,4,4,256,256]{4,3,2,1,0:T(8,128)(2,1)} %bitcast.29), custom_call_target="tpu_custom_call" | custom-call | flops 536870912 | bytes 4194304 | tf_op jit(solution)/shard_map/partial_products/pallas_call | solution.py:71
  144.9 13.4 %all_to_all.31 = bf16[4,128,512]{2,1,0:T(8,128)(2,1)S(1)} all-to-all(bf16[4,128,512]{2,1,0:T(8,128)(2,1)} %partial_products.1), channel_id=1, replica_groups={{0,4,8,12},{1,5,9,13},{2,6,10,14},{3,7,11,15},{16,20,24,28},{17,21,25,2..., dimensions={0} | all-to-all | bytes 1048576 | tf_op jit(solution)/shard_map/all_to_all | solution.py:53
  158.3 0.7 reduce_sum.32
  (3 shorter events, 0.0 us)
Async XLA Ops:
  6.5 53.2 %copy-start = (bf16[512,896]{1,0:T(8,128)(2,1)S(1)}, bf16[512,896]{1,0:T(8,128)(2,1)}, u32[]{:S(2)}) copy-start(bf16[512,896]{1,0:T(8,128)(2,1)} %param.7) | copy-start | bytes 2752516
  6.5 82.4 %copy-start.2 = (bf16[128,256]{1,0:T(8,128)(2,1)S(1)}, bf16[128,256]{1,0:T(8,128)(2,1)}, u32[]{:S(2)}) copy-start(bf16[128,256]{1,0:T(8,128)(2,1)} %param.6) | copy-start | bytes 196612
  6.5 131.0 %all-gather.3.cloned.1.call-start = ((), (), s32[]{:S(2)}) async-start(), calls=%async_computation.5 | async-start | bytes 4718592 | tf_op jit(solution)/shard_map/all_gather | solution.py:49
  6.5 2.4 %collective-permute-start = (bf16[256,256]{1,0:T(8,128)(2,1)}, bf16[256,256]{1,0:T(8,128)(2,1)S(1)}, u32[]{:S(2)}, u32[]{:S(2)}) collective-permute-start(bf16[256,256]{1,0:T(8,128)(2,1)} %param.10), channel_id=1, source_target_pairs={{0,0},{1,16},{2,32},{3,48},{4,4},{5,20},{6,36},{7,52},{8,8},{9,24}... | collective-permute-start | bytes 393224 | tf_op jit(solution)/shard_map/ppermute | solution.py:34
  9.0 49.9 %collective-permute-start.1 = (bf16[256,256]{1,0:T(8,128)(2,1)S(1)}, bf16[256,256]{1,0:T(8,128)(2,1)S(1)}, u32[]{:S(2)}, u32[]{:S(2)}) collective-permute-start(bf16[256,256]{1,0:T(8,128)(2,1)S(1)} %collective-permute-done), channel_id=1, source_target_pairs={{0,128},{16,144},{32,160},{48,176},{64,192},{80,208},{96,224},{112... | collective-permute-start | bytes 393224 | tf_op jit(solution)/shard_map/ppermute | solution.py:42
  16.7 42.1 %collective-permute-start.2 = (bf16[256,256]{1,0:T(8,128)(2,1)S(1)}, bf16[256,256]{1,0:T(8,128)(2,1)S(1)}, u32[]{:S(2)}, u32[]{:S(2)}) collective-permute-start(bf16[256,256]{1,0:T(8,128)(2,1)S(1)} %collective-permute-done), channel_id=1, source_target_pairs={{0,256},{16,272},{32,288},{48,304},{64,320},{80,336},{96,352},{112... | collective-permute-start | bytes 393224 | tf_op jit(solution)/shard_map/ppermute | solution.py:42
  18.6 40.2 %collective-permute-start.3 = (bf16[256,256]{1,0:T(8,128)(2,1)S(1)}, bf16[256,256]{1,0:T(8,128)(2,1)S(1)}, u32[]{:S(2)}, u32[]{:S(2)}) collective-permute-start(bf16[256,256]{1,0:T(8,128)(2,1)S(1)} %collective-permute-done), channel_id=1, source_target_pairs={{0,384},{16,400},{32,416},{48,432},{64,448},{80,464},{96,480},{112... | collective-permute-start | bytes 393224 | tf_op jit(solution)/shard_map/ppermute | solution.py:42
  22.0 59.1 %copy-start.3 = (s32[4]{0:T(128)}, s32[4]{0:T(128)S(1)}, u32[]{:S(2)}) copy-start(s32[4]{0:T(128)S(1)} %get-tuple-element.10.indices_ref) | copy-start | bytes 52
  22.2 95.7 %copy-start.4 = (bf16[896,256]{1,0:T(8,128)(2,1)S(1)}, bf16[896,256]{1,0:T(8,128)(2,1)}, u32[]{:S(2)}) copy-start(bf16[896,256]{1,0:T(8,128)(2,1)} %param.8) | copy-start | bytes 1376260
  83.2 34.6 %all-to-all-start.2 = ((bf16[16,4,8,896]{3,2,1,0:T(8,128)(2,1)}), bf16[16,4,8,896]{3,2,1,0:T(8,128)(2,1)S(1)}, u32[]{:S(2)}, u32[]{:S(2)}) async-start(bf16[16,4,8,896]{3,2,1,0:T(8,128)(2,1)} %pick.3), calls=%async_computation.2 | async-start | bytes 1835008 | tf_op jit(solution)/shard_map/all_to_all | solution.py:138
  121.7 15.9 %all-to-all-start.3 = ((bf16[4,128,256]{2,1,0:T(8,128)(2,1)}), bf16[4,128,256]{2,1,0:T(8,128)(2,1)S(1)}, u32[]{:S(2)}, u32[]{:S(2)}) async-start(bf16[4,128,256]{2,1,0:T(8,128)(2,1)} %broadcast_in_dim.25), calls=%async_computation.3 | async-start | bytes 524288 | tf_op jit(solution)/shard_map/all_to_all | solution.py:53
  137.6 0.7 copy-start.1
Sparse Core Ops, SparseCore 0:
  59.8 58.7 all-gather.2

commit v8 on v7

--- a/solution.py
+++ b/solution.py
@@ -16,6 +16,7 @@
 
 NEAR_DP = 8
 LOCAL_MP = 4
+LANES = 128
 
 
 def weight_block(out_weight):
@@ -61,27 +62,32 @@
     far = (lax.axis_index("dp") // NEAR_DP).astype(jnp.int32).reshape(1)
 
     def body(far_ref, attended_ref, columns_ref, out_ref):
-        total = jnp.zeros((tokens, width), jnp.float32)
-        for local in range(local_count):
-            total += jnp.dot(
-                attended_ref[local], columns_ref[0, local, 0], preferred_element_type=jnp.float32
-            )
-        out_ref[0] = total.astype(out_ref.dtype)
+        for part in range(part_count):
+            total = jnp.zeros((tokens, width), jnp.float32)
+            for local in range(local_count):
+                total += jnp.dot(
+                    attended_ref[local],
+                    columns_ref[part, local, 0],
+                    preferred_element_type=jnp.float32,
+                )
+            out_ref[0, :, part * width : (part + 1) * width] = total.astype(out_ref.dtype)
 
     return pl.pallas_call(
         body,
         out_shape=jax.ShapeDtypeStruct((far_count, tokens, part_count * width), attended.dtype),
         grid_spec=pltpu.PrefetchScalarGridSpec(
             num_scalar_prefetch=1,
-            grid=(far_count, part_count),
+            grid=(far_count,),
             in_specs=[
-                pl.BlockSpec(attended.shape, lambda i, j, far_ref: (0, 0, 0)),
+                pl.BlockSpec(attended.shape, lambda i, far_ref: (0, 0, 0)),
                 pl.BlockSpec(
-                    (1, local_count, 1, row_count, width),
-                    lambda i, j, far_ref: (j, 0, i ^ far_ref[0], 0, 0),
+                    (part_count, local_count, 1, row_count, width),
+                    lambda i, far_ref: (0, 0, i ^ far_ref[0], 0, 0),
                 ),
             ],
-            out_specs=pl.BlockSpec((1, tokens, width), lambda i, j, far_ref: (i, 0, j)),
+            out_specs=pl.BlockSpec(
+                (1, tokens, part_count * width), lambda i, far_ref: (i, 0, 0)
+            ),
         ),
         cost_estimate=pl.CostEstimate(
             flops=2 * tokens * columns.size,
@@ -95,13 +101,15 @@
 def pick(indices, blocks, copies):
     def body(indices_ref, blocks_ref, out_ref):
         for j in range(indices.shape[0]):
-            block = blocks_ref[indices_ref[j]]
+            block = blocks_ref[indices_ref[j, 0]]
             for c in range(copies):
                 out_ref[c, j] = block
 
     return pl.pallas_call(
         body,
-        out_shape=jax.ShapeDtypeStruct((copies, *indices.shape, *blocks.shape[1:]), blocks.dtype),
+        out_shape=jax.ShapeDtypeStruct(
+            (copies, indices.shape[0], *blocks.shape[1:]), blocks.dtype
+        ),
         in_specs=[
             pl.BlockSpec(memory_space=pltpu.SMEM),
             pl.BlockSpec(memory_space=pltpu.VMEM),
@@ -111,30 +119,31 @@
     )(indices, blocks)
 
 
-def rows_to_send(database, neighbours, piece):
-    dp_count = lax.axis_size("dp")
-    part_rows = NROW // lax.axis_size("mp")
-    enc_width = database.shape[1]
+def request(neighbours):
+    dp_count = lax.axis_size("dp")
     flat_ids = neighbours.reshape(1, -1)
     shard_ids = jnp.arange(dp_count, dtype=jnp.int32)[:, None]
     asked = jnp.sum(jnp.where(flat_ids // BLK_DEV == shard_ids, flat_ids % BLK_DEV, 0), axis=1)
-    wanted = lax.all_to_all(
-        asked.reshape(dp_count, 1), "dp", split_axis=0, concat_axis=0, tiled=True
-    ).reshape(dp_count)
+    asked = jnp.broadcast_to(asked[:, None], (dp_count, LANES))
+    return lax.all_to_all(asked, "dp", split_axis=0, concat_axis=0, tiled=True)
+
+
+def rows_to_send(database, wanted):
+    part_rows = NROW // lax.axis_size("mp")
+    enc_width = database.shape[1]
     stored = lax.dynamic_slice(
         database.reshape(BLK_DEV, NROW, enc_width),
         (0, lax.axis_index("mp") * part_rows, 0),
         (BLK_DEV, part_rows, enc_width),
     )
-    wanted, piece = lax.optimization_barrier((wanted, piece))
-    return pick(wanted, stored, 1)[0], piece
+    return pick(wanted, stored, 1)[0]
 
 
 def near_rows(arrived, neighbours):
     mp_count = lax.axis_size("mp")
     part_rows, enc_width = arrived.shape[1:]
     per_owner = neighbours.size
-    copies = pick(neighbours.reshape(-1) // BLK_DEV, arrived, mp_count)
+    copies = pick(neighbours.reshape(-1, 1) // BLK_DEV, arrived, mp_count)
     gathered = lax.all_to_all(copies, "mp", split_axis=0, concat_axis=0, tiled=True)
     gathered = gathered.reshape(mp_count, per_owner // NEIGH, NEIGH * part_rows, enc_width)
     return gathered.transpose(1, 0, 2, 3).reshape(-1, enc_width)
@@ -145,8 +154,10 @@
     inner_width = key_weight.shape[1]
     head_count = inner_width // HEAD_DIM
     mp_count = lax.axis_size("mp")
-    piece = far_blocks(weight_block(out_weight))
-    outgoing, piece = rows_to_send(database, neighbours, piece)
+    moved = weight_block(out_weight)
+    wanted, moved = lax.optimization_barrier((request(neighbours), moved))
+    wanted, piece = lax.optimization_barrier((wanted, far_blocks(moved)))
+    outgoing = rows_to_send(database, wanted)
     columns = near_gather(piece)
     columns = columns.reshape(-1, LOCAL_MP, *columns.shape[1:])
     arrived = lax.all_to_all(outgoing, "dp", split_axis=0, concat_axis=0, tiled=True)

time: 167 us -> 161 us (0.964)
  the two profiles are of different devices: /device:TPU:8 before, /device:TPU:72 now
where the time goes in v8:
time: 161 us; the launch traced here: 160 us
  waiting for transfers between devices  63.5 us (39%)
  starting transfers between devices  35 us (22%)
  blocking collectives  30.3 us (19%)
  between operations  13.6 us (8%)
  Pallas kernels  8.26 us (5%)
  local copies, waits for them, and re-layouts  4.79 us (3%)
  matrix products  2.62 us (2%)
  other arithmetic  2.5 us (2%)
    all_to_all x1, waiting for transfers between devices, near_rows(): lax.all_to_all(copies, 'mp', split_axis=0, concat_axis=0, tiled=True)  28.7 us
    all_to_all x1, blocking collectives, request(): return lax.all_to_all(asked, 'dp', split_axis=0, concat_axis=0, tiled=True)  17 us
    all_to_all x1, waiting for transfers between devices, on_device(): lax.all_to_all(outgoing, 'dp', split_axis=0, concat_axis=0, tiled=True)  13.8 us
    all_to_all x1, blocking collectives, exchange(): lax.all_to_all(blocks, 'mp', split_axis=0, concat_axis=0, axis_index_grou...  13.3 us
    all_to_all x1, waiting for transfers between devices, exchange(): lax.all_to_all(blocks, 'mp', split_axis=0, concat_axis=0, axis_index_grou...  12.7 us
    ppermute x1, starting transfers between devices, weight_block(): return lax.ppermute(out_weight, ('dp', 'mp'), moves)  9.23 us
    ppermute x3, starting transfers between devices, far_blocks(): blocks.append(lax.ppermute(moved, 'dp', pairs))  9.2 us
    ppermute x3, waiting for transfers between devices, far_blocks(): blocks.append(lax.ppermute(moved, 'dp', pairs))  8.22 us
  transfers between devices with their start and end apart: 8, of which 5 were waited for; matrix products, arithmetic and copies ran while one was open for 4% of the time, Pallas kernels for 2%

profile of v8, /device:TPU:72, one launch (start us, length us, event | category | flops | bytes accessed | tf_op | source)
XLA Modules:
  0.0 160.4 jit_solution(12835007454565058816)
XLA Ops:
  6.5 0.0 copy-start
  6.5 0.0 copy-start.3
  6.5 0.0 all-gather.3.cloned.1.call-start
  6.5 9.2 %collective-permute-start = (bf16[256,256]{1,0:T(8,128)(2,1)}, bf16[256,256]{1,0:T(8,128)(2,1)S(1)}, u32[]{:S(2)}, u32[]{:S(2)}) collective-permute-start(bf16[256,256]{1,0:T(8,128)(2,1)} %param.10), channel_id=1, source_target_pairs={{0,0},{1,16},{2,32},{3,48},{4,4},{5,20},{6,36},{7,52},{8,8},{9,24}... | collective-permute-start | bytes 393224 | tf_op jit(solution)/shard_map/ppermute | solution.py:35
  15.8 0.8 reshape.229
  16.6 0.1 select_reduce_fusion
  16.6 0.1 broadcast_in_dim.30
  16.7 0.0 copy-start.4
  16.8 17.0 %all_to_all.29 = s32[32,1,128]{2,1,0:T(1,128)} all-to-all(s32[32,1,128]{2,1,0:T(1,128)S(1)} %broadcast_in_dim.30), channel_id=1, replica_groups=mesh['dp'=32,'mp'=16] {'dp'}, dimensions={0} | all-to-all | bytes 32768 | tf_op jit(solution)/shard_map/all_to_all | solution.py:128
  33.8 0.0 collective-permute-done
  33.8 3.3 %collective-permute-start.1 = (bf16[256,256]{1,0:T(8,128)(2,1)S(1)}, bf16[256,256]{1,0:T(8,128)(2,1)S(1)}, u32[]{:S(2)}, u32[]{:S(2)}) collective-permute-start(bf16[256,256]{1,0:T(8,128)(2,1)S(1)} %collective-permute-done), channel_id=1, source_target_pairs={{0,128},{16,144},{32,160},{48,176},{64,192},{80,208},{96,224},{112... | collective-permute-start | bytes 393224 | tf_op jit(solution)/shard_map/ppermute | solution.py:43
  37.1 2.5 %collective-permute-start.2 = (bf16[256,256]{1,0:T(8,128)(2,1)S(1)}, bf16[256,256]{1,0:T(8,128)(2,1)S(1)}, u32[]{:S(2)}, u32[]{:S(2)}) collective-permute-start(bf16[256,256]{1,0:T(8,128)(2,1)S(1)} %collective-permute-done), channel_id=1, source_target_pairs={{0,256},{16,272},{32,288},{48,304},{64,320},{80,336},{96,352},{112... | collective-permute-start | bytes 393224 | tf_op jit(solution)/shard_map/ppermute | solution.py:43
  39.7 3.3 %collective-permute-start.3 = (bf16[256,256]{1,0:T(8,128)(2,1)S(1)}, bf16[256,256]{1,0:T(8,128)(2,1)S(1)}, u32[]{:S(2)}, u32[]{:S(2)}) collective-permute-start(bf16[256,256]{1,0:T(8,128)(2,1)S(1)} %collective-permute-done), channel_id=1, source_target_pairs={{0,384},{16,400},{32,416},{48,432},{64,448},{80,464},{96,480},{112... | collective-permute-start | bytes 393224 | tf_op jit(solution)/shard_map/ppermute | solution.py:43
  43.0 0.0 collective-permute-done.1
  43.0 4.7 %collective-permute-done.2 = bf16[256,256]{1,0:T(8,128)(2,1)S(1)} collective-permute-done((bf16[256,256]{1,0:T(8,128)(2,1)S(1)}, bf16[256,256]{1,0:T(8,128)(2,1)S(1)}, u32[]{:S(2)}, u32[]{:S(2)}) %collective-permute-start.2) | collective-permute-done | bytes 131104 | tf_op jit(solution)/shard_map/ppermute | solution.py:43
  47.8 3.5 %collective-permute-done.3 = bf16[256,256]{1,0:T(8,128)(2,1)S(1)} collective-permute-done((bf16[256,256]{1,0:T(8,128)(2,1)S(1)}, bf16[256,256]{1,0:T(8,128)(2,1)S(1)}, u32[]{:S(2)}, u32[]{:S(2)}) %collective-permute-start.3) | collective-permute-done | bytes 131104 | tf_op jit(solution)/shard_map/ppermute | solution.py:43
  51.3 0.9 pad_maximum_fusion
  52.1 0.0 all-gather.3.cloned.1.call-update
  52.1 0.0 copy-done
  52.2 0.6 constant_dynamic-slice_fusion.blocks_ref
  52.8 1.7 %pick.2 = bf16[1,32,8,896]{3,2,1,0:T(8,128)(2,1)} custom-call(s32[32,128]{1,0:T(8,128)} %bitcast.40, bf16[4,8,896]{2,1,0:T(8,128)(2,1)} %constant_dynamic-slice_fusion.blocks_ref), custom_call_target="tpu_custom_call" | custom-call | tf_op jit(solution)/shard_map/pick/pallas_call | solution.py:108
  54.5 5.4 %all-to-all-start.1 = ((bf16[32,8,896]{2,1,0:T(8,128)(2,1)}), bf16[32,8,896]{2,1,0:T(8,128)(2,1)S(1)}, u32[]{:S(2)}, u32[]{:S(2)}) async-start(bf16[32,8,896]{2,1,0:T(8,128)(2,1)} %bitcast.31), calls=%async_computation.1 | async-start | bytes 917504 | tf_op jit(solution)/shard_map/all_to_all | solution.py:163
  60.0 0.8 reshape.239
  60.8 0.6 add_select_fusion.indices_ref
  61.3 13.8 %all-to-all-done.1.blocks_ref = bf16[32,8,896]{2,1,0:T(8,128)(2,1)S(1)} async-done(((bf16[32,8,896]{2,1,0:T(8,128)(2,1)}), bf16[32,8,896]{2,1,0:T(8,128)(2,1)S(1)}, u32[]{:S(2)}, u32[]{:S(2)}) %all-to-all-start.1) | async-done | bytes 458784 | tf_op jit(solution)/shard_map/all_to_all | solution.py:163
  75.1 0.0 copy-start.1
  75.1 0.8 copy-done.1
  75.9 2.0 %pick.3 = bf16[16,4,8,896]{3,2,1,0:T(8,128)(2,1)} custom-call(s32[4,1]{1,0:T(4,128)} %add_select_fusion.indices_ref, bf16[32,8,896]{2,1,0:T(8,128)(2,1)} %copy-done.1), custom_call_target="tpu_custom_call" | custom-call | tf_op jit(solution)/shard_map/pick/pallas_call | solution.py:108
  77.9 7.7 %all-to-all-start.2 = ((bf16[16,4,8,896]{3,2,1,0:T(8,128)(2,1)}), bf16[16,4,8,896]{3,2,1,0:T(8,128)(2,1)S(1)}, u32[]{:S(2)}, u32[]{:S(2)}) async-start(bf16[16,4,8,896]{3,2,1,0:T(8,128)(2,1)} %pick.3), calls=%async_computation.2 | async-start | bytes 1835008 | tf_op jit(solution)/shard_map/all_to_all | solution.py:147
  85.6 0.0 copy-done.3
  85.6 28.7 %all-to-all-done.2 = bf16[16,4,8,896]{3,2,1,0:T(8,128)(2,1)S(1)} async-done(((bf16[16,4,8,896]{3,2,1,0:T(8,128)(2,1)}), bf16[16,4,8,896]{3,2,1,0:T(8,128)(2,1)S(1)}, u32[]{:S(2)}, u32[]{:S(2)}) %all-to-all-start.2) | async-done | bytes 917536 | tf_op jit(solution)/shard_map/all_to_all | solution.py:147
  114.4 0.1 copy.36
  114.5 0.0 copy-done.4
  114.5 0.4 convolution_convert_fusion
  114.9 0.1 reshape.234
  115.0 1.5 convolution_convert_fusion.1
  116.4 0.1 reshape.233
  116.5 0.2 fusion.2
  116.7 0.2 fusion.12
  116.9 0.5 fusion.4
  117.4 0.1 copy.40
  117.5 0.7 broadcast_in_dim.32
  118.3 3.4 %all-to-all-start.3 = ((bf16[4,128,256]{2,1,0:T(8,128)(2,1)}), bf16[4,128,256]{2,1,0:T(8,128)(2,1)S(1)}, u32[]{:S(2)}, u32[]{:S(2)}) async-start(bf16[4,128,256]{2,1,0:T(8,128)(2,1)} %broadcast_in_dim.32), calls=%async_computation.3 | async-start | bytes 524288 | tf_op jit(solution)/shard_map/all_to_all | solution.py:54
  121.7 12.7 %all-to-all-done.3.attended_ref = bf16[4,128,256]{2,1,0:T(8,128)(2,1)S(1)} async-done(((bf16[4,128,256]{2,1,0:T(8,128)(2,1)}), bf16[4,128,256]{2,1,0:T(8,128)(2,1)S(1)}, u32[]{:S(2)}, u32[]{:S(2)}) %all-to-all-start.3) | async-done | bytes 262176 | tf_op jit(solution)/shard_map/all_to_all | solution.py:54
  134.4 0.7 copy-done.2
  135.1 4.5 %partial_products.1 = bf16[4,128,512]{2,1,0:T(8,128)(2,1)} custom-call(s32[1]{0:T(128)} %bitcast.far_ref, bf16[4,128,256]{2,1,0:T(8,128)(2,1)} %copy-done.2, bf16[2,4,4,256,256]{4,3,2,1,0:T(8,128)(2,1)} %bitcast.29), custom_call_target="tpu_custom_call" | custom-call | flops 536870912 | bytes 4194304 | tf_op jit(solution)/shard_map/partial_products/pallas_call | solution.py:75
  139.6 13.3 %all_to_all.30 = bf16[4,128,512]{2,1,0:T(8,128)(2,1)S(1)} all-to-all(bf16[4,128,512]{2,1,0:T(8,128)(2,1)} %partial_products.1), channel_id=1, replica_groups={{0,4,8,12},{1,5,9,13},{2,6,10,14},{3,7,11,15},{16,20,24,28},{17,21,25,2..., dimensions={0} | all-to-all | bytes 1048576 | tf_op jit(solution)/shard_map/all_to_all | solution.py:54
  152.9 0.7 reduce_sum.32
  (5 shorter events, 0.0 us)
Async XLA Ops:
  6.5 45.6 %copy-start = (bf16[512,896]{1,0:T(8,128)(2,1)S(1)}, bf16[512,896]{1,0:T(8,128)(2,1)}, u32[]{:S(2)}) copy-start(bf16[512,896]{1,0:T(8,128)(2,1)} %param.7) | copy-start | bytes 2752516
  6.5 79.1 %copy-start.3 = (bf16[128,256]{1,0:T(8,128)(2,1)S(1)}, bf16[128,256]{1,0:T(8,128)(2,1)}, u32[]{:S(2)}) copy-start(bf16[128,256]{1,0:T(8,128)(2,1)} %param.6) | copy-start | bytes 196612
  6.5 127.9 %all-gather.3.cloned.1.call-start = ((), (), s32[]{:S(2)}) async-start(), calls=%async_computation.5 | async-start | bytes 4718592 | tf_op jit(solution)/shard_map/all_gather | solution.py:50
  6.5 27.3 %collective-permute-start = (bf16[256,256]{1,0:T(8,128)(2,1)}, bf16[256,256]{1,0:T(8,128)(2,1)S(1)}, u32[]{:S(2)}, u32[]{:S(2)}) collective-permute-start(bf16[256,256]{1,0:T(8,128)(2,1)} %param.10), channel_id=1, source_target_pairs={{0,0},{1,16},{2,32},{3,48},{4,4},{5,20},{6,36},{7,52},{8,8},{9,24}... | collective-permute-start | bytes 393224 | tf_op jit(solution)/shard_map/ppermute | solution.py:35
  16.7 97.7 %copy-start.4 = (bf16[896,256]{1,0:T(8,128)(2,1)S(1)}, bf16[896,256]{1,0:T(8,128)(2,1)}, u32[]{:S(2)}) copy-start(bf16[896,256]{1,0:T(8,128)(2,1)} %param.8) | copy-start | bytes 1376260
  33.8 9.2 %collective-permute-start.1 = (bf16[256,256]{1,0:T(8,128)(2,1)S(1)}, bf16[256,256]{1,0:T(8,128)(2,1)S(1)}, u32[]{:S(2)}, u32[]{:S(2)}) collective-permute-start(bf16[256,256]{1,0:T(8,128)(2,1)S(1)} %collective-permute-done), channel_id=1, source_target_pairs={{0,128},{16,144},{32,160},{48,176},{64,192},{80,208},{96,224},{112... | collective-permute-start | bytes 393224 | tf_op jit(solution)/shard_map/ppermute | solution.py:43
  37.1 10.6 %collective-permute-start.2 = (bf16[256,256]{1,0:T(8,128)(2,1)S(1)}, bf16[256,256]{1,0:T(8,128)(2,1)S(1)}, u32[]{:S(2)}, u32[]{:S(2)}) collective-permute-start(bf16[256,256]{1,0:T(8,128)(2,1)S(1)} %collective-permute-done), channel_id=1, source_target_pairs={{0,256},{16,272},{32,288},{48,304},{64,320},{80,336},{96,352},{112... | collective-permute-start | bytes 393224 | tf_op jit(solution)/shard_map/ppermute | solution.py:43
  39.7 11.6 %collective-permute-start.3 = (bf16[256,256]{1,0:T(8,128)(2,1)S(1)}, bf16[256,256]{1,0:T(8,128)(2,1)S(1)}, u32[]{:S(2)}, u32[]{:S(2)}) collective-permute-start(bf16[256,256]{1,0:T(8,128)(2,1)S(1)} %collective-permute-done), channel_id=1, source_target_pairs={{0,384},{16,400},{32,416},{48,432},{64,448},{80,464},{96,480},{112... | collective-permute-start | bytes 393224 | tf_op jit(solution)/shard_map/ppermute | solution.py:43
  54.5 20.6 %all-to-all-start.1 = ((bf16[32,8,896]{2,1,0:T(8,128)(2,1)}), bf16[32,8,896]{2,1,0:T(8,128)(2,1)S(1)}, u32[]{:S(2)}, u32[]{:S(2)}) async-start(bf16[32,8,896]{2,1,0:T(8,128)(2,1)} %bitcast.31), calls=%async_computation.1 | async-start | bytes 917504 | tf_op jit(solution)/shard_map/all_to_all | solution.py:163
  75.1 0.8 copy-start.1
  77.9 36.5 %all-to-all-start.2 = ((bf16[16,4,8,896]{3,2,1,0:T(8,128)(2,1)}), bf16[16,4,8,896]{3,2,1,0:T(8,128)(2,1)S(1)}, u32[]{:S(2)}, u32[]{:S(2)}) async-start(bf16[16,4,8,896]{3,2,1,0:T(8,128)(2,1)} %pick.3), calls=%async_computation.2 | async-start | bytes 1835008 | tf_op jit(solution)/shard_map/all_to_all | solution.py:147
  118.3 16.1 %all-to-all-start.3 = ((bf16[4,128,256]{2,1,0:T(8,128)(2,1)}), bf16[4,128,256]{2,1,0:T(8,128)(2,1)S(1)}, u32[]{:S(2)}, u32[]{:S(2)}) async-start(bf16[4,128,256]{2,1,0:T(8,128)(2,1)} %broadcast_in_dim.32), calls=%async_computation.3 | async-start | bytes 524288 | tf_op jit(solution)/shard_map/all_to_all | solution.py:54
  134.4 0.7 copy-start.2
Sparse Core Ops, SparseCore 0:
  52.3 59.0 all-gather.2

commit v9 on v8

--- a/solution.py
+++ b/solution.py
@@ -15,23 +15,20 @@
 
 
 NEAR_DP = 8
-LOCAL_MP = 4
 LANES = 128
 
 
 def weight_block(out_weight):
     dp_count = lax.axis_size("dp")
     mp_count = lax.axis_size("mp")
+    ratio = dp_count // mp_count
+    far_count = dp_count // NEAR_DP
     moves = []
     for d in range(dp_count):
         for m in range(mp_count):
-            near = d % NEAR_DP
-            local = m % LOCAL_MP
-            ratio = NEAR_DP // LOCAL_MP
-            to_near = near % ratio * LOCAL_MP + local
-            to_local = near // ratio
-            target = (d - near + to_near) * mp_count + m - local + to_local
-            moves.append((d * mp_count + m, target))
+            near = d % ratio * (mp_count // far_count) + m // far_count
+            place = m % far_count * NEAR_DP + near
+            moves.append((d * mp_count + m, place * mp_count + d // ratio))
     return lax.ppermute(out_weight, ("dp", "mp"), moves)
 
 
@@ -50,51 +47,57 @@
     return lax.all_gather(piece, "dp", axis=0, axis_index_groups=groups)
 
 
-def exchange(blocks, groups):
-    return lax.all_to_all(
-        blocks, "mp", split_axis=0, concat_axis=0, axis_index_groups=groups, tiled=True
-    )
-
-
-def partial_products(attended, columns):
-    part_count, local_count, far_count, row_count, width = columns.shape
+def product(attended, columns):
+    part_count, outer_count, far_count, row_count, width = columns.shape
     tokens = attended.shape[1]
     far = (lax.axis_index("dp") // NEAR_DP).astype(jnp.int32).reshape(1)
 
-    def body(far_ref, attended_ref, columns_ref, out_ref):
+    def body(far_ref, attended_ref, columns_ref, out_ref, total_ref):
+        outer = pl.program_id(0)
+        parts = [jnp.zeros((tokens, width), jnp.float32) for _ in range(part_count)]
+        for slot in range(far_count):
+            block = attended_ref[outer * far_count + (slot ^ far_ref[0])]
+            for part in range(part_count):
+                parts[part] += jnp.dot(
+                    block, columns_ref[part, 0, slot], preferred_element_type=jnp.float32
+                )
         for part in range(part_count):
-            total = jnp.zeros((tokens, width), jnp.float32)
-            for local in range(local_count):
-                total += jnp.dot(
-                    attended_ref[local],
-                    columns_ref[part, local, 0],
-                    preferred_element_type=jnp.float32,
-                )
-            out_ref[0, :, part * width : (part + 1) * width] = total.astype(out_ref.dtype)
+            lanes = slice(part * width, (part + 1) * width)
+
+            @pl.when(outer == 0)
+            def _():
+                total_ref[:, lanes] = parts[part]
+
+            @pl.when(outer > 0)
+            def _():
+                total_ref[:, lanes] += parts[part]
+
+        @pl.when(outer == outer_count - 1)
+        def _():
+            out_ref[...] = total_ref[...].astype(out_ref.dtype)
 
     return pl.pallas_call(
         body,
-        out_shape=jax.ShapeDtypeStruct((far_count, tokens, part_count * width), attended.dtype),
+        out_shape=jax.ShapeDtypeStruct((tokens, part_count * width), attended.dtype),
         grid_spec=pltpu.PrefetchScalarGridSpec(
             num_scalar_prefetch=1,
-            grid=(far_count,),
+            grid=(outer_count,),
             in_specs=[
                 pl.BlockSpec(attended.shape, lambda i, far_ref: (0, 0, 0)),
                 pl.BlockSpec(
-                    (part_count, local_count, 1, row_count, width),
-                    lambda i, far_ref: (0, 0, i ^ far_ref[0], 0, 0),
+                    (part_count, 1, far_count, row_count, width),
+                    lambda i, far_ref: (0, i, 0, 0, 0),
                 ),
             ],
-            out_specs=pl.BlockSpec(
-                (1, tokens, part_count * width), lambda i, far_ref: (i, 0, 0)
-            ),
+            out_specs=pl.BlockSpec((tokens, part_count * width), lambda i, far_ref: (0, 0)),
+            scratch_shapes=[pltpu.VMEM((tokens, part_count * width), jnp.float32)],
         ),
         cost_estimate=pl.CostEstimate(
             flops=2 * tokens * columns.size,
             bytes_accessed=2 * columns.size,
             transcendentals=0,
         ),
-        name="partial_products",
+        name="product",
     )(far, attended, columns)
 
 
@@ -155,12 +158,13 @@
     head_count = inner_width // HEAD_DIM
     mp_count = lax.axis_size("mp")
     moved = weight_block(out_weight)
-    wanted, moved = lax.optimization_barrier((request(neighbours), moved))
-    wanted, piece = lax.optimization_barrier((wanted, far_blocks(moved)))
+    wanted, _ = lax.optimization_barrier((request(neighbours), moved))
     outgoing = rows_to_send(database, wanted)
+    arrived = lax.all_to_all(outgoing, "dp", split_axis=0, concat_axis=0, tiled=True)
+    arrived, piece = lax.optimization_barrier((arrived, far_blocks(moved)))
     columns = near_gather(piece)
-    columns = columns.reshape(-1, LOCAL_MP, *columns.shape[1:])
-    arrived = lax.all_to_all(outgoing, "dp", split_axis=0, concat_axis=0, tiled=True)
+    ratio = lax.axis_size("dp") // mp_count
+    columns = columns.reshape(ratio, -1, *columns.shape[1:])
     encoded_rows = near_rows(arrived, neighbours)
     near_keys = jnp.dot(encoded_rows, key_weight, preferred_element_type=jnp.float32).astype(
         jnp.bfloat16
@@ -180,12 +184,9 @@
         "chqk,ckhd->cqhd", weights, value_blocks, preferred_element_type=jnp.float32
     )
     attended = attended.astype(jnp.bfloat16).reshape(span_count * SPAN, inner_width)
-    copies = jnp.broadcast_to(attended[None], (LOCAL_MP, *attended.shape))
-    local_groups = [list(range(m, m + LOCAL_MP)) for m in range(0, mp_count, LOCAL_MP)]
-    ring_groups = [list(range(r, mp_count, LOCAL_MP)) for r in range(LOCAL_MP)]
-    partials = partial_products(exchange(copies, local_groups), columns)
-    partials = exchange(partials, ring_groups).astype(jnp.float32)
-    return jnp.sum(partials, axis=0).astype(jnp.bfloat16)
+    copies = jnp.broadcast_to(attended[None], (mp_count, *attended.shape))
+    attended = lax.all_to_all(copies, "mp", split_axis=0, concat_axis=0, tiled=True)
+    return product(attended, columns)
 
 
 def solution(mesh):

time: 161 us -> 156 us (0.969)
  the two profiles are of different devices: /device:TPU:72 before, /device:TPU:17 now
where the time goes in v9:
time: 156 us; the launch traced here: 155 us
  waiting for transfers between devices  76.7 us (49%)
  starting transfers between devices  46.4 us (30%)
  between operations  13.5 us (9%)
  Pallas kernels  8.36 us (5%)
  local copies, waits for them, and re-layouts  5.93 us (4%)
  matrix products  2.62 us (2%)
  other arithmetic  1.75 us (1%)
    all_to_all x1, waiting for transfers between devices, on_device(): lax.all_to_all(copies, 'mp', split_axis=0, concat_axis=0, tiled=True)  28.5 us
    all_to_all x1, waiting for transfers between devices, near_rows(): lax.all_to_all(copies, 'mp', split_axis=0, concat_axis=0, tiled=True)  28 us
    all_to_all x1, starting transfers between devices, request(): return lax.all_to_all(asked, 'dp', split_axis=0, concat_axis=0, tiled=True)  15.8 us
    ppermute x3, waiting for transfers between devices, far_blocks(): blocks.append(lax.ppermute(moved, 'dp', pairs))  13.7 us
    ppermute x3, starting transfers between devices, far_blocks(): blocks.append(lax.ppermute(moved, 'dp', pairs))  8.37 us
    all_to_all x1, starting transfers between devices, on_device(): lax.all_to_all(outgoing, 'dp', split_axis=0, concat_axis=0, tiled=True)  6.91 us
    all_to_all x1, waiting for transfers between devices, request(): return lax.all_to_all(asked, 'dp', split_axis=0, concat_axis=0, tiled=True)  6.5 us
    all_to_all x1, starting transfers between devices, near_rows(): lax.all_to_all(copies, 'mp', split_axis=0, concat_axis=0, tiled=True)  5.74 us
  transfers between devices with their start and end apart: 9, of which 6 were waited for; matrix products, arithmetic and copies ran while one was open for 6% of the time, Pallas kernels for 1%

profile of v9, /device:TPU:17, one launch (start us, length us, event | category | flops | bytes accessed | tf_op | source)
XLA Modules:
  0.0 155.4 jit_solution(12918121173878129123)
XLA Ops:
  6.5 0.0 copy-start
  6.5 0.0 copy-start.4
  6.5 5.2 %collective-permute-start = (bf16[256,256]{1,0:T(8,128)(2,1)}, bf16[256,256]{1,0:T(8,128)(2,1)S(1)}, u32[]{:S(2)}, u32[]{:S(2)}) collective-permute-start(bf16[256,256]{1,0:T(8,128)(2,1)} %param.10), channel_id=1, source_target_pairs={{0,0},{1,128},{2,256},{3,384},{4,16},{5,144},{6,272},{7,400},{8,32... | collective-permute-start | bytes 393224 | tf_op jit(solution)/shard_map/ppermute | solution.py:32
  11.8 0.8 reshape.229
  12.5 0.1 select_reduce_fusion
  12.6 0.7 broadcast_in_dim.30
  13.3 0.0 copy-start.5
  13.3 15.8 %all-to-all-start = ((s32[32,1,128]{2,1,0:T(1,128)}), s32[32,1,128]{2,1,0:T(1,128)S(1)}, u32[]{:S(2)}, u32[]{:S(2)}) async-start(s32[32,1,128]{2,1,0:T(1,128)} %broadcast_in_dim.30), calls=%async_computation | async-start | bytes 32768 | tf_op jit(solution)/shard_map/all_to_all | solution.py:131
  29.2 0.0 copy-done
  29.2 0.6 constant_dynamic-slice_fusion.blocks_ref
  29.8 6.5 %all-to-all-done = s32[32,1,128]{2,1,0:T(1,128)S(1)} async-done(((s32[32,1,128]{2,1,0:T(1,128)}), s32[32,1,128]{2,1,0:T(1,128)S(1)}, u32[]{:S(2)}, u32[]{:S(2)}) %all-to-all-start) | async-done | bytes 16416 | tf_op jit(solution)/shard_map/all_to_all | solution.py:131
  36.3 0.0 copy-start.3
  36.3 0.0 collective-permute-done
  36.3 0.6 copy-done.3
  36.9 1.7 %pick.2 = bf16[1,32,8,896]{3,2,1,0:T(8,128)(2,1)} custom-call(s32[32,128]{1,0:T(8,128)} %bitcast.40, bf16[4,8,896]{2,1,0:T(8,128)(2,1)} %constant_dynamic-slice_fusion.blocks_ref), custom_call_target="tpu_custom_call" | custom-call | tf_op jit(solution)/shard_map/pick/pallas_call | solution.py:111
  38.7 6.9 %all-to-all-start.1 = ((bf16[32,8,896]{2,1,0:T(8,128)(2,1)}), bf16[32,8,896]{2,1,0:T(8,128)(2,1)S(1)}, u32[]{:S(2)}, u32[]{:S(2)}) async-start(bf16[32,8,896]{2,1,0:T(8,128)(2,1)} %bitcast.31), calls=%async_computation.1 | async-start | bytes 917504 | tf_op jit(solution)/shard_map/all_to_all | solution.py:163
  45.6 0.0 all-gather.3.cloned.1.call-start
  45.6 3.1 %collective-permute-start.1 = (bf16[256,256]{1,0:T(8,128)(2,1)S(1)}, bf16[256,256]{1,0:T(8,128)(2,1)S(1)}, u32[]{:S(2)}, u32[]{:S(2)}) collective-permute-start(bf16[256,256]{1,0:T(8,128)(2,1)S(1)} %collective-permute-done), channel_id=1, source_target_pairs={{0,128},{16,144},{32,160},{48,176},{64,192},{80,208},{96,224},{112... | collective-permute-start | bytes 393224 | tf_op jit(solution)/shard_map/ppermute | solution.py:40
  48.8 2.1 %collective-permute-start.2 = (bf16[256,256]{1,0:T(8,128)(2,1)S(1)}, bf16[256,256]{1,0:T(8,128)(2,1)S(1)}, u32[]{:S(2)}, u32[]{:S(2)}) collective-permute-start(bf16[256,256]{1,0:T(8,128)(2,1)S(1)} %collective-permute-done), channel_id=1, source_target_pairs={{0,256},{16,272},{32,288},{48,304},{64,320},{80,336},{96,352},{112... | collective-permute-start | bytes 393224 | tf_op jit(solution)/shard_map/ppermute | solution.py:40
  50.9 3.1 %collective-permute-start.3 = (bf16[256,256]{1,0:T(8,128)(2,1)S(1)}, bf16[256,256]{1,0:T(8,128)(2,1)S(1)}, u32[]{:S(2)}, u32[]{:S(2)}) collective-permute-start(bf16[256,256]{1,0:T(8,128)(2,1)S(1)} %collective-permute-done), channel_id=1, source_target_pairs={{0,384},{16,400},{32,416},{48,432},{64,448},{80,464},{96,480},{112... | collective-permute-start | bytes 393224 | tf_op jit(solution)/shard_map/ppermute | solution.py:40
  54.0 3.3 %collective-permute-done.1 = bf16[256,256]{1,0:T(8,128)(2,1)S(1)} collective-permute-done((bf16[256,256]{1,0:T(8,128)(2,1)S(1)}, bf16[256,256]{1,0:T(8,128)(2,1)S(1)}, u32[]{:S(2)}, u32[]{:S(2)}) %collective-permute-start.1) | collective-permute-done | bytes 131104 | tf_op jit(solution)/shard_map/ppermute | solution.py:40
  57.4 6.0 %collective-permute-done.2 = bf16[256,256]{1,0:T(8,128)(2,1)S(1)} collective-permute-done((bf16[256,256]{1,0:T(8,128)(2,1)S(1)}, bf16[256,256]{1,0:T(8,128)(2,1)S(1)}, u32[]{:S(2)}, u32[]{:S(2)}) %collective-permute-start.2) | collective-permute-done | bytes 131104 | tf_op jit(solution)/shard_map/ppermute | solution.py:40
  63.4 4.4 %collective-permute-done.3 = bf16[256,256]{1,0:T(8,128)(2,1)S(1)} collective-permute-done((bf16[256,256]{1,0:T(8,128)(2,1)S(1)}, bf16[256,256]{1,0:T(8,128)(2,1)S(1)}, u32[]{:S(2)}, u32[]{:S(2)}) %collective-permute-start.3) | collective-permute-done | bytes 131104 | tf_op jit(solution)/shard_map/ppermute | solution.py:40
  67.8 0.9 pad_maximum_fusion
  68.6 0.0 all-to-all-done.1.blocks_ref
  68.7 0.0 all-gather.3.cloned.1.call-update
  68.7 0.8 reshape.239
  69.5 0.6 add_select_fusion.indices_ref
  70.1 0.0 copy-done.2
  70.1 2.1 %pick.3 = bf16[16,4,8,896]{3,2,1,0:T(8,128)(2,1)} custom-call(s32[4,1]{1,0:T(4,128)} %add_select_fusion.indices_ref, bf16[32,8,896]{2,1,0:T(8,128)(2,1)} %copy-done.2), custom_call_target="tpu_custom_call" | custom-call | tf_op jit(solution)/shard_map/pick/pallas_call | solution.py:111
  72.1 5.7 %all-to-all-start.2 = ((bf16[16,4,8,896]{3,2,1,0:T(8,128)(2,1)}), bf16[16,4,8,896]{3,2,1,0:T(8,128)(2,1)S(1)}, u32[]{:S(2)}, u32[]{:S(2)}) async-start(bf16[16,4,8,896]{3,2,1,0:T(8,128)(2,1)} %pick.3), calls=%async_computation.2 | async-start | bytes 1835008 | tf_op jit(solution)/shard_map/all_to_all | solution.py:150
  77.9 0.0 copy-done.4
  77.9 28.0 %all-to-all-done.2 = bf16[16,4,8,896]{3,2,1,0:T(8,128)(2,1)S(1)} async-done(((bf16[16,4,8,896]{3,2,1,0:T(8,128)(2,1)}), bf16[16,4,8,896]{3,2,1,0:T(8,128)(2,1)S(1)}, u32[]{:S(2)}, u32[]{:S(2)}) %all-to-all-start.2) | async-done | bytes 917536 | tf_op jit(solution)/shard_map/all_to_all | solution.py:150
  105.9 0.1 copy.36
  106.0 0.0 copy-done.5
  106.0 0.4 convolution_convert_fusion
  106.5 0.1 reshape.234
  106.5 1.5 convolution_convert_fusion.1
  108.0 0.1 reshape.233
  108.1 0.2 fusion.2
  108.3 0.2 fusion.12
  108.5 0.5 fusion.4
  109.0 0.1 copy.40
  109.1 1.1 broadcast_in_dim.32
  110.2 4.3 %all-to-all-start.3 = ((bf16[16,128,256]{2,1,0:T(8,128)(2,1)}), bf16[16,128,256]{2,1,0:T(8,128)(2,1)S(1)}, u32[]{:S(2)}, u32[]{:S(2)}) async-start(bf16[16,128,256]{2,1,0:T(8,128)(2,1)} %broadcast_in_dim.32), calls=%async_computation.3 | async-start | bytes 2097152 | tf_op jit(solution)/shard_map/all_to_all | solution.py:188
  114.5 28.5 %all-to-all-done.3.attended_ref = bf16[16,128,256]{2,1,0:T(8,128)(2,1)S(1)} async-done(((bf16[16,128,256]{2,1,0:T(8,128)(2,1)}), bf16[16,128,256]{2,1,0:T(8,128)(2,1)S(1)}, u32[]{:S(2)}, u32[]{:S(2)}) %all-to-all-start.3) | async-done | bytes 1048608 | tf_op jit(solution)/shard_map/all_to_all | solution.py:188
  143.0 1.0 copy-done.1
  144.0 4.6 %product.1 = bf16[128,512]{1,0:T(8,128)(2,1)} custom-call(s32[1]{0:T(128)} %bitcast.far_ref, bf16[16,128,256]{2,1,0:T(8,128)(2,1)} %copy-done.1, bf16[2,4,4,256,256]{4,3,2,1,0:T(8,128)(2,1)} %bitcast.29), custom_call_target="tpu_custom_call" | custom-call | flops 536870912 | bytes 4194304 | tf_op jit(solution)/shard_map/product/pallas_call | solution.py:79
  (6 shorter events, 0.1 us)
Async XLA Ops:
  6.5 22.7 %copy-start = (bf16[512,896]{1,0:T(8,128)(2,1)S(1)}, bf16[512,896]{1,0:T(8,128)(2,1)}, u32[]{:S(2)}) copy-start(bf16[512,896]{1,0:T(8,128)(2,1)} %param.7) | copy-start | bytes 2752516
  6.5 71.3 %copy-start.4 = (bf16[128,256]{1,0:T(8,128)(2,1)S(1)}, bf16[128,256]{1,0:T(8,128)(2,1)}, u32[]{:S(2)}) copy-start(bf16[128,256]{1,0:T(8,128)(2,1)} %param.6) | copy-start | bytes 196612
  6.5 29.8 %collective-permute-start = (bf16[256,256]{1,0:T(8,128)(2,1)}, bf16[256,256]{1,0:T(8,128)(2,1)S(1)}, u32[]{:S(2)}, u32[]{:S(2)}) collective-permute-start(bf16[256,256]{1,0:T(8,128)(2,1)} %param.10), channel_id=1, source_target_pairs={{0,0},{1,128},{2,256},{3,384},{4,16},{5,144},{6,272},{7,400},{8,32... | collective-permute-start | bytes 393224 | tf_op jit(solution)/shard_map/ppermute | solution.py:32
  13.3 92.7 %copy-start.5 = (bf16[896,256]{1,0:T(8,128)(2,1)S(1)}, bf16[896,256]{1,0:T(8,128)(2,1)}, u32[]{:S(2)}) copy-start(bf16[896,256]{1,0:T(8,128)(2,1)} %param.8) | copy-start | bytes 1376260
  13.3 23.0 %all-to-all-start = ((s32[32,1,128]{2,1,0:T(1,128)}), s32[32,1,128]{2,1,0:T(1,128)S(1)}, u32[]{:S(2)}, u32[]{:S(2)}) async-start(s32[32,1,128]{2,1,0:T(1,128)} %broadcast_in_dim.30), calls=%async_computation | async-start | bytes 32768 | tf_op jit(solution)/shard_map/all_to_all | solution.py:131
  36.3 0.6 copy-start.3
  38.7 30.0 %all-to-all-start.1 = ((bf16[32,8,896]{2,1,0:T(8,128)(2,1)}), bf16[32,8,896]{2,1,0:T(8,128)(2,1)S(1)}, u32[]{:S(2)}, u32[]{:S(2)}) async-start(bf16[32,8,896]{2,1,0:T(8,128)(2,1)} %bitcast.31), calls=%async_computation.1 | async-start | bytes 917504 | tf_op jit(solution)/shard_map/all_to_all | solution.py:163
  45.6 97.4 %all-gather.3.cloned.1.call-start = ((), (), s32[]{:S(2)}) async-start(), calls=%async_computation.4 | async-start | bytes 4718592 | tf_op jit(solution)/shard_map/all_gather | solution.py:47
  45.6 11.7 %collective-permute-start.1 = (bf16[256,256]{1,0:T(8,128)(2,1)S(1)}, bf16[256,256]{1,0:T(8,128)(2,1)S(1)}, u32[]{:S(2)}, u32[]{:S(2)}) collective-permute-start(bf16[256,256]{1,0:T(8,128)(2,1)S(1)} %collective-permute-done), channel_id=1, source_target_pairs={{0,128},{16,144},{32,160},{48,176},{64,192},{80,208},{96,224},{112... | collective-permute-start | bytes 393224 | tf_op jit(solution)/shard_map/ppermute | solution.py:40
  48.8 14.6 %collective-permute-start.2 = (bf16[256,256]{1,0:T(8,128)(2,1)S(1)}, bf16[256,256]{1,0:T(8,128)(2,1)S(1)}, u32[]{:S(2)}, u32[]{:S(2)}) collective-permute-start(bf16[256,256]{1,0:T(8,128)(2,1)S(1)} %collective-permute-done), channel_id=1, source_target_pairs={{0,256},{16,272},{32,288},{48,304},{64,320},{80,336},{96,352},{112... | collective-permute-start | bytes 393224 | tf_op jit(solution)/shard_map/ppermute | solution.py:40
  50.9 16.8 %collective-permute-start.3 = (bf16[256,256]{1,0:T(8,128)(2,1)S(1)}, bf16[256,256]{1,0:T(8,128)(2,1)S(1)}, u32[]{:S(2)}, u32[]{:S(2)}) collective-permute-start(bf16[256,256]{1,0:T(8,128)(2,1)S(1)} %collective-permute-done), channel_id=1, source_target_pairs={{0,384},{16,400},{32,416},{48,432},{64,448},{80,464},{96,480},{112... | collective-permute-start | bytes 393224 | tf_op jit(solution)/shard_map/ppermute | solution.py:40
  68.6 1.4 copy-start.2
  72.1 33.8 %all-to-all-start.2 = ((bf16[16,4,8,896]{3,2,1,0:T(8,128)(2,1)}), bf16[16,4,8,896]{3,2,1,0:T(8,128)(2,1)S(1)}, u32[]{:S(2)}, u32[]{:S(2)}) async-start(bf16[16,4,8,896]{3,2,1,0:T(8,128)(2,1)} %pick.3), calls=%async_computation.2 | async-start | bytes 1835008 | tf_op jit(solution)/shard_map/all_to_all | solution.py:150
  110.2 32.8 %all-to-all-start.3 = ((bf16[16,128,256]{2,1,0:T(8,128)(2,1)}), bf16[16,128,256]{2,1,0:T(8,128)(2,1)S(1)}, u32[]{:S(2)}, u32[]{:S(2)}) async-start(bf16[16,128,256]{2,1,0:T(8,128)(2,1)} %broadcast_in_dim.32), calls=%async_computation.3 | async-start | bytes 2097152 | tf_op jit(solution)/shard_map/all_to_all | solution.py:188
  143.0 1.0 copy-start.1
Sparse Core Ops, SparseCore 0:
  68.8 55.8 all-gather.2

commit v10 on v9

--- a/solution.py
+++ b/solution.py
@@ -144,47 +144,77 @@
 
 def near_rows(arrived, neighbours):
     mp_count = lax.axis_size("mp")
-    part_rows, enc_width = arrived.shape[1:]
-    per_owner = neighbours.size
     copies = pick(neighbours.reshape(-1, 1) // BLK_DEV, arrived, mp_count)
-    gathered = lax.all_to_all(copies, "mp", split_axis=0, concat_axis=0, tiled=True)
-    gathered = gathered.reshape(mp_count, per_owner // NEIGH, NEIGH * part_rows, enc_width)
-    return gathered.transpose(1, 0, 2, 3).reshape(-1, enc_width)
+    return lax.all_to_all(copies, "mp", split_axis=0, concat_axis=0, tiled=True)
+
+
+def attend(rows, queries, key_weight, value_weight, copies):
+    source_count, block_count, part_rows, enc_width = rows.shape
+    tokens, inner_width = queries.shape
+    span_count = tokens // SPAN
+    span_rows = NEIGH * part_rows
+    scale = 1.0 / math.sqrt(HEAD_DIM)
+
+    def body(rows_ref, queries_ref, key_ref, value_ref, out_ref, encoded_ref):
+        for source in range(source_count):
+            for block in range(block_count):
+                span, place = divmod(block, NEIGH)
+                start = (span * source_count + source) * span_rows + place * part_rows
+                encoded_ref[start : start + part_rows] = rows_ref[source, block]
+        encoded = encoded_ref[...]
+        keys = jnp.dot(encoded, key_ref[...], preferred_element_type=jnp.float32)
+        keys = keys.astype(jnp.bfloat16)
+        values = jnp.dot(encoded, value_ref[...], preferred_element_type=jnp.float32)
+        values = values.astype(jnp.bfloat16)
+        for span in range(span_count):
+            own = slice(span * NEIGH * NROW, (span + 1) * NEIGH * NROW)
+            own_tokens = slice(span * SPAN, (span + 1) * SPAN)
+            for head in range(inner_width // HEAD_DIM):
+                lanes = slice(head * HEAD_DIM, (head + 1) * HEAD_DIM)
+                scores = lax.dot_general(
+                    queries_ref[own_tokens, lanes],
+                    keys[own, lanes],
+                    (((1,), (1,)), ((), ())),
+                    preferred_element_type=jnp.float32,
+                )
+                scores = scores * scale
+                weights = jnp.exp(scores - jnp.max(scores, axis=-1, keepdims=True))
+                weights = weights / jnp.sum(weights, axis=-1, keepdims=True)
+                result = jnp.dot(
+                    weights.astype(jnp.bfloat16),
+                    values[own, lanes],
+                    preferred_element_type=jnp.float32,
+                ).astype(out_ref.dtype)
+                for copy in range(copies):
+                    out_ref[copy, own_tokens, lanes] = result
+
+    return pl.pallas_call(
+        body,
+        out_shape=jax.ShapeDtypeStruct((copies, tokens, inner_width), jnp.bfloat16),
+        in_specs=[pl.BlockSpec(memory_space=pltpu.VMEM)] * 4,
+        out_specs=pl.BlockSpec(memory_space=pltpu.VMEM),
+        scratch_shapes=[pltpu.VMEM((block_count * NROW, enc_width), jnp.bfloat16)],
+        cost_estimate=pl.CostEstimate(
+            flops=4 * block_count * NROW * enc_width * inner_width,
+            bytes_accessed=2 * (rows.size + 2 * key_weight.size + copies * queries.size),
+            transcendentals=span_count * SPAN * NEIGH * NROW * inner_width // HEAD_DIM,
+        ),
+        name="attend",
+    )(rows, queries, key_weight, value_weight)
 
 
 def on_device(queries, database, key_weight, value_weight, out_weight, neighbours):
-    span_count = neighbours.shape[0]
-    inner_width = key_weight.shape[1]
-    head_count = inner_width // HEAD_DIM
     mp_count = lax.axis_size("mp")
     moved = weight_block(out_weight)
-    wanted, _ = lax.optimization_barrier((request(neighbours), moved))
-    outgoing = rows_to_send(database, wanted)
+    outgoing = rows_to_send(database, request(neighbours))
+    outgoing, _ = lax.optimization_barrier((outgoing, moved))
     arrived = lax.all_to_all(outgoing, "dp", split_axis=0, concat_axis=0, tiled=True)
     arrived, piece = lax.optimization_barrier((arrived, far_blocks(moved)))
     columns = near_gather(piece)
     ratio = lax.axis_size("dp") // mp_count
     columns = columns.reshape(ratio, -1, *columns.shape[1:])
-    encoded_rows = near_rows(arrived, neighbours)
-    near_keys = jnp.dot(encoded_rows, key_weight, preferred_element_type=jnp.float32).astype(
-        jnp.bfloat16
-    )
-    near_values = jnp.dot(encoded_rows, value_weight, preferred_element_type=jnp.float32).astype(
-        jnp.bfloat16
-    )
-    key_blocks = near_keys.reshape(span_count, NEIGH * NROW, head_count, HEAD_DIM)
-    value_blocks = near_values.reshape(span_count, NEIGH * NROW, head_count, HEAD_DIM)
-    query_blocks = queries.reshape(span_count, SPAN, head_count, HEAD_DIM)
-    scores = jnp.einsum(
-        "cqhd,ckhd->chqk", query_blocks, key_blocks, preferred_element_type=jnp.float32
-    )
-    scores = scores / math.sqrt(HEAD_DIM)
-    weights = jax.nn.softmax(scores, axis=-1).astype(jnp.bfloat16)
-    attended = jnp.einsum(
-        "chqk,ckhd->cqhd", weights, value_blocks, preferred_element_type=jnp.float32
-    )
-    attended = attended.astype(jnp.bfloat16).reshape(span_count * SPAN, inner_width)
-    copies = jnp.broadcast_to(attended[None], (mp_count, *attended.shape))
+    rows = near_rows(arrived, neighbours)
+    copies = attend(rows, queries, key_weight, value_weight, mp_count)
     attended = lax.all_to_all(copies, "mp", split_axis=0, concat_axis=0, tiled=True)
     return product(attended, columns)
 

time: 156 us -> 156 us (level)
  the two profiles are of different devices: /device:TPU:17 before, /device:TPU:8 now
where the time goes in v10:
time: 156 us; the launch traced here: 155 us
  waiting for transfers between devices  49.8 us (32%)
  starting transfers between devices  39.1 us (25%)
  blocking collectives  33.7 us (22%)
  between operations  13.5 us (9%)
  Pallas kernels  12.6 us (8%)
  local copies, waits for them, and re-layouts  4.47 us (3%)
  other arithmetic  1.57 us (1%)
    all_to_all x1, blocking collectives, near_rows(): return lax.all_to_all(copies, 'mp', split_axis=0, concat_axis=0, tiled=True)  33.7 us
    all_to_all x1, waiting for transfers between devices, on_device(): lax.all_to_all(copies, 'mp', split_axis=0, concat_axis=0, tiled=True)  28.7 us
    all_to_all x1, starting transfers between devices, request(): return lax.all_to_all(asked, 'dp', split_axis=0, concat_axis=0, tiled=True)  17.8 us
    ppermute x3, waiting for transfers between devices, far_blocks(): blocks.append(lax.ppermute(moved, 'dp', pairs))  12.8 us
    ppermute x3, starting transfers between devices, far_blocks(): blocks.append(lax.ppermute(moved, 'dp', pairs))  9.21 us
    all_to_all x1, waiting for transfers between devices, request(): return lax.all_to_all(asked, 'dp', split_axis=0, concat_axis=0, tiled=True)  8.25 us
    all_to_all x1, starting transfers between devices, on_device(): lax.all_to_all(outgoing, 'dp', split_axis=0, concat_axis=0, tiled=True)  5.04 us
    pallas_call x1, Pallas kernels, product(): pl.pallas_call(body, out_shape=jax.ShapeDtypeStruct((tokens, part_count *...  4.55 us
  transfers between devices with their start and end apart: 8, of which 5 were waited for; matrix products, arithmetic and copies ran while one was open for 3% of the time, Pallas kernels for 5%

profile of v10, /device:TPU:8, one launch (start us, length us, event | category | flops | bytes accessed | tf_op | source)
XLA Modules:
  0.0 154.7 jit_solution(1625168124745225592)
XLA Ops:
  6.5 0.0 copy-start
  6.5 3.4 %collective-permute-start = (bf16[256,256]{1,0:T(8,128)(2,1)}, bf16[256,256]{1,0:T(8,128)(2,1)S(1)}, u32[]{:S(2)}, u32[]{:S(2)}) collective-permute-start(bf16[256,256]{1,0:T(8,128)(2,1)} %param.10), channel_id=1, source_target_pairs={{0,0},{1,128},{2,256},{3,384},{4,16},{5,144},{6,272},{7,400},{8,32... | collective-permute-start | bytes 393224 | tf_op jit(solution)/shard_map/ppermute | solution.py:32
  9.9 0.8 reshape.211
  10.7 0.1 select_reduce_fusion
  10.8 0.7 broadcast_in_dim.21
  11.5 17.8 %all-to-all-start = ((s32[32,1,128]{2,1,0:T(1,128)}), s32[32,1,128]{2,1,0:T(1,128)S(1)}, u32[]{:S(2)}, u32[]{:S(2)}) async-start(s32[32,1,128]{2,1,0:T(1,128)} %broadcast_in_dim.21), calls=%async_computation | async-start | bytes 32768 | tf_op jit(solution)/shard_map/all_to_all | solution.py:131
  29.3 0.0 copy-done
  29.3 0.6 constant_dynamic-slice_fusion.blocks_ref
  30.0 8.3 %all-to-all-done = s32[32,1,128]{2,1,0:T(1,128)S(1)} async-done(((s32[32,1,128]{2,1,0:T(1,128)}), s32[32,1,128]{2,1,0:T(1,128)S(1)}, u32[]{:S(2)}, u32[]{:S(2)}) %all-to-all-start) | async-done | bytes 16416 | tf_op jit(solution)/shard_map/all_to_all | solution.py:131
  38.2 0.0 copy-start.3
  38.2 0.6 copy-done.3
  38.8 1.7 %pick.2 = bf16[1,32,8,896]{3,2,1,0:T(8,128)(2,1)} custom-call(s32[32,128]{1,0:T(8,128)} %bitcast.16, bf16[4,8,896]{2,1,0:T(8,128)(2,1)} %constant_dynamic-slice_fusion.blocks_ref), custom_call_target="tpu_custom_call" | custom-call | tf_op jit(solution)/shard_map/pick/pallas_call | solution.py:111
  40.6 0.0 collective-permute-done
  40.6 5.0 %all-to-all-start.1 = ((bf16[32,8,896]{2,1,0:T(8,128)(2,1)}), bf16[32,8,896]{2,1,0:T(8,128)(2,1)S(1)}, u32[]{:S(2)}, u32[]{:S(2)}) async-start(bf16[32,8,896]{2,1,0:T(8,128)(2,1)} %bitcast.11), calls=%async_computation.1 | async-start | bytes 917504 | tf_op jit(solution)/shard_map/all_to_all | solution.py:211
  45.6 0.0 all-gather.3.cloned.1.call-start
  45.6 2.2 %collective-permute-start.1 = (bf16[256,256]{1,0:T(8,128)(2,1)S(1)}, bf16[256,256]{1,0:T(8,128)(2,1)S(1)}, u32[]{:S(2)}, u32[]{:S(2)}) collective-permute-start(bf16[256,256]{1,0:T(8,128)(2,1)S(1)} %collective-permute-done), channel_id=1, source_target_pairs={{0,128},{16,144},{32,160},{48,176},{64,192},{80,208},{96,224},{112... | collective-permute-start | bytes 393224 | tf_op jit(solution)/shard_map/ppermute | solution.py:40
  47.9 4.6 %collective-permute-start.2 = (bf16[256,256]{1,0:T(8,128)(2,1)S(1)}, bf16[256,256]{1,0:T(8,128)(2,1)S(1)}, u32[]{:S(2)}, u32[]{:S(2)}) collective-permute-start(bf16[256,256]{1,0:T(8,128)(2,1)S(1)} %collective-permute-done), channel_id=1, source_target_pairs={{0,256},{16,272},{32,288},{48,304},{64,320},{80,336},{96,352},{112... | collective-permute-start | bytes 393224 | tf_op jit(solution)/shard_map/ppermute | solution.py:40
  52.5 2.4 %collective-permute-start.3 = (bf16[256,256]{1,0:T(8,128)(2,1)S(1)}, bf16[256,256]{1,0:T(8,128)(2,1)S(1)}, u32[]{:S(2)}, u32[]{:S(2)}) collective-permute-start(bf16[256,256]{1,0:T(8,128)(2,1)S(1)} %collective-permute-done), channel_id=1, source_target_pairs={{0,384},{16,400},{32,416},{48,432},{64,448},{80,464},{96,480},{112... | collective-permute-start | bytes 393224 | tf_op jit(solution)/shard_map/ppermute | solution.py:40
  54.9 2.8 %collective-permute-done.1 = bf16[256,256]{1,0:T(8,128)(2,1)S(1)} collective-permute-done((bf16[256,256]{1,0:T(8,128)(2,1)S(1)}, bf16[256,256]{1,0:T(8,128)(2,1)S(1)}, u32[]{:S(2)}, u32[]{:S(2)}) %collective-permute-start.1) | collective-permute-done | bytes 131104 | tf_op jit(solution)/shard_map/ppermute | solution.py:40
  57.7 5.9 %collective-permute-done.2 = bf16[256,256]{1,0:T(8,128)(2,1)S(1)} collective-permute-done((bf16[256,256]{1,0:T(8,128)(2,1)S(1)}, bf16[256,256]{1,0:T(8,128)(2,1)S(1)}, u32[]{:S(2)}, u32[]{:S(2)}) %collective-permute-start.2) | collective-permute-done | bytes 131104 | tf_op jit(solution)/shard_map/ppermute | solution.py:40
  63.6 4.1 %collective-permute-done.3 = bf16[256,256]{1,0:T(8,128)(2,1)S(1)} collective-permute-done((bf16[256,256]{1,0:T(8,128)(2,1)S(1)}, bf16[256,256]{1,0:T(8,128)(2,1)S(1)}, u32[]{:S(2)}, u32[]{:S(2)}) %collective-permute-start.3) | collective-permute-done | bytes 131104 | tf_op jit(solution)/shard_map/ppermute | solution.py:40
  67.6 0.9 pad_maximum_fusion
  68.5 0.0 all-to-all-done.1.blocks_ref
  68.5 0.0 copy-start.2
  68.5 0.0 all-gather.3.cloned.1.call-update
  68.6 0.8 reshape.216
  69.4 0.6 add_select_fusion.indices_ref
  69.9 0.0 copy-done.2
  69.9 2.0 %pick.3 = bf16[16,4,8,896]{3,2,1,0:T(8,128)(2,1)} custom-call(s32[4,1]{1,0:T(4,128)} %add_select_fusion.indices_ref, bf16[32,8,896]{2,1,0:T(8,128)(2,1)} %copy-done.2), custom_call_target="tpu_custom_call" | custom-call | tf_op jit(solution)/shard_map/pick/pallas_call | solution.py:111
  72.0 33.7 %all_to_all.23.rows_ref = bf16[16,4,8,896]{3,2,1,0:T(8,128)(2,1)} all-to-all(bf16[16,4,8,896]{3,2,1,0:T(8,128)(2,1)} %pick.3), channel_id=1, replica_groups=mesh['dp'=32,'mp'=16] {'mp'}, dimensions={0} | all-to-all | bytes 1835008 | tf_op jit(solution)/shard_map/all_to_all | solution.py:148
  105.7 4.3 %attend.1 = bf16[16,128,256]{2,1,0:T(8,128)(2,1)} custom-call(bf16[16,4,8,896]{3,2,1,0:T(8,128)(2,1)} %all_to_all.23.rows_ref, bf16[128,256]{1,0:T(8,128)(2,1)} %queries_ref.1, bf16[896,256]{1,0:T(8,128)(2,1)} %key_ref.1, bf16[896,256]{1,0:T(8,128)(2,1)} %value_ref.1), custom_call_target="tpu_custom_call" | custom-call | flops 469762048 | bytes 2883584 | tf_op jit(solution)/shard_map/attend/pallas_call | solution.py:191
  110.0 3.7 %all-to-all-start.3 = ((bf16[16,128,256]{2,1,0:T(8,128)(2,1)}), bf16[16,128,256]{2,1,0:T(8,128)(2,1)S(1)}, u32[]{:S(2)}, u32[]{:S(2)}) async-start(bf16[16,128,256]{2,1,0:T(8,128)(2,1)} %attend.1), calls=%async_computation.3 | async-start | bytes 2097152 | tf_op jit(solution)/shard_map/all_to_all | solution.py:218
  113.6 28.7 %all-to-all-done.3.attended_ref = bf16[16,128,256]{2,1,0:T(8,128)(2,1)S(1)} async-done(((bf16[16,128,256]{2,1,0:T(8,128)(2,1)}), bf16[16,128,256]{2,1,0:T(8,128)(2,1)S(1)}, u32[]{:S(2)}, u32[]{:S(2)}) %all-to-all-start.3) | async-done | bytes 1048608 | tf_op jit(solution)/shard_map/all_to_all | solution.py:218
  142.4 0.0 copy-start.1
  142.4 0.0 all-gather.3.cloned.1.call-done
  142.4 1.0 copy-done.1
  143.4 4.6 %product.1 = bf16[128,512]{1,0:T(8,128)(2,1)} custom-call(s32[1]{0:T(128)} %bitcast.far_ref, bf16[16,128,256]{2,1,0:T(8,128)(2,1)} %copy-done.1, bf16[2,4,4,256,256]{4,3,2,1,0:T(8,128)(2,1)} %bitcast.10), custom_call_target="tpu_custom_call" | custom-call | flops 536870912 | bytes 4194304 | tf_op jit(solution)/shard_map/product/pallas_call | solution.py:79
  (1 shorter events, 0.0 us)
Async XLA Ops:
  6.5 22.8 %copy-start = (bf16[512,896]{1,0:T(8,128)(2,1)S(1)}, bf16[512,896]{1,0:T(8,128)(2,1)}, u32[]{:S(2)}) copy-start(bf16[512,896]{1,0:T(8,128)(2,1)} %param.7) | copy-start | bytes 2752516
  6.5 34.0 %collective-permute-start = (bf16[256,256]{1,0:T(8,128)(2,1)}, bf16[256,256]{1,0:T(8,128)(2,1)S(1)}, u32[]{:S(2)}, u32[]{:S(2)}) collective-permute-start(bf16[256,256]{1,0:T(8,128)(2,1)} %param.10), channel_id=1, source_target_pairs={{0,0},{1,128},{2,256},{3,384},{4,16},{5,144},{6,272},{7,400},{8,32... | collective-permute-start | bytes 393224 | tf_op jit(solution)/shard_map/ppermute | solution.py:32
  11.5 26.7 %all-to-all-start = ((s32[32,1,128]{2,1,0:T(1,128)}), s32[32,1,128]{2,1,0:T(1,128)S(1)}, u32[]{:S(2)}, u32[]{:S(2)}) async-start(s32[32,1,128]{2,1,0:T(1,128)} %broadcast_in_dim.21), calls=%async_computation | async-start | bytes 32768 | tf_op jit(solution)/shard_map/all_to_all | solution.py:131
  38.2 0.6 copy-start.3
  40.6 28.0 %all-to-all-start.1 = ((bf16[32,8,896]{2,1,0:T(8,128)(2,1)}), bf16[32,8,896]{2,1,0:T(8,128)(2,1)S(1)}, u32[]{:S(2)}, u32[]{:S(2)}) async-start(bf16[32,8,896]{2,1,0:T(8,128)(2,1)} %bitcast.11), calls=%async_computation.1 | async-start | bytes 917504 | tf_op jit(solution)/shard_map/all_to_all | solution.py:211
  45.6 96.8 %all-gather.3.cloned.1.call-start = ((), (), s32[]{:S(2)}) async-start(), calls=%async_computation.4 | async-start | bytes 4718592 | tf_op jit(solution)/shard_map/all_gather | solution.py:47
  45.6 12.0 %collective-permute-start.1 = (bf16[256,256]{1,0:T(8,128)(2,1)S(1)}, bf16[256,256]{1,0:T(8,128)(2,1)S(1)}, u32[]{:S(2)}, u32[]{:S(2)}) collective-permute-start(bf16[256,256]{1,0:T(8,128)(2,1)S(1)} %collective-permute-done), channel_id=1, source_target_pairs={{0,128},{16,144},{32,160},{48,176},{64,192},{80,208},{96,224},{112... | collective-permute-start | bytes 393224 | tf_op jit(solution)/shard_map/ppermute | solution.py:40
  47.9 15.7 %collective-permute-start.2 = (bf16[256,256]{1,0:T(8,128)(2,1)S(1)}, bf16[256,256]{1,0:T(8,128)(2,1)S(1)}, u32[]{:S(2)}, u32[]{:S(2)}) collective-permute-start(bf16[256,256]{1,0:T(8,128)(2,1)S(1)} %collective-permute-done), channel_id=1, source_target_pairs={{0,256},{16,272},{32,288},{48,304},{64,320},{80,336},{96,352},{112... | collective-permute-start | bytes 393224 | tf_op jit(solution)/shard_map/ppermute | solution.py:40
  52.5 15.2 %collective-permute-start.3 = (bf16[256,256]{1,0:T(8,128)(2,1)S(1)}, bf16[256,256]{1,0:T(8,128)(2,1)S(1)}, u32[]{:S(2)}, u32[]{:S(2)}) collective-permute-start(bf16[256,256]{1,0:T(8,128)(2,1)S(1)} %collective-permute-done), channel_id=1, source_target_pairs={{0,384},{16,400},{32,416},{48,432},{64,448},{80,464},{96,480},{112... | collective-permute-start | bytes 393224 | tf_op jit(solution)/shard_map/ppermute | solution.py:40
  68.5 1.4 copy-start.2
  110.0 32.4 %all-to-all-start.3 = ((bf16[16,128,256]{2,1,0:T(8,128)(2,1)}), bf16[16,128,256]{2,1,0:T(8,128)(2,1)S(1)}, u32[]{:S(2)}, u32[]{:S(2)}) async-start(bf16[16,128,256]{2,1,0:T(8,128)(2,1)} %attend.1), calls=%async_computation.3 | async-start | bytes 2097152 | tf_op jit(solution)/shard_map/all_to_all | solution.py:218
  142.4 1.0 copy-start.1
Sparse Core Ops, SparseCore 0:
  68.7 55.9 all-gather.2

commit v11 on v10

--- a/solution.py
+++ b/solution.py
@@ -15,29 +15,25 @@
 
 
 NEAR_DP = 8
+LOCAL_MP = 4
 LANES = 128
 
 
-def weight_block(out_weight):
+def far_blocks(out_weight):
     dp_count = lax.axis_size("dp")
     mp_count = lax.axis_size("mp")
-    ratio = dp_count // mp_count
-    far_count = dp_count // NEAR_DP
-    moves = []
-    for d in range(dp_count):
-        for m in range(mp_count):
-            near = d % ratio * (mp_count // far_count) + m // far_count
-            place = m % far_count * NEAR_DP + near
-            moves.append((d * mp_count + m, place * mp_count + d // ratio))
-    return lax.ppermute(out_weight, ("dp", "mp"), moves)
-
-
-def far_blocks(moved):
-    dp_count = lax.axis_size("dp")
-    blocks = [moved]
-    for step in range(1, dp_count // NEAR_DP):
-        pairs = [(d, d ^ (step * NEAR_DP)) for d in range(dp_count)]
-        blocks.append(lax.ppermute(moved, "dp", pairs))
+    ratio = NEAR_DP // LOCAL_MP
+    blocks = []
+    for step in range(dp_count // NEAR_DP):
+        moves = []
+        for d in range(dp_count):
+            for m in range(mp_count):
+                near = d % NEAR_DP
+                local = m % LOCAL_MP
+                to_near = near % ratio * LOCAL_MP + local
+                to_d = (d - near) ^ (step * NEAR_DP) | to_near
+                moves.append((d * mp_count + m, to_d * mp_count + m - local + near // ratio))
+        blocks.append(lax.ppermute(out_weight, ("dp", "mp"), moves))
     return jnp.stack(blocks)
 
 
@@ -47,57 +43,51 @@
     return lax.all_gather(piece, "dp", axis=0, axis_index_groups=groups)
 
 
-def product(attended, columns):
-    part_count, outer_count, far_count, row_count, width = columns.shape
+def exchange(blocks, groups):
+    return lax.all_to_all(
+        blocks, "mp", split_axis=0, concat_axis=0, axis_index_groups=groups, tiled=True
+    )
+
+
+def partial_products(attended, columns):
+    part_count, local_count, far_count, row_count, width = columns.shape
     tokens = attended.shape[1]
     far = (lax.axis_index("dp") // NEAR_DP).astype(jnp.int32).reshape(1)
 
-    def body(far_ref, attended_ref, columns_ref, out_ref, total_ref):
-        outer = pl.program_id(0)
-        parts = [jnp.zeros((tokens, width), jnp.float32) for _ in range(part_count)]
-        for slot in range(far_count):
-            block = attended_ref[outer * far_count + (slot ^ far_ref[0])]
-            for part in range(part_count):
-                parts[part] += jnp.dot(
-                    block, columns_ref[part, 0, slot], preferred_element_type=jnp.float32
+    def body(far_ref, attended_ref, columns_ref, out_ref):
+        for part in range(part_count):
+            total = jnp.zeros((tokens, width), jnp.float32)
+            for local in range(local_count):
+                total += jnp.dot(
+                    attended_ref[local],
+                    columns_ref[part, local, 0],
+                    preferred_element_type=jnp.float32,
                 )
-        for part in range(part_count):
-            lanes = slice(part * width, (part + 1) * width)
-
-            @pl.when(outer == 0)
-            def _():
-                total_ref[:, lanes] = parts[part]
-
-            @pl.when(outer > 0)
-            def _():
-                total_ref[:, lanes] += parts[part]
-
-        @pl.when(outer == outer_count - 1)
-        def _():
-            out_ref[...] = total_ref[...].astype(out_ref.dtype)
+            out_ref[0, :, part * width : (part + 1) * width] = total.astype(out_ref.dtype)
 
     return pl.pallas_call(
         body,
-        out_shape=jax.ShapeDtypeStruct((tokens, part_count * width), attended.dtype),
+        out_shape=jax.ShapeDtypeStruct((far_count, tokens, part_count * width), attended.dtype),
         grid_spec=pltpu.PrefetchScalarGridSpec(
             num_scalar_prefetch=1,
-            grid=(outer_count,),
+            grid=(far_count,),
             in_specs=[
                 pl.BlockSpec(attended.shape, lambda i, far_ref: (0, 0, 0)),
                 pl.BlockSpec(
-                    (part_count, 1, far_count, row_count, width),
-                    lambda i, far_ref: (0, i, 0, 0, 0),
+                    (part_count, local_count, 1, row_count, width),
+                    lambda i, far_ref: (0, 0, i ^ far_ref[0], 0, 0),
                 ),
             ],
-            out_specs=pl.BlockSpec((tokens, part_count * width), lambda i, far_ref: (0, 0)),
-            scratch_shapes=[pltpu.VMEM((tokens, part_count * width), jnp.float32)],
+            out_specs=pl.BlockSpec(
+                (1, tokens, part_count * width), lambda i, far_ref: (i, 0, 0)
+            ),
         ),
         cost_estimate=pl.CostEstimate(
             flops=2 * tokens * columns.size,
             bytes_accessed=2 * columns.size,
             transcendentals=0,
         ),
-        name="product",
+        name="partial_products",
     )(far, attended, columns)
 
 
@@ -205,18 +195,18 @@
 
 def on_device(queries, database, key_weight, value_weight, out_weight, neighbours):
     mp_count = lax.axis_size("mp")
-    moved = weight_block(out_weight)
-    outgoing = rows_to_send(database, request(neighbours))
-    outgoing, _ = lax.optimization_barrier((outgoing, moved))
+    wanted, piece = lax.optimization_barrier((request(neighbours), far_blocks(out_weight)))
+    outgoing = rows_to_send(database, wanted)
+    columns = near_gather(piece)
+    columns = columns.reshape(-1, LOCAL_MP, *columns.shape[1:])
     arrived = lax.all_to_all(outgoing, "dp", split_axis=0, concat_axis=0, tiled=True)
-    arrived, piece = lax.optimization_barrier((arrived, far_blocks(moved)))
-    columns = near_gather(piece)
-    ratio = lax.axis_size("dp") // mp_count
-    columns = columns.reshape(ratio, -1, *columns.shape[1:])
     rows = near_rows(arrived, neighbours)
-    copies = attend(rows, queries, key_weight, value_weight, mp_count)
-    attended = lax.all_to_all(copies, "mp", split_axis=0, concat_axis=0, tiled=True)
-    return product(attended, columns)
+    copies = attend(rows, queries, key_weight, value_weight, LOCAL_MP)
+    local_groups = [list(range(m, m + LOCAL_MP)) for m in range(0, mp_count, LOCAL_MP)]
+    ring_groups = [list(range(r, mp_count, LOCAL_MP)) for r in range(LOCAL_MP)]
+    partials = partial_products(exchange(copies, local_groups), columns)
+    partials = exchange(partials, ring_groups).astype(jnp.float32)
+    return jnp.sum(partials, axis=0).astype(jnp.bfloat16)
 
 
 def solution(mesh):

time: 156 us -> 159 us (1.019)
  the two profiles are of different devices: /device:TPU:8 before, /device:TPU:16 now
where the time goes in v11:
time: 159 us
  blocking collectives  47.1 us (30%)
  starting transfers between devices  44.4 us (28%)
  waiting for transfers between devices  34.6 us (22%)
  between operations  13.5 us (8%)
  Pallas kernels  12.2 us (8%)
  local copies, waits for them, and re-layouts  4.37 us (3%)
  other arithmetic  2.32 us (1%)
    all_to_all x1, blocking collectives, near_rows(): return lax.all_to_all(copies, 'mp', split_axis=0, concat_axis=0, tiled=True)  34 us
    all_to_all x1, starting transfers between devices, request(): return lax.all_to_all(asked, 'dp', split_axis=0, concat_axis=0, tiled=True)  19 us
    all_to_all x1, waiting for transfers between devices, on_device(): lax.all_to_all(outgoing, 'dp', split_axis=0, concat_axis=0, tiled=True)  14.5 us
    ppermute x4, starting transfers between devices, far_blocks(): blocks.append(lax.ppermute(out_weight, ('dp', 'mp'), moves))  13.7 us
    all_to_all x1, blocking collectives, exchange(): lax.all_to_all(blocks, 'mp', split_axis=0, concat_axis=0, axis_index_grou...  13.1 us
    all_to_all x1, waiting for transfers between devices, request(): return lax.all_to_all(asked, 'dp', split_axis=0, concat_axis=0, tiled=True)  10.2 us
    all_to_all x1, waiting for transfers between devices, exchange(): lax.all_to_all(blocks, 'mp', split_axis=0, concat_axis=0, axis_index_grou...  9.89 us
    all_to_all x1, starting transfers between devices, on_device(): lax.all_to_all(outgoing, 'dp', split_axis=0, concat_axis=0, tiled=True)  8.33 us
  transfers between devices with their start and end apart: 8, of which 3 were waited for; matrix products, arithmetic and copies ran while one was open for 3% of the time, Pallas kernels for 5%

profile of v11, /device:TPU:16, one launch (start us, length us, event | category | flops | bytes accessed | tf_op | source)
XLA Modules:
  0.0 158.5 jit_solution(15834929264231297799)
XLA Ops:
  6.5 0.0 copy-start
  6.5 1.7 %collective-permute-start = (bf16[256,256]{1,0:T(8,128)(2,1)}, bf16[256,256]{1,0:T(8,128)(2,1)S(1)}, u32[]{:S(2)}, u32[]{:S(2)}) collective-permute-start(bf16[256,256]{1,0:T(8,128)(2,1)} %param.10), channel_id=1, source_target_pairs={{0,0},{1,16},{2,32},{3,48},{4,4},{5,20},{6,36},{7,52},{8,8},{9,24}... | collective-permute-start | bytes 393224 | tf_op jit(solution)/shard_map/ppermute | solution.py:36
  8.2 3.5 %collective-permute-start.1 = (bf16[256,256]{1,0:T(8,128)(2,1)}, bf16[256,256]{1,0:T(8,128)(2,1)S(1)}, u32[]{:S(2)}, u32[]{:S(2)}) collective-permute-start(bf16[256,256]{1,0:T(8,128)(2,1)} %param.10), channel_id=1, source_target_pairs={{0,128},{1,144},{2,160},{3,176},{4,132},{5,148},{6,164},{7,180},{8... | collective-permute-start | bytes 393224 | tf_op jit(solution)/shard_map/ppermute | solution.py:36
  11.7 6.1 %collective-permute-start.2 = (bf16[256,256]{1,0:T(8,128)(2,1)}, bf16[256,256]{1,0:T(8,128)(2,1)S(1)}, u32[]{:S(2)}, u32[]{:S(2)}) collective-permute-start(bf16[256,256]{1,0:T(8,128)(2,1)} %param.10), channel_id=1, source_target_pairs={{0,256},{1,272},{2,288},{3,304},{4,260},{5,276},{6,292},{7,308},{8... | collective-permute-start | bytes 393224 | tf_op jit(solution)/shard_map/ppermute | solution.py:36
  17.8 2.5 %collective-permute-start.3 = (bf16[256,256]{1,0:T(8,128)(2,1)}, bf16[256,256]{1,0:T(8,128)(2,1)S(1)}, u32[]{:S(2)}, u32[]{:S(2)}) collective-permute-start(bf16[256,256]{1,0:T(8,128)(2,1)} %param.10), channel_id=1, source_target_pairs={{0,384},{1,400},{2,416},{3,432},{4,388},{5,404},{6,420},{7,436},{8... | collective-permute-start | bytes 393224 | tf_op jit(solution)/shard_map/ppermute | solution.py:36
  20.2 0.8 reshape.211
  21.0 0.1 select_reduce_fusion
  21.1 0.7 broadcast_in_dim.21
  21.8 19.0 %all-to-all-start = ((s32[32,1,128]{2,1,0:T(1,128)}), s32[32,1,128]{2,1,0:T(1,128)S(1)}, u32[]{:S(2)}, u32[]{:S(2)}) async-start(s32[32,1,128]{2,1,0:T(1,128)} %broadcast_in_dim.21), calls=%async_computation | async-start | bytes 32768 | tf_op jit(solution)/shard_map/all_to_all | solution.py:121
  40.8 0.0 all-gather.3.cloned.1.call-start
  40.8 0.0 collective-permute-done
  40.8 0.0 collective-permute-done.1
  40.8 0.0 collective-permute-done.2
  40.9 0.0 collective-permute-done.3
  40.9 0.9 pad_maximum_fusion
  41.8 10.2 %all-to-all-done = s32[32,1,128]{2,1,0:T(1,128)S(1)} async-done(((s32[32,1,128]{2,1,0:T(1,128)}), s32[32,1,128]{2,1,0:T(1,128)S(1)}, u32[]{:S(2)}, u32[]{:S(2)}) %all-to-all-start) | async-done | bytes 16416 | tf_op jit(solution)/shard_map/all_to_all | solution.py:121
  51.9 0.0 copy-start.3
  51.9 0.0 all-gather.3.cloned.1.call-update
  51.9 0.0 copy-done
  52.0 0.6 constant_dynamic-slice_fusion.blocks_ref
  52.6 0.0 copy-done.3
  52.6 1.8 %pick.2 = bf16[1,32,8,896]{3,2,1,0:T(8,128)(2,1)} custom-call(s32[32,128]{1,0:T(8,128)} %bitcast.16, bf16[4,8,896]{2,1,0:T(8,128)(2,1)} %constant_dynamic-slice_fusion.blocks_ref), custom_call_target="tpu_custom_call" | custom-call | tf_op jit(solution)/shard_map/pick/pallas_call | solution.py:101
  54.4 8.3 %all-to-all-start.1 = ((bf16[32,8,896]{2,1,0:T(8,128)(2,1)}), bf16[32,8,896]{2,1,0:T(8,128)(2,1)S(1)}, u32[]{:S(2)}, u32[]{:S(2)}) async-start(bf16[32,8,896]{2,1,0:T(8,128)(2,1)} %bitcast.11), calls=%async_computation.1 | async-start | bytes 917504 | tf_op jit(solution)/shard_map/all_to_all | solution.py:202
  62.7 0.8 reshape.216
  63.5 0.6 add_select_fusion.indices_ref
  64.1 14.5 %all-to-all-done.1.blocks_ref = bf16[32,8,896]{2,1,0:T(8,128)(2,1)S(1)} async-done(((bf16[32,8,896]{2,1,0:T(8,128)(2,1)}), bf16[32,8,896]{2,1,0:T(8,128)(2,1)S(1)}, u32[]{:S(2)}, u32[]{:S(2)}) %all-to-all-start.1) | async-done | bytes 458784 | tf_op jit(solution)/shard_map/all_to_all | solution.py:202
  78.6 0.0 copy-start.1
  78.6 0.8 copy-done.1
  79.3 2.1 %pick.3 = bf16[16,4,8,896]{3,2,1,0:T(8,128)(2,1)} custom-call(s32[4,1]{1,0:T(4,128)} %add_select_fusion.indices_ref, bf16[32,8,896]{2,1,0:T(8,128)(2,1)} %copy-done.1), custom_call_target="tpu_custom_call" | custom-call | tf_op jit(solution)/shard_map/pick/pallas_call | solution.py:101
  81.4 34.0 %all_to_all.29.rows_ref = bf16[16,4,8,896]{3,2,1,0:T(8,128)(2,1)} all-to-all(bf16[16,4,8,896]{3,2,1,0:T(8,128)(2,1)} %pick.3), channel_id=1, replica_groups=mesh['dp'=32,'mp'=16] {'mp'}, dimensions={0} | all-to-all | bytes 1835008 | tf_op jit(solution)/shard_map/all_to_all | solution.py:138
  115.4 3.9 %attend.1 = bf16[4,128,256]{2,1,0:T(8,128)(2,1)} custom-call(bf16[16,4,8,896]{3,2,1,0:T(8,128)(2,1)} %all_to_all.29.rows_ref, bf16[128,256]{1,0:T(8,128)(2,1)} %queries_ref.1, bf16[896,256]{1,0:T(8,128)(2,1)} %key_ref.1, bf16[896,256]{1,0:T(8,128)(2,1)} %value_ref.1), custom_call_target="tpu_custom_call" | custom-call | flops 469762048 | bytes 2097152 | tf_op jit(solution)/shard_map/attend/pallas_call | solution.py:181
  119.3 3.4 %all-to-all-start.3 = ((bf16[4,128,256]{2,1,0:T(8,128)(2,1)}), bf16[4,128,256]{2,1,0:T(8,128)(2,1)S(1)}, u32[]{:S(2)}, u32[]{:S(2)}) async-start(bf16[4,128,256]{2,1,0:T(8,128)(2,1)} %attend.1), calls=%async_computation.3 | async-start | bytes 524288 | tf_op jit(solution)/shard_map/all_to_all | solution.py:47
  122.8 9.9 %all-to-all-done.3.attended_ref = bf16[4,128,256]{2,1,0:T(8,128)(2,1)S(1)} async-done(((bf16[4,128,256]{2,1,0:T(8,128)(2,1)}), bf16[4,128,256]{2,1,0:T(8,128)(2,1)S(1)}, u32[]{:S(2)}, u32[]{:S(2)}) %all-to-all-start.3) | async-done | bytes 262176 | tf_op jit(solution)/shard_map/all_to_all | solution.py:47
  132.7 0.0 copy-start.2
  132.7 0.0 all-gather.3.cloned.1.call-done
  132.7 0.7 copy-done.2
  133.4 4.5 %partial_products.1 = bf16[4,128,512]{2,1,0:T(8,128)(2,1)} custom-call(s32[1]{0:T(128)} %bitcast.far_ref, bf16[4,128,256]{2,1,0:T(8,128)(2,1)} %copy-done.2, bf16[2,4,4,256,256]{4,3,2,1,0:T(8,128)(2,1)} %bitcast.10), custom_call_target="tpu_custom_call" | custom-call | flops 536870912 | bytes 4194304 | tf_op jit(solution)/shard_map/partial_products/pallas_call | solution.py:68
  137.9 13.1 %all_to_all.30 = bf16[4,128,512]{2,1,0:T(8,128)(2,1)S(1)} all-to-all(bf16[4,128,512]{2,1,0:T(8,128)(2,1)} %partial_products.1), channel_id=1, replica_groups={{0,4,8,12},{1,5,9,13},{2,6,10,14},{3,7,11,15},{16,20,24,28},{17,21,25,2..., dimensions={0} | all-to-all | bytes 1048576 | tf_op jit(solution)/shard_map/all_to_all | solution.py:47
  150.9 0.7 reduce_sum.22
  (1 shorter events, 0.0 us)
Async XLA Ops:
  6.5 45.4 %copy-start = (bf16[512,896]{1,0:T(8,128)(2,1)S(1)}, bf16[512,896]{1,0:T(8,128)(2,1)}, u32[]{:S(2)}) copy-start(bf16[512,896]{1,0:T(8,128)(2,1)} %param.7) | copy-start | bytes 2752516
  6.5 34.3 %collective-permute-start = (bf16[256,256]{1,0:T(8,128)(2,1)}, bf16[256,256]{1,0:T(8,128)(2,1)S(1)}, u32[]{:S(2)}, u32[]{:S(2)}) collective-permute-start(bf16[256,256]{1,0:T(8,128)(2,1)} %param.10), channel_id=1, source_target_pairs={{0,0},{1,16},{2,32},{3,48},{4,4},{5,20},{6,36},{7,52},{8,8},{9,24}... | collective-permute-start | bytes 393224 | tf_op jit(solution)/shard_map/ppermute | solution.py:36
  8.2 32.6 %collective-permute-start.1 = (bf16[256,256]{1,0:T(8,128)(2,1)}, bf16[256,256]{1,0:T(8,128)(2,1)S(1)}, u32[]{:S(2)}, u32[]{:S(2)}) collective-permute-start(bf16[256,256]{1,0:T(8,128)(2,1)} %param.10), channel_id=1, source_target_pairs={{0,128},{1,144},{2,160},{3,176},{4,132},{5,148},{6,164},{7,180},{8... | collective-permute-start | bytes 393224 | tf_op jit(solution)/shard_map/ppermute | solution.py:36
  11.7 29.1 %collective-permute-start.2 = (bf16[256,256]{1,0:T(8,128)(2,1)}, bf16[256,256]{1,0:T(8,128)(2,1)S(1)}, u32[]{:S(2)}, u32[]{:S(2)}) collective-permute-start(bf16[256,256]{1,0:T(8,128)(2,1)} %param.10), channel_id=1, source_target_pairs={{0,256},{1,272},{2,288},{3,304},{4,260},{5,276},{6,292},{7,308},{8... | collective-permute-start | bytes 393224 | tf_op jit(solution)/shard_map/ppermute | solution.py:36
  17.8 23.1 %collective-permute-start.3 = (bf16[256,256]{1,0:T(8,128)(2,1)}, bf16[256,256]{1,0:T(8,128)(2,1)S(1)}, u32[]{:S(2)}, u32[]{:S(2)}) collective-permute-start(bf16[256,256]{1,0:T(8,128)(2,1)} %param.10), channel_id=1, source_target_pairs={{0,384},{1,400},{2,416},{3,432},{4,388},{5,404},{6,420},{7,436},{8... | collective-permute-start | bytes 393224 | tf_op jit(solution)/shard_map/ppermute | solution.py:36
  21.8 30.1 %all-to-all-start = ((s32[32,1,128]{2,1,0:T(1,128)}), s32[32,1,128]{2,1,0:T(1,128)S(1)}, u32[]{:S(2)}, u32[]{:S(2)}) async-start(s32[32,1,128]{2,1,0:T(1,128)} %broadcast_in_dim.21), calls=%async_computation | async-start | bytes 32768 | tf_op jit(solution)/shard_map/all_to_all | solution.py:121
  40.8 91.9 %all-gather.3.cloned.1.call-start = ((), (), s32[]{:S(2)}) async-start(), calls=%async_computation.5 | async-start | bytes 4718592 | tf_op jit(solution)/shard_map/all_gather | solution.py:43
  51.9 0.7 copy-start.3
  54.4 24.2 %all-to-all-start.1 = ((bf16[32,8,896]{2,1,0:T(8,128)(2,1)}), bf16[32,8,896]{2,1,0:T(8,128)(2,1)S(1)}, u32[]{:S(2)}, u32[]{:S(2)}) async-start(bf16[32,8,896]{2,1,0:T(8,128)(2,1)} %bitcast.11), calls=%async_computation.1 | async-start | bytes 917504 | tf_op jit(solution)/shard_map/all_to_all | solution.py:202
  78.6 0.8 copy-start.1
  119.3 13.3 %all-to-all-start.3 = ((bf16[4,128,256]{2,1,0:T(8,128)(2,1)}), bf16[4,128,256]{2,1,0:T(8,128)(2,1)S(1)}, u32[]{:S(2)}, u32[]{:S(2)}) async-start(bf16[4,128,256]{2,1,0:T(8,128)(2,1)} %attend.1), calls=%async_computation.3 | async-start | bytes 524288 | tf_op jit(solution)/shard_map/all_to_all | solution.py:47
  132.7 0.7 copy-start.2
Sparse Core Ops, SparseCore 0:
  52.1 63.6 all-gather.2

commit v12 on v11

--- a/solution.py
+++ b/solution.py
@@ -19,21 +19,28 @@
 LANES = 128
 
 
-def far_blocks(out_weight):
+def weight_block(out_weight):
     dp_count = lax.axis_size("dp")
     mp_count = lax.axis_size("mp")
-    ratio = NEAR_DP // LOCAL_MP
-    blocks = []
-    for step in range(dp_count // NEAR_DP):
-        moves = []
-        for d in range(dp_count):
-            for m in range(mp_count):
-                near = d % NEAR_DP
-                local = m % LOCAL_MP
-                to_near = near % ratio * LOCAL_MP + local
-                to_d = (d - near) ^ (step * NEAR_DP) | to_near
-                moves.append((d * mp_count + m, to_d * mp_count + m - local + near // ratio))
-        blocks.append(lax.ppermute(out_weight, ("dp", "mp"), moves))
+    moves = []
+    for d in range(dp_count):
+        for m in range(mp_count):
+            near = d % NEAR_DP
+            local = m % LOCAL_MP
+            ratio = NEAR_DP // LOCAL_MP
+            to_near = near % ratio * LOCAL_MP + local
+            to_local = near // ratio
+            target = (d - near + to_near) * mp_count + m - local + to_local
+            moves.append((d * mp_count + m, target))
+    return lax.ppermute(out_weight, ("dp", "mp"), moves)
+
+
+def far_blocks(moved):
+    dp_count = lax.axis_size("dp")
+    blocks = [moved]
+    for step in range(1, dp_count // NEAR_DP):
+        pairs = [(d, d ^ (step * NEAR_DP)) for d in range(dp_count)]
+        blocks.append(lax.ppermute(moved, "dp", pairs))
     return jnp.stack(blocks)
 
 
@@ -195,11 +202,13 @@
 
 def on_device(queries, database, key_weight, value_weight, out_weight, neighbours):
     mp_count = lax.axis_size("mp")
-    wanted, piece = lax.optimization_barrier((request(neighbours), far_blocks(out_weight)))
-    outgoing = rows_to_send(database, wanted)
+    moved = weight_block(out_weight)
+    outgoing = rows_to_send(database, request(neighbours))
+    outgoing, _ = lax.optimization_barrier((outgoing, moved))
+    arrived = lax.all_to_all(outgoing, "dp", split_axis=0, concat_axis=0, tiled=True)
+    arrived, piece = lax.optimization_barrier((arrived, far_blocks(moved)))
     columns = near_gather(piece)
     columns = columns.reshape(-1, LOCAL_MP, *columns.shape[1:])
-    arrived = lax.all_to_all(outgoing, "dp", split_axis=0, concat_axis=0, tiled=True)
     rows = near_rows(arrived, neighbours)
     copies = attend(rows, queries, key_weight, value_weight, LOCAL_MP)
     local_groups = [list(range(m, m + LOCAL_MP)) for m in range(0, mp_count, LOCAL_MP)]

time: 159 us -> 152 us (0.956)
  the two profiles are of different devices: /device:TPU:16 before, /device:TPU:8 now
where the time goes in v12:
time: 152 us; the launch traced here: 151 us
  blocking collectives  49.9 us (33%)
  starting transfers between devices  36.8 us (24%)
  waiting for transfers between devices  32.5 us (21%)
  between operations  13.5 us (9%)
  Pallas kernels  12.2 us (8%)
  local copies, waits for them, and re-layouts  3.5 us (2%)
  other arithmetic  2.32 us (2%)
    all_to_all x1, blocking collectives, near_rows(): return lax.all_to_all(copies, 'mp', split_axis=0, concat_axis=0, tiled=True)  36.2 us
    all_to_all x1, starting transfers between devices, request(): return lax.all_to_all(asked, 'dp', split_axis=0, concat_axis=0, tiled=True)  17.4 us
    all_to_all x1, blocking collectives, exchange(): lax.all_to_all(blocks, 'mp', split_axis=0, concat_axis=0, axis_index_grou...  13.7 us
    ppermute x3, waiting for transfers between devices, far_blocks(): blocks.append(lax.ppermute(moved, 'dp', pairs))  12.7 us
    all_to_all x1, waiting for transfers between devices, exchange(): lax.all_to_all(blocks, 'mp', split_axis=0, concat_axis=0, axis_index_grou...  9.89 us
    ppermute x3, starting transfers between devices, far_blocks(): blocks.append(lax.ppermute(moved, 'dp', pairs))  9.21 us
    all_to_all x1, waiting for transfers between devices, request(): return lax.all_to_all(asked, 'dp', split_axis=0, concat_axis=0, tiled=True)  8.25 us
    all_to_all x1, starting transfers between devices, on_device(): lax.all_to_all(outgoing, 'dp', split_axis=0, concat_axis=0, tiled=True)  5.04 us
  transfers between devices with their start and end apart: 8, of which 6 were waited for; matrix products, arithmetic and copies ran while one was open for 3% of the time, Pallas kernels for 5%

profile of v12, /device:TPU:8, one launch (start us, length us, event | category | flops | bytes accessed | tf_op | source)
XLA Modules:
  0.0 150.7 jit_solution(11146124297740622505)
XLA Ops:
  6.5 0.0 copy-start
  6.5 1.7 %collective-permute-start = (bf16[256,256]{1,0:T(8,128)(2,1)}, bf16[256,256]{1,0:T(8,128)(2,1)S(1)}, u32[]{:S(2)}, u32[]{:S(2)}) collective-permute-start(bf16[256,256]{1,0:T(8,128)(2,1)} %param.10), channel_id=1, source_target_pairs={{0,0},{1,16},{2,32},{3,48},{4,4},{5,20},{6,36},{7,52},{8,8},{9,24}... | collective-permute-start | bytes 393224 | tf_op jit(solution)/shard_map/ppermute | solution.py:35
  8.2 0.8 reshape.211
  9.0 0.1 select_reduce_fusion
  9.1 0.7 broadcast_in_dim.21
  9.8 17.4 %all-to-all-start = ((s32[32,1,128]{2,1,0:T(1,128)}), s32[32,1,128]{2,1,0:T(1,128)S(1)}, u32[]{:S(2)}, u32[]{:S(2)}) async-start(s32[32,1,128]{2,1,0:T(1,128)} %broadcast_in_dim.21), calls=%async_computation | async-start | bytes 32768 | tf_op jit(solution)/shard_map/all_to_all | solution.py:128
  27.2 0.0 copy-done
  27.2 0.6 constant_dynamic-slice_fusion.blocks_ref
  27.9 8.2 %all-to-all-done = s32[32,1,128]{2,1,0:T(1,128)S(1)} async-done(((s32[32,1,128]{2,1,0:T(1,128)}), s32[32,1,128]{2,1,0:T(1,128)S(1)}, u32[]{:S(2)}, u32[]{:S(2)}) %all-to-all-start) | async-done | bytes 16416 | tf_op jit(solution)/shard_map/all_to_all | solution.py:128
  36.1 0.0 copy-start.3
  36.1 0.6 copy-done.3
  36.7 1.8 %pick.2 = bf16[1,32,8,896]{3,2,1,0:T(8,128)(2,1)} custom-call(s32[32,128]{1,0:T(8,128)} %bitcast.16, bf16[4,8,896]{2,1,0:T(8,128)(2,1)} %constant_dynamic-slice_fusion.blocks_ref), custom_call_target="tpu_custom_call" | custom-call | tf_op jit(solution)/shard_map/pick/pallas_call | solution.py:108
  38.5 0.0 collective-permute-done
  38.5 5.0 %all-to-all-start.1 = ((bf16[32,8,896]{2,1,0:T(8,128)(2,1)}), bf16[32,8,896]{2,1,0:T(8,128)(2,1)S(1)}, u32[]{:S(2)}, u32[]{:S(2)}) async-start(bf16[32,8,896]{2,1,0:T(8,128)(2,1)} %bitcast.11), calls=%async_computation.1 | async-start | bytes 917504 | tf_op jit(solution)/shard_map/all_to_all | solution.py:208
  43.5 0.0 all-gather.3.cloned.1.call-start
  43.5 2.2 %collective-permute-start.1 = (bf16[256,256]{1,0:T(8,128)(2,1)S(1)}, bf16[256,256]{1,0:T(8,128)(2,1)S(1)}, u32[]{:S(2)}, u32[]{:S(2)}) collective-permute-start(bf16[256,256]{1,0:T(8,128)(2,1)S(1)} %collective-permute-done), channel_id=1, source_target_pairs={{0,128},{16,144},{32,160},{48,176},{64,192},{80,208},{96,224},{112... | collective-permute-start | bytes 393224 | tf_op jit(solution)/shard_map/ppermute | solution.py:43
  45.8 4.6 %collective-permute-start.2 = (bf16[256,256]{1,0:T(8,128)(2,1)S(1)}, bf16[256,256]{1,0:T(8,128)(2,1)S(1)}, u32[]{:S(2)}, u32[]{:S(2)}) collective-permute-start(bf16[256,256]{1,0:T(8,128)(2,1)S(1)} %collective-permute-done), channel_id=1, source_target_pairs={{0,256},{16,272},{32,288},{48,304},{64,320},{80,336},{96,352},{112... | collective-permute-start | bytes 393224 | tf_op jit(solution)/shard_map/ppermute | solution.py:43
  50.4 2.4 %collective-permute-start.3 = (bf16[256,256]{1,0:T(8,128)(2,1)S(1)}, bf16[256,256]{1,0:T(8,128)(2,1)S(1)}, u32[]{:S(2)}, u32[]{:S(2)}) collective-permute-start(bf16[256,256]{1,0:T(8,128)(2,1)S(1)} %collective-permute-done), channel_id=1, source_target_pairs={{0,384},{16,400},{32,416},{48,432},{64,448},{80,464},{96,480},{112... | collective-permute-start | bytes 393224 | tf_op jit(solution)/shard_map/ppermute | solution.py:43
  52.8 2.8 %collective-permute-done.1 = bf16[256,256]{1,0:T(8,128)(2,1)S(1)} collective-permute-done((bf16[256,256]{1,0:T(8,128)(2,1)S(1)}, bf16[256,256]{1,0:T(8,128)(2,1)S(1)}, u32[]{:S(2)}, u32[]{:S(2)}) %collective-permute-start.1) | collective-permute-done | bytes 131104 | tf_op jit(solution)/shard_map/ppermute | solution.py:43
  55.5 5.8 %collective-permute-done.2 = bf16[256,256]{1,0:T(8,128)(2,1)S(1)} collective-permute-done((bf16[256,256]{1,0:T(8,128)(2,1)S(1)}, bf16[256,256]{1,0:T(8,128)(2,1)S(1)}, u32[]{:S(2)}, u32[]{:S(2)}) %collective-permute-start.2) | collective-permute-done | bytes 131104 | tf_op jit(solution)/shard_map/ppermute | solution.py:43
  61.4 4.1 %collective-permute-done.3 = bf16[256,256]{1,0:T(8,128)(2,1)S(1)} collective-permute-done((bf16[256,256]{1,0:T(8,128)(2,1)S(1)}, bf16[256,256]{1,0:T(8,128)(2,1)S(1)}, u32[]{:S(2)}, u32[]{:S(2)}) %collective-permute-start.3) | collective-permute-done | bytes 131104 | tf_op jit(solution)/shard_map/ppermute | solution.py:43
  65.4 0.9 pad_maximum_fusion
  66.3 0.0 all-to-all-done.1.blocks_ref
  66.3 0.0 copy-start.1
  66.3 0.0 all-gather.3.cloned.1.call-update
  66.4 0.8 reshape.216
  67.2 0.6 add_select_fusion.indices_ref
  67.8 0.0 copy-done.1
  67.8 2.0 %pick.3 = bf16[16,4,8,896]{3,2,1,0:T(8,128)(2,1)} custom-call(s32[4,1]{1,0:T(4,128)} %add_select_fusion.indices_ref, bf16[32,8,896]{2,1,0:T(8,128)(2,1)} %copy-done.1), custom_call_target="tpu_custom_call" | custom-call | tf_op jit(solution)/shard_map/pick/pallas_call | solution.py:108
  69.8 36.2 %all_to_all.28.rows_ref = bf16[16,4,8,896]{3,2,1,0:T(8,128)(2,1)} all-to-all(bf16[16,4,8,896]{3,2,1,0:T(8,128)(2,1)} %pick.3), channel_id=1, replica_groups=mesh['dp'=32,'mp'=16] {'mp'}, dimensions={0} | all-to-all | bytes 1835008 | tf_op jit(solution)/shard_map/all_to_all | solution.py:145
  106.0 4.0 %attend.1 = bf16[4,128,256]{2,1,0:T(8,128)(2,1)} custom-call(bf16[16,4,8,896]{3,2,1,0:T(8,128)(2,1)} %all_to_all.28.rows_ref, bf16[128,256]{1,0:T(8,128)(2,1)} %queries_ref.1, bf16[896,256]{1,0:T(8,128)(2,1)} %key_ref.1, bf16[896,256]{1,0:T(8,128)(2,1)} %value_ref.1), custom_call_target="tpu_custom_call" | custom-call | flops 469762048 | bytes 2097152 | tf_op jit(solution)/shard_map/attend/pallas_call | solution.py:188
  109.9 3.4 %all-to-all-start.3 = ((bf16[4,128,256]{2,1,0:T(8,128)(2,1)}), bf16[4,128,256]{2,1,0:T(8,128)(2,1)S(1)}, u32[]{:S(2)}, u32[]{:S(2)}) async-start(bf16[4,128,256]{2,1,0:T(8,128)(2,1)} %attend.1), calls=%async_computation.3 | async-start | bytes 524288 | tf_op jit(solution)/shard_map/all_to_all | solution.py:54
  113.4 9.9 %all-to-all-done.3.attended_ref = bf16[4,128,256]{2,1,0:T(8,128)(2,1)S(1)} async-done(((bf16[4,128,256]{2,1,0:T(8,128)(2,1)}), bf16[4,128,256]{2,1,0:T(8,128)(2,1)S(1)}, u32[]{:S(2)}, u32[]{:S(2)}) %all-to-all-start.3) | async-done | bytes 262176 | tf_op jit(solution)/shard_map/all_to_all | solution.py:54
  123.3 0.0 copy-start.2
  123.3 1.7 %all-gather.3.cloned.1.call-done = bf16[32,256,256]{2,1,0:T(8,128)(2,1)} async-done(((bf16[4,256,256]{2,1,0:T(8,128)(2,1)}), bf16[32,256,256]{2,1,0:T(8,128)(2,1)}) %all-gather.3.cloned.1.call-update) | async-done | bytes 4194320 | tf_op jit(solution)/shard_map/all_gather | solution.py:50
  125.0 0.0 copy-done.2
  125.0 4.5 %partial_products.1 = bf16[4,128,512]{2,1,0:T(8,128)(2,1)} custom-call(s32[1]{0:T(128)} %bitcast.far_ref, bf16[4,128,256]{2,1,0:T(8,128)(2,1)} %copy-done.2, bf16[2,4,4,256,256]{4,3,2,1,0:T(8,128)(2,1)} %bitcast.10), custom_call_target="tpu_custom_call" | custom-call | flops 536870912 | bytes 4194304 | tf_op jit(solution)/shard_map/partial_products/pallas_call | solution.py:75
  129.4 13.7 %all_to_all.29 = bf16[4,128,512]{2,1,0:T(8,128)(2,1)S(1)} all-to-all(bf16[4,128,512]{2,1,0:T(8,128)(2,1)} %partial_products.1), channel_id=1, replica_groups={{0,4,8,12},{1,5,9,13},{2,6,10,14},{3,7,11,15},{16,20,24,28},{17,21,25,2..., dimensions={0} | all-to-all | bytes 1048576 | tf_op jit(solution)/shard_map/all_to_all | solution.py:54
  143.2 0.7 reduce_sum.22
  (1 shorter events, 0.0 us)
Async XLA Ops:
  6.5 20.7 %copy-start = (bf16[512,896]{1,0:T(8,128)(2,1)S(1)}, bf16[512,896]{1,0:T(8,128)(2,1)}, u32[]{:S(2)}) copy-start(bf16[512,896]{1,0:T(8,128)(2,1)} %param.7) | copy-start | bytes 2752516
  6.5 31.9 %collective-permute-start = (bf16[256,256]{1,0:T(8,128)(2,1)}, bf16[256,256]{1,0:T(8,128)(2,1)S(1)}, u32[]{:S(2)}, u32[]{:S(2)}) collective-permute-start(bf16[256,256]{1,0:T(8,128)(2,1)} %param.10), channel_id=1, source_target_pairs={{0,0},{1,16},{2,32},{3,48},{4,4},{5,20},{6,36},{7,52},{8,8},{9,24}... | collective-permute-start | bytes 393224 | tf_op jit(solution)/shard_map/ppermute | solution.py:35
  9.8 26.3 %all-to-all-start = ((s32[32,1,128]{2,1,0:T(1,128)}), s32[32,1,128]{2,1,0:T(1,128)S(1)}, u32[]{:S(2)}, u32[]{:S(2)}) async-start(s32[32,1,128]{2,1,0:T(1,128)} %broadcast_in_dim.21), calls=%async_computation | async-start | bytes 32768 | tf_op jit(solution)/shard_map/all_to_all | solution.py:128
  36.1 0.6 copy-start.3
  38.5 27.9 %all-to-all-start.1 = ((bf16[32,8,896]{2,1,0:T(8,128)(2,1)}), bf16[32,8,896]{2,1,0:T(8,128)(2,1)S(1)}, u32[]{:S(2)}, u32[]{:S(2)}) async-start(bf16[32,8,896]{2,1,0:T(8,128)(2,1)} %bitcast.11), calls=%async_computation.1 | async-start | bytes 917504 | tf_op jit(solution)/shard_map/all_to_all | solution.py:208
  43.5 81.5 %all-gather.3.cloned.1.call-start = ((), (), s32[]{:S(2)}) async-start(), calls=%async_computation.5 | async-start | bytes 4718592 | tf_op jit(solution)/shard_map/all_gather | solution.py:50
  43.5 12.0 %collective-permute-start.1 = (bf16[256,256]{1,0:T(8,128)(2,1)S(1)}, bf16[256,256]{1,0:T(8,128)(2,1)S(1)}, u32[]{:S(2)}, u32[]{:S(2)}) collective-permute-start(bf16[256,256]{1,0:T(8,128)(2,1)S(1)} %collective-permute-done), channel_id=1, source_target_pairs={{0,128},{16,144},{32,160},{48,176},{64,192},{80,208},{96,224},{112... | collective-permute-start | bytes 393224 | tf_op jit(solution)/shard_map/ppermute | solution.py:43
  45.8 15.6 %collective-permute-start.2 = (bf16[256,256]{1,0:T(8,128)(2,1)S(1)}, bf16[256,256]{1,0:T(8,128)(2,1)S(1)}, u32[]{:S(2)}, u32[]{:S(2)}) collective-permute-start(bf16[256,256]{1,0:T(8,128)(2,1)S(1)} %collective-permute-done), channel_id=1, source_target_pairs={{0,256},{16,272},{32,288},{48,304},{64,320},{80,336},{96,352},{112... | collective-permute-start | bytes 393224 | tf_op jit(solution)/shard_map/ppermute | solution.py:43
  50.4 15.1 %collective-permute-start.3 = (bf16[256,256]{1,0:T(8,128)(2,1)S(1)}, bf16[256,256]{1,0:T(8,128)(2,1)S(1)}, u32[]{:S(2)}, u32[]{:S(2)}) collective-permute-start(bf16[256,256]{1,0:T(8,128)(2,1)S(1)} %collective-permute-done), channel_id=1, source_target_pairs={{0,384},{16,400},{32,416},{48,432},{64,448},{80,464},{96,480},{112... | collective-permute-start | bytes 393224 | tf_op jit(solution)/shard_map/ppermute | solution.py:43
  66.3 1.4 copy-start.1
  109.9 13.3 %all-to-all-start.3 = ((bf16[4,128,256]{2,1,0:T(8,128)(2,1)}), bf16[4,128,256]{2,1,0:T(8,128)(2,1)S(1)}, u32[]{:S(2)}, u32[]{:S(2)}) async-start(bf16[4,128,256]{2,1,0:T(8,128)(2,1)} %attend.1), calls=%async_computation.3 | async-start | bytes 524288 | tf_op jit(solution)/shard_map/all_to_all | solution.py:54
  123.3 1.7 %copy-start.2 = (bf16[4,128,256]{2,1,0:T(8,128)(2,1)}, bf16[4,128,256]{2,1,0:T(8,128)(2,1)S(1)}, u32[]{:S(2)}) copy-start(bf16[4,128,256]{2,1,0:T(8,128)(2,1)S(1)} %all-to-all-done.3.attended_ref) | copy-start | bytes 786436
Sparse Core Ops, SparseCore 0:
  66.5 58.4 all-gather.2

commit v13 on v12

--- a/solution.py
+++ b/solution.py
@@ -136,7 +136,11 @@
         (0, lax.axis_index("mp") * part_rows, 0),
         (BLK_DEV, part_rows, enc_width),
     )
-    return pick(wanted, stored, 1)[0]
+    wanted = wanted[:, :1].reshape(-1, 1, 1)
+    outgoing = stored[0][None]
+    for block in range(1, BLK_DEV):
+        outgoing = jnp.where(wanted == block, stored[block][None], outgoing)
+    return jnp.broadcast_to(outgoing, (wanted.shape[0], part_rows, enc_width))
 
 
 def near_rows(arrived, neighbours):

time: 152 us -> 154 us (1.013)
  starting transfers between devices: 36.8 us -> 44.7 us
  blocking collectives: 49.9 us -> 45 us
  Pallas kernels: 12.2 us -> 10.5 us
    all_to_all x1, starting transfers between devices: 5.04 us -> 16.2 us  [on_device(): lax.all_to_all(outgoing, 'dp', split_axis=0, concat_axis=0, tiled=True)]
    all_to_all x1, blocking collectives: 36.2 us -> 31.3 us  [near_rows(): return lax.all_to_all(copies, 'mp', split_axis=0, concat_axis=0, tiled=True)]
    all_gather x1, waiting for transfers between devices: 1.69 us -> 5.96 us  [near_gather(): return lax.all_gather(piece, 'dp', axis=0, axis_index_groups=groups)]
    all_to_all x1, starting transfers between devices: 17.4 us -> 14 us  [request(): return lax.all_to_all(asked, 'dp', split_axis=0, concat_axis=0, tiled=True)]
    pallas_call x2 -> x1, Pallas kernels: 3.8 us -> 2.02 us  [pick(): pl.pallas_call(body, out_shape=jax.ShapeDtypeStruct((copies, indices.shap...]
    all_to_all x1, waiting for transfers between devices: 8.25 us -> 6.49 us  [request(): return lax.all_to_all(asked, 'dp', split_axis=0, concat_axis=0, tiled=True)]
    ppermute x3, waiting for transfers between devices: 12.7 us -> 11 us  [far_blocks(): blocks.append(lax.ppermute(moved, 'dp', pairs))]
  transfers between devices with their start and end apart: 8 -> 8, of which waited for: 6 -> 4; matrix products, arithmetic and copies ran while one was open for 3% -> 3% of each run, Pallas kernels for 5% -> 4%
where the time goes in v13:
time: 154 us
  blocking collectives  45 us (29%)
  starting transfers between devices  44.7 us (29%)
  waiting for transfers between devices  33.4 us (22%)
  between operations  13.5 us (9%)
  Pallas kernels  10.5 us (7%)
  other arithmetic  3.45 us (2%)
  local copies, waits for them, and re-layouts  3.04 us (2%)
    all_to_all x1, blocking collectives, near_rows(): return lax.all_to_all(copies, 'mp', split_axis=0, concat_axis=0, tiled=True)  31.3 us
    all_to_all x1, starting transfers between devices, on_device(): lax.all_to_all(outgoing, 'dp', split_axis=0, concat_axis=0, tiled=True)  16.2 us
    all_to_all x1, starting transfers between devices, request(): return lax.all_to_all(asked, 'dp', split_axis=0, concat_axis=0, tiled=True)  14 us
    all_to_all x1, blocking collectives, exchange(): lax.all_to_all(blocks, 'mp', split_axis=0, concat_axis=0, axis_index_grou...  13.7 us
    ppermute x3, waiting for transfers between devices, far_blocks(): blocks.append(lax.ppermute(moved, 'dp', pairs))  11 us
    all_to_all x1, waiting for transfers between devices, exchange(): lax.all_to_all(blocks, 'mp', split_axis=0, concat_axis=0, axis_index_grou...  9.99 us
    ppermute x3, starting transfers between devices, far_blocks(): blocks.append(lax.ppermute(moved, 'dp', pairs))  9.6 us
    all_to_all x1, waiting for transfers between devices, request(): return lax.all_to_all(asked, 'dp', split_axis=0, concat_axis=0, tiled=True)  6.49 us
  transfers between devices with their start and end apart: 8, of which 4 were waited for; matrix products, arithmetic and copies ran while one was open for 3% of the time, Pallas kernels for 4%

profile of v13, /device:TPU:8, one launch (start us, length us, event | category | flops | bytes accessed | tf_op | source)
XLA Modules:
  0.0 153.6 jit_solution(10203284704762877803)
XLA Ops:
  6.5 0.8 reshape.239
  7.3 0.1 select_reduce_fusion
  7.4 0.7 broadcast_in_dim.79
  8.1 14.0 %all-to-all-start = ((s32[32,1,128]{2,1,0:T(1,128)}), s32[32,1,128]{2,1,0:T(1,128)S(1)}, u32[]{:S(2)}, u32[]{:S(2)}) async-start(s32[32,1,128]{2,1,0:T(1,128)} %broadcast_in_dim.79), calls=%async_computation | async-start | bytes 32768 | tf_op jit(solution)/shard_map/all_to_all | solution.py:128
  22.1 1.6 %collective-permute-start = (bf16[256,256]{1,0:T(8,128)(2,1)}, bf16[256,256]{1,0:T(8,128)(2,1)S(1)}, u32[]{:S(2)}, u32[]{:S(2)}) collective-permute-start(bf16[256,256]{1,0:T(8,128)(2,1)} %param.10), channel_id=1, source_target_pairs={{0,0},{1,16},{2,32},{3,48},{4,4},{5,20},{6,36},{7,52},{8,8},{9,24}... | collective-permute-start | bytes 393224 | tf_op jit(solution)/shard_map/ppermute | solution.py:35
  23.6 0.8 dynamic-slice_bitcast_fusion.3
  24.4 6.5 %all-to-all-done = s32[32,1,128]{2,1,0:T(1,128)S(1)} async-done(((s32[32,1,128]{2,1,0:T(1,128)}), s32[32,1,128]{2,1,0:T(1,128)S(1)}, u32[]{:S(2)}, u32[]{:S(2)}) %all-to-all-start) | async-done | bytes 16416 | tf_op jit(solution)/shard_map/all_to_all | solution.py:128
  30.9 0.1 compare_reduce_fusion.2
  31.0 1.0 select_select_fusion
  32.0 0.0 collective-permute-done
  32.0 16.2 %all-to-all-start.1 = ((bf16[32,8,896]{2,1,0:T(8,128)(2,1)}), bf16[32,8,896]{2,1,0:T(8,128)(2,1)S(1)}, u32[]{:S(2)}, u32[]{:S(2)}) async-start(bf16[32,8,896]{2,1,0:T(8,128)(2,1)} %select_select_fusion), calls=%async_computation.1 | async-start | bytes 917504 | tf_op jit(solution)/shard_map/all_to_all | solution.py:212
  48.2 0.0 all-gather.3.cloned.1.call-start
  48.3 3.4 %collective-permute-start.3 = (bf16[256,256]{1,0:T(8,128)(2,1)S(1)}, bf16[256,256]{1,0:T(8,128)(2,1)S(1)}, u32[]{:S(2)}, u32[]{:S(2)}) collective-permute-start(bf16[256,256]{1,0:T(8,128)(2,1)S(1)} %collective-permute-done), channel_id=1, source_target_pairs={{0,384},{16,400},{32,416},{48,432},{64,448},{80,464},{96,480},{112... | collective-permute-start | bytes 393224 | tf_op jit(solution)/shard_map/ppermute | solution.py:43
  51.6 4.3 %collective-permute-start.1 = (bf16[256,256]{1,0:T(8,128)(2,1)S(1)}, bf16[256,256]{1,0:T(8,128)(2,1)S(1)}, u32[]{:S(2)}, u32[]{:S(2)}) collective-permute-start(bf16[256,256]{1,0:T(8,128)(2,1)S(1)} %collective-permute-done), channel_id=1, source_target_pairs={{0,128},{16,144},{32,160},{48,176},{64,192},{80,208},{96,224},{112... | collective-permute-start | bytes 393224 | tf_op jit(solution)/shard_map/ppermute | solution.py:43
  56.0 1.9 %collective-permute-start.2 = (bf16[256,256]{1,0:T(8,128)(2,1)S(1)}, bf16[256,256]{1,0:T(8,128)(2,1)S(1)}, u32[]{:S(2)}, u32[]{:S(2)}) collective-permute-start(bf16[256,256]{1,0:T(8,128)(2,1)S(1)} %collective-permute-done), channel_id=1, source_target_pairs={{0,256},{16,272},{32,288},{48,304},{64,320},{80,336},{96,352},{112... | collective-permute-start | bytes 393224 | tf_op jit(solution)/shard_map/ppermute | solution.py:43
  57.9 11.0 %collective-permute-done.3 = bf16[256,256]{1,0:T(8,128)(2,1)S(1)} collective-permute-done((bf16[256,256]{1,0:T(8,128)(2,1)S(1)}, bf16[256,256]{1,0:T(8,128)(2,1)S(1)}, u32[]{:S(2)}, u32[]{:S(2)}) %collective-permute-start.3) | collective-permute-done | bytes 131104 | tf_op jit(solution)/shard_map/ppermute | solution.py:43
  68.8 0.0 collective-permute-done.1
  68.8 0.0 collective-permute-done.2
  68.8 0.9 pad_maximum_fusion
  69.7 0.0 all-to-all-done.1.blocks_ref
  69.7 0.0 copy-start
  69.7 0.0 all-gather.3.cloned.1.call-update
  69.8 0.8 reshape.244
  70.6 0.6 add_select_fusion.indices_ref
  71.1 0.0 copy-done
  71.1 2.0 %pick.1 = bf16[16,4,8,896]{3,2,1,0:T(8,128)(2,1)} custom-call(s32[4,1]{1,0:T(4,128)} %add_select_fusion.indices_ref, bf16[32,8,896]{2,1,0:T(8,128)(2,1)} %copy-done), custom_call_target="tpu_custom_call" | custom-call | tf_op jit(solution)/shard_map/pick/pallas_call | solution.py:108
  73.2 31.3 %all_to_all.29.rows_ref = bf16[16,4,8,896]{3,2,1,0:T(8,128)(2,1)} all-to-all(bf16[16,4,8,896]{3,2,1,0:T(8,128)(2,1)} %pick.1), channel_id=1, replica_groups=mesh['dp'=32,'mp'=16] {'mp'}, dimensions={0} | all-to-all | bytes 1835008 | tf_op jit(solution)/shard_map/all_to_all | solution.py:149
  104.5 4.0 %attend.1 = bf16[4,128,256]{2,1,0:T(8,128)(2,1)} custom-call(bf16[16,4,8,896]{3,2,1,0:T(8,128)(2,1)} %all_to_all.29.rows_ref, bf16[128,256]{1,0:T(8,128)(2,1)} %queries_ref.1, bf16[896,256]{1,0:T(8,128)(2,1)} %key_ref.1, bf16[896,256]{1,0:T(8,128)(2,1)} %value_ref.1), custom_call_target="tpu_custom_call" | custom-call | flops 469762048 | bytes 2097152 | tf_op jit(solution)/shard_map/attend/pallas_call | solution.py:192
  108.4 3.4 %all-to-all-start.3 = ((bf16[4,128,256]{2,1,0:T(8,128)(2,1)}), bf16[4,128,256]{2,1,0:T(8,128)(2,1)S(1)}, u32[]{:S(2)}, u32[]{:S(2)}) async-start(bf16[4,128,256]{2,1,0:T(8,128)(2,1)} %attend.1), calls=%async_computation.3 | async-start | bytes 524288 | tf_op jit(solution)/shard_map/all_to_all | solution.py:54
  111.9 10.0 %all-to-all-done.3.attended_ref = bf16[4,128,256]{2,1,0:T(8,128)(2,1)S(1)} async-done(((bf16[4,128,256]{2,1,0:T(8,128)(2,1)}), bf16[4,128,256]{2,1,0:T(8,128)(2,1)S(1)}, u32[]{:S(2)}, u32[]{:S(2)}) %all-to-all-start.3) | async-done | bytes 262176 | tf_op jit(solution)/shard_map/all_to_all | solution.py:54
  121.9 0.0 copy-start.1
  121.9 6.0 %all-gather.3.cloned.1.call-done = bf16[32,256,256]{2,1,0:T(8,128)(2,1)} async-done(((bf16[4,256,256]{2,1,0:T(8,128)(2,1)}), bf16[32,256,256]{2,1,0:T(8,128)(2,1)}) %all-gather.3.cloned.1.call-update) | async-done | bytes 4194320 | tf_op jit(solution)/shard_map/all_gather | solution.py:50
  127.8 0.0 copy-done.1
  127.8 4.5 %partial_products.1 = bf16[4,128,512]{2,1,0:T(8,128)(2,1)} custom-call(s32[1]{0:T(128)} %bitcast.far_ref, bf16[4,128,256]{2,1,0:T(8,128)(2,1)} %copy-done.1, bf16[2,4,4,256,256]{4,3,2,1,0:T(8,128)(2,1)} %bitcast.16), custom_call_target="tpu_custom_call" | custom-call | flops 536870912 | bytes 4194304 | tf_op jit(solution)/shard_map/partial_products/pallas_call | solution.py:75
  132.3 13.7 %all_to_all.30 = bf16[4,128,512]{2,1,0:T(8,128)(2,1)S(1)} all-to-all(bf16[4,128,512]{2,1,0:T(8,128)(2,1)} %partial_products.1), channel_id=1, replica_groups={{0,4,8,12},{1,5,9,13},{2,6,10,14},{3,7,11,15},{16,20,24,28},{17,21,25,2..., dimensions={0} | all-to-all | bytes 1048576 | tf_op jit(solution)/shard_map/all_to_all | solution.py:54
  146.0 0.7 reduce_sum.22
  (1 shorter events, 0.0 us)
Async XLA Ops:
  8.1 22.8 %all-to-all-start = ((s32[32,1,128]{2,1,0:T(1,128)}), s32[32,1,128]{2,1,0:T(1,128)S(1)}, u32[]{:S(2)}, u32[]{:S(2)}) async-start(s32[32,1,128]{2,1,0:T(1,128)} %broadcast_in_dim.79), calls=%async_computation | async-start | bytes 32768 | tf_op jit(solution)/shard_map/all_to_all | solution.py:128
  22.1 10.0 %collective-permute-start = (bf16[256,256]{1,0:T(8,128)(2,1)}, bf16[256,256]{1,0:T(8,128)(2,1)S(1)}, u32[]{:S(2)}, u32[]{:S(2)}) collective-permute-start(bf16[256,256]{1,0:T(8,128)(2,1)} %param.10), channel_id=1, source_target_pairs={{0,0},{1,16},{2,32},{3,48},{4,4},{5,20},{6,36},{7,52},{8,8},{9,24}... | collective-permute-start | bytes 393224 | tf_op jit(solution)/shard_map/ppermute | solution.py:35
  32.0 37.7 %all-to-all-start.1 = ((bf16[32,8,896]{2,1,0:T(8,128)(2,1)}), bf16[32,8,896]{2,1,0:T(8,128)(2,1)S(1)}, u32[]{:S(2)}, u32[]{:S(2)}) async-start(bf16[32,8,896]{2,1,0:T(8,128)(2,1)} %select_select_fusion), calls=%async_computation.1 | async-start | bytes 917504 | tf_op jit(solution)/shard_map/all_to_all | solution.py:212
  48.2 79.6 %all-gather.3.cloned.1.call-start = ((), (), s32[]{:S(2)}) async-start(), calls=%async_computation.5 | async-start | bytes 4718592 | tf_op jit(solution)/shard_map/all_gather | solution.py:50
  48.3 20.6 %collective-permute-start.3 = (bf16[256,256]{1,0:T(8,128)(2,1)S(1)}, bf16[256,256]{1,0:T(8,128)(2,1)S(1)}, u32[]{:S(2)}, u32[]{:S(2)}) collective-permute-start(bf16[256,256]{1,0:T(8,128)(2,1)S(1)} %collective-permute-done), channel_id=1, source_target_pairs={{0,384},{16,400},{32,416},{48,432},{64,448},{80,464},{96,480},{112... | collective-permute-start | bytes 393224 | tf_op jit(solution)/shard_map/ppermute | solution.py:43
  51.6 17.2 %collective-permute-start.1 = (bf16[256,256]{1,0:T(8,128)(2,1)S(1)}, bf16[256,256]{1,0:T(8,128)(2,1)S(1)}, u32[]{:S(2)}, u32[]{:S(2)}) collective-permute-start(bf16[256,256]{1,0:T(8,128)(2,1)S(1)} %collective-permute-done), channel_id=1, source_target_pairs={{0,128},{16,144},{32,160},{48,176},{64,192},{80,208},{96,224},{112... | collective-permute-start | bytes 393224 | tf_op jit(solution)/shard_map/ppermute | solution.py:43
  56.0 12.9 %collective-permute-start.2 = (bf16[256,256]{1,0:T(8,128)(2,1)S(1)}, bf16[256,256]{1,0:T(8,128)(2,1)S(1)}, u32[]{:S(2)}, u32[]{:S(2)}) collective-permute-start(bf16[256,256]{1,0:T(8,128)(2,1)S(1)} %collective-permute-done), channel_id=1, source_target_pairs={{0,256},{16,272},{32,288},{48,304},{64,320},{80,336},{96,352},{112... | collective-permute-start | bytes 393224 | tf_op jit(solution)/shard_map/ppermute | solution.py:43
  69.7 1.4 copy-start
  108.4 13.4 %all-to-all-start.3 = ((bf16[4,128,256]{2,1,0:T(8,128)(2,1)}), bf16[4,128,256]{2,1,0:T(8,128)(2,1)S(1)}, u32[]{:S(2)}, u32[]{:S(2)}) async-start(bf16[4,128,256]{2,1,0:T(8,128)(2,1)} %attend.1), calls=%async_computation.3 | async-start | bytes 524288 | tf_op jit(solution)/shard_map/all_to_all | solution.py:54
  121.9 6.0 %copy-start.1 = (bf16[4,128,256]{2,1,0:T(8,128)(2,1)}, bf16[4,128,256]{2,1,0:T(8,128)(2,1)S(1)}, u32[]{:S(2)}) copy-start(bf16[4,128,256]{2,1,0:T(8,128)(2,1)S(1)} %all-to-all-done.3.attended_ref) | copy-start | bytes 786436
Sparse Core Ops, SparseCore 0:
  69.9 57.8 all-gather.2

commit v14 on v13

--- a/solution.py
+++ b/solution.py
@@ -208,7 +208,6 @@
     mp_count = lax.axis_size("mp")
     moved = weight_block(out_weight)
     outgoing = rows_to_send(database, request(neighbours))
-    outgoing, _ = lax.optimization_barrier((outgoing, moved))
     arrived = lax.all_to_all(outgoing, "dp", split_axis=0, concat_axis=0, tiled=True)
     arrived, piece = lax.optimization_barrier((arrived, far_blocks(moved)))
     columns = near_gather(piece)

time: 154 us -> 156 us (1.013)
  blocking collectives: 45 us -> 61.6 us
  starting transfers between devices: 44.7 us -> 33.7 us
  waiting for transfers between devices: 33.4 us -> 28.4 us
    all_to_all x1, blocking collectives: 31.3 us -> 48.9 us  [near_rows(): return lax.all_to_all(copies, 'mp', split_axis=0, concat_axis=0, tiled=True)]
    all_to_all x1, starting transfers between devices: 16.2 us -> 5.04 us  [on_device(): lax.all_to_all(outgoing, 'dp', split_axis=0, concat_axis=0, tiled=True)]
    all_gather x1, waiting for transfers between devices: 5.96 us -> 0.01 us  [near_gather(): return lax.all_gather(piece, 'dp', axis=0, axis_index_groups=groups)]
    ppermute x3, waiting for transfers between devices: 11 us -> 7.54 us  [far_blocks(): blocks.append(lax.ppermute(moved, 'dp', pairs))]
    all_to_all x1, waiting for transfers between devices: 9.99 us -> 12.7 us  [exchange(): lax.all_to_all(blocks, 'mp', split_axis=0, concat_axis=0, axis_index_grou...]
  transfers between devices with their start and end apart: 8 -> 8, of which waited for: 4 -> 4; matrix products, arithmetic and copies ran while one was open for 3% -> 2% of each run, Pallas kernels for 4% -> 4%
where the time goes in v14:
time: 156 us; the launch traced here: 155 us
  blocking collectives  61.6 us (39%)
  starting transfers between devices  33.7 us (22%)
  waiting for transfers between devices  28.4 us (18%)
  between operations  13.5 us (9%)
  Pallas kernels  10.5 us (7%)
  local copies, waits for them, and re-layouts  3.75 us (2%)
  other arithmetic  3.45 us (2%)
    all_to_all x1, blocking collectives, near_rows(): return lax.all_to_all(copies, 'mp', split_axis=0, concat_axis=0, tiled=True)  48.9 us
    all_to_all x1, starting transfers between devices, request(): return lax.all_to_all(asked, 'dp', split_axis=0, concat_axis=0, tiled=True)  14 us
    all_to_all x1, waiting for transfers between devices, exchange(): lax.all_to_all(blocks, 'mp', split_axis=0, concat_axis=0, axis_index_grou...  12.7 us
    all_to_all x1, blocking collectives, exchange(): lax.all_to_all(blocks, 'mp', split_axis=0, concat_axis=0, axis_index_grou...  12.7 us
    ppermute x3, starting transfers between devices, far_blocks(): blocks.append(lax.ppermute(moved, 'dp', pairs))  9.66 us
    all_to_all x1, waiting for transfers between devices, request(): return lax.all_to_all(asked, 'dp', split_axis=0, concat_axis=0, tiled=True)  8.04 us
    ppermute x3, waiting for transfers between devices, far_blocks(): blocks.append(lax.ppermute(moved, 'dp', pairs))  7.54 us
    all_to_all x1, starting transfers between devices, on_device(): lax.all_to_all(outgoing, 'dp', split_axis=0, concat_axis=0, tiled=True)  5.04 us
  transfers between devices with their start and end apart: 8, of which 4 were waited for; matrix products, arithmetic and copies ran while one was open for 2% of the time, Pallas kernels for 4%

profile of v14, /device:TPU:8, one launch (start us, length us, event | category | flops | bytes accessed | tf_op | source)
XLA Modules:
  0.0 154.8 jit_solution(6859284184628442099)
XLA Ops:
  6.5 0.8 reshape.239
  7.3 0.1 select_reduce_fusion
  7.4 0.7 broadcast_in_dim.79
  8.1 14.0 %all-to-all-start = ((s32[32,1,128]{2,1,0:T(1,128)}), s32[32,1,128]{2,1,0:T(1,128)S(1)}, u32[]{:S(2)}, u32[]{:S(2)}) async-start(s32[32,1,128]{2,1,0:T(1,128)} %broadcast_in_dim.79), calls=%async_computation | async-start | bytes 32768 | tf_op jit(solution)/shard_map/all_to_all | solution.py:128
  22.1 0.8 dynamic-slice_bitcast_fusion.3
  22.9 8.0 %all-to-all-done = s32[32,1,128]{2,1,0:T(1,128)S(1)} async-done(((s32[32,1,128]{2,1,0:T(1,128)}), s32[32,1,128]{2,1,0:T(1,128)S(1)}, u32[]{:S(2)}, u32[]{:S(2)}) %all-to-all-start) | async-done | bytes 16416 | tf_op jit(solution)/shard_map/all_to_all | solution.py:128
  30.9 0.1 compare_reduce_fusion.2
  31.0 1.0 select_select_fusion
  32.0 5.0 %all-to-all-start.1 = ((bf16[32,8,896]{2,1,0:T(8,128)(2,1)}), bf16[32,8,896]{2,1,0:T(8,128)(2,1)S(1)}, u32[]{:S(2)}, u32[]{:S(2)}) async-start(bf16[32,8,896]{2,1,0:T(8,128)(2,1)} %select_select_fusion), calls=%async_computation.1 | async-start | bytes 917504 | tf_op jit(solution)/shard_map/all_to_all | solution.py:211
  37.1 0.0 all-gather.3.cloned.1.call-start
  37.1 1.6 %collective-permute-start = (bf16[256,256]{1,0:T(8,128)(2,1)}, bf16[256,256]{1,0:T(8,128)(2,1)S(1)}, u32[]{:S(2)}, u32[]{:S(2)}) collective-permute-start(bf16[256,256]{1,0:T(8,128)(2,1)} %param.10), channel_id=1, source_target_pairs={{0,0},{1,16},{2,32},{3,48},{4,4},{5,20},{6,36},{7,52},{8,8},{9,24}... | collective-permute-start | bytes 393224 | tf_op jit(solution)/shard_map/ppermute | solution.py:35
  38.7 0.0 collective-permute-done
  38.7 3.4 %collective-permute-start.3 = (bf16[256,256]{1,0:T(8,128)(2,1)S(1)}, bf16[256,256]{1,0:T(8,128)(2,1)S(1)}, u32[]{:S(2)}, u32[]{:S(2)}) collective-permute-start(bf16[256,256]{1,0:T(8,128)(2,1)S(1)} %collective-permute-done), channel_id=1, source_target_pairs={{0,384},{16,400},{32,416},{48,432},{64,448},{80,464},{96,480},{112... | collective-permute-start | bytes 393224 | tf_op jit(solution)/shard_map/ppermute | solution.py:43
  42.1 4.3 %collective-permute-start.1 = (bf16[256,256]{1,0:T(8,128)(2,1)S(1)}, bf16[256,256]{1,0:T(8,128)(2,1)S(1)}, u32[]{:S(2)}, u32[]{:S(2)}) collective-permute-start(bf16[256,256]{1,0:T(8,128)(2,1)S(1)} %collective-permute-done), channel_id=1, source_target_pairs={{0,128},{16,144},{32,160},{48,176},{64,192},{80,208},{96,224},{112... | collective-permute-start | bytes 393224 | tf_op jit(solution)/shard_map/ppermute | solution.py:43
  46.5 1.9 %collective-permute-start.2 = (bf16[256,256]{1,0:T(8,128)(2,1)S(1)}, bf16[256,256]{1,0:T(8,128)(2,1)S(1)}, u32[]{:S(2)}, u32[]{:S(2)}) collective-permute-start(bf16[256,256]{1,0:T(8,128)(2,1)S(1)} %collective-permute-done), channel_id=1, source_target_pairs={{0,256},{16,272},{32,288},{48,304},{64,320},{80,336},{96,352},{112... | collective-permute-start | bytes 393224 | tf_op jit(solution)/shard_map/ppermute | solution.py:43
  48.4 3.1 %collective-permute-done.3 = bf16[256,256]{1,0:T(8,128)(2,1)S(1)} collective-permute-done((bf16[256,256]{1,0:T(8,128)(2,1)S(1)}, bf16[256,256]{1,0:T(8,128)(2,1)S(1)}, u32[]{:S(2)}, u32[]{:S(2)}) %collective-permute-start.3) | collective-permute-done | bytes 131104 | tf_op jit(solution)/shard_map/ppermute | solution.py:43
  51.5 0.0 collective-permute-done.1
  51.5 4.5 %collective-permute-done.2 = bf16[256,256]{1,0:T(8,128)(2,1)S(1)} collective-permute-done((bf16[256,256]{1,0:T(8,128)(2,1)S(1)}, bf16[256,256]{1,0:T(8,128)(2,1)S(1)}, u32[]{:S(2)}, u32[]{:S(2)}) %collective-permute-start.2) | collective-permute-done | bytes 131104 | tf_op jit(solution)/shard_map/ppermute | solution.py:43
  55.9 0.9 pad_maximum_fusion
  56.8 0.0 all-to-all-done.1.blocks_ref
  56.8 0.0 copy-start
  56.8 0.0 all-gather.3.cloned.1.call-update
  56.8 0.8 reshape.244
  57.6 0.6 add_select_fusion.indices_ref
  58.2 0.0 copy-done
  58.2 2.0 %pick.1 = bf16[16,4,8,896]{3,2,1,0:T(8,128)(2,1)} custom-call(s32[4,1]{1,0:T(4,128)} %add_select_fusion.indices_ref, bf16[32,8,896]{2,1,0:T(8,128)(2,1)} %copy-done), custom_call_target="tpu_custom_call" | custom-call | tf_op jit(solution)/shard_map/pick/pallas_call | solution.py:108
  60.2 48.9 %all_to_all.29.rows_ref = bf16[16,4,8,896]{3,2,1,0:T(8,128)(2,1)} all-to-all(bf16[16,4,8,896]{3,2,1,0:T(8,128)(2,1)} %pick.1), channel_id=1, replica_groups=mesh['dp'=32,'mp'=16] {'mp'}, dimensions={0} | all-to-all | bytes 1835008 | tf_op jit(solution)/shard_map/all_to_all | solution.py:149
  109.2 4.0 %attend.1 = bf16[4,128,256]{2,1,0:T(8,128)(2,1)} custom-call(bf16[16,4,8,896]{3,2,1,0:T(8,128)(2,1)} %all_to_all.29.rows_ref, bf16[128,256]{1,0:T(8,128)(2,1)} %queries_ref.1, bf16[896,256]{1,0:T(8,128)(2,1)} %key_ref.1, bf16[896,256]{1,0:T(8,128)(2,1)} %value_ref.1), custom_call_target="tpu_custom_call" | custom-call | flops 469762048 | bytes 2097152 | tf_op jit(solution)/shard_map/attend/pallas_call | solution.py:192
  113.1 3.4 %all-to-all-start.3 = ((bf16[4,128,256]{2,1,0:T(8,128)(2,1)}), bf16[4,128,256]{2,1,0:T(8,128)(2,1)S(1)}, u32[]{:S(2)}, u32[]{:S(2)}) async-start(bf16[4,128,256]{2,1,0:T(8,128)(2,1)} %attend.1), calls=%async_computation.3 | async-start | bytes 524288 | tf_op jit(solution)/shard_map/all_to_all | solution.py:54
  116.5 12.7 %all-to-all-done.3.attended_ref = bf16[4,128,256]{2,1,0:T(8,128)(2,1)S(1)} async-done(((bf16[4,128,256]{2,1,0:T(8,128)(2,1)}), bf16[4,128,256]{2,1,0:T(8,128)(2,1)S(1)}, u32[]{:S(2)}, u32[]{:S(2)}) %all-to-all-start.3) | async-done | bytes 262176 | tf_op jit(solution)/shard_map/all_to_all | solution.py:54
  129.3 0.0 copy-start.1
  129.3 0.0 all-gather.3.cloned.1.call-done
  129.3 0.7 copy-done.1
  130.0 4.5 %partial_products.1 = bf16[4,128,512]{2,1,0:T(8,128)(2,1)} custom-call(s32[1]{0:T(128)} %bitcast.far_ref, bf16[4,128,256]{2,1,0:T(8,128)(2,1)} %copy-done.1, bf16[2,4,4,256,256]{4,3,2,1,0:T(8,128)(2,1)} %bitcast.16), custom_call_target="tpu_custom_call" | custom-call | flops 536870912 | bytes 4194304 | tf_op jit(solution)/shard_map/partial_products/pallas_call | solution.py:75
  134.5 12.7 %all_to_all.30 = bf16[4,128,512]{2,1,0:T(8,128)(2,1)S(1)} all-to-all(bf16[4,128,512]{2,1,0:T(8,128)(2,1)} %partial_products.1), channel_id=1, replica_groups={{0,4,8,12},{1,5,9,13},{2,6,10,14},{3,7,11,15},{16,20,24,28},{17,21,25,2..., dimensions={0} | all-to-all | bytes 1048576 | tf_op jit(solution)/shard_map/all_to_all | solution.py:54
  147.2 0.7 reduce_sum.22
  (1 shorter events, 0.0 us)
Async XLA Ops:
  8.1 22.8 %all-to-all-start = ((s32[32,1,128]{2,1,0:T(1,128)}), s32[32,1,128]{2,1,0:T(1,128)S(1)}, u32[]{:S(2)}, u32[]{:S(2)}) async-start(s32[32,1,128]{2,1,0:T(1,128)} %broadcast_in_dim.79), calls=%async_computation | async-start | bytes 32768 | tf_op jit(solution)/shard_map/all_to_all | solution.py:128
  32.0 24.8 %all-to-all-start.1 = ((bf16[32,8,896]{2,1,0:T(8,128)(2,1)}), bf16[32,8,896]{2,1,0:T(8,128)(2,1)S(1)}, u32[]{:S(2)}, u32[]{:S(2)}) async-start(bf16[32,8,896]{2,1,0:T(8,128)(2,1)} %select_select_fusion), calls=%async_computation.1 | async-start | bytes 917504 | tf_op jit(solution)/shard_map/all_to_all | solution.py:211
  37.1 92.2 %all-gather.3.cloned.1.call-start = ((), (), s32[]{:S(2)}) async-start(), calls=%async_computation.5 | async-start | bytes 4718592 | tf_op jit(solution)/shard_map/all_gather | solution.py:50
  37.1 1.6 %collective-permute-start = (bf16[256,256]{1,0:T(8,128)(2,1)}, bf16[256,256]{1,0:T(8,128)(2,1)S(1)}, u32[]{:S(2)}, u32[]{:S(2)}) collective-permute-start(bf16[256,256]{1,0:T(8,128)(2,1)} %param.10), channel_id=1, source_target_pairs={{0,0},{1,16},{2,32},{3,48},{4,4},{5,20},{6,36},{7,52},{8,8},{9,24}... | collective-permute-start | bytes 393224 | tf_op jit(solution)/shard_map/ppermute | solution.py:35
  38.7 12.8 %collective-permute-start.3 = (bf16[256,256]{1,0:T(8,128)(2,1)S(1)}, bf16[256,256]{1,0:T(8,128)(2,1)S(1)}, u32[]{:S(2)}, u32[]{:S(2)}) collective-permute-start(bf16[256,256]{1,0:T(8,128)(2,1)S(1)} %collective-permute-done), channel_id=1, source_target_pairs={{0,384},{16,400},{32,416},{48,432},{64,448},{80,464},{96,480},{112... | collective-permute-start | bytes 393224 | tf_op jit(solution)/shard_map/ppermute | solution.py:43
  42.1 9.3 %collective-permute-start.1 = (bf16[256,256]{1,0:T(8,128)(2,1)S(1)}, bf16[256,256]{1,0:T(8,128)(2,1)S(1)}, u32[]{:S(2)}, u32[]{:S(2)}) collective-permute-start(bf16[256,256]{1,0:T(8,128)(2,1)S(1)} %collective-permute-done), channel_id=1, source_target_pairs={{0,128},{16,144},{32,160},{48,176},{64,192},{80,208},{96,224},{112... | collective-permute-start | bytes 393224 | tf_op jit(solution)/shard_map/ppermute | solution.py:43
  46.5 9.5 %collective-permute-start.2 = (bf16[256,256]{1,0:T(8,128)(2,1)S(1)}, bf16[256,256]{1,0:T(8,128)(2,1)S(1)}, u32[]{:S(2)}, u32[]{:S(2)}) collective-permute-start(bf16[256,256]{1,0:T(8,128)(2,1)S(1)} %collective-permute-done), channel_id=1, source_target_pairs={{0,256},{16,272},{32,288},{48,304},{64,320},{80,336},{96,352},{112... | collective-permute-start | bytes 393224 | tf_op jit(solution)/shard_map/ppermute | solution.py:43
  56.8 1.4 copy-start
  113.1 16.2 %all-to-all-start.3 = ((bf16[4,128,256]{2,1,0:T(8,128)(2,1)}), bf16[4,128,256]{2,1,0:T(8,128)(2,1)S(1)}, u32[]{:S(2)}, u32[]{:S(2)}) async-start(bf16[4,128,256]{2,1,0:T(8,128)(2,1)} %attend.1), calls=%async_computation.3 | async-start | bytes 524288 | tf_op jit(solution)/shard_map/all_to_all | solution.py:54
  129.3 0.7 copy-start.1
Sparse Core Ops, SparseCore 0:
  57.0 71.9 all-gather.2

commit v15 on v12

--- a/solution.py
+++ b/solution.py
@@ -37,11 +37,11 @@
 
 def far_blocks(moved):
     dp_count = lax.axis_size("dp")
-    blocks = [moved]
-    for step in range(1, dp_count // NEAR_DP):
+    blocks = {0: moved}
+    for step in sorted(range(1, dp_count // NEAR_DP), key=lambda k: (k != 2, k)):
         pairs = [(d, d ^ (step * NEAR_DP)) for d in range(dp_count)]
-        blocks.append(lax.ppermute(moved, "dp", pairs))
-    return jnp.stack(blocks)
+        blocks[step] = lax.ppermute(moved, "dp", pairs)
+    return jnp.stack([blocks[k] for k in sorted(blocks)])
 
 
 def near_gather(piece):

time: 152 us -> 152 us (level)
  no operation moved by 1% of the time
where the time goes in v15:
time: 152 us; the launch traced here: 151 us
  blocking collectives  49.9 us (33%)
  starting transfers between devices  36.8 us (24%)
  waiting for transfers between devices  32.5 us (21%)
  between operations  13.5 us (9%)
  Pallas kernels  12.2 us (8%)
  local copies, waits for them, and re-layouts  3.5 us (2%)
  other arithmetic  2.32 us (2%)
    all_to_all x1, blocking collectives, near_rows(): return lax.all_to_all(copies, 'mp', split_axis=0, concat_axis=0, tiled=True)  36.2 us
    all_to_all x1, starting transfers between devices, request(): return lax.all_to_all(asked, 'dp', split_axis=0, concat_axis=0, tiled=True)  17.4 us
    all_to_all x1, blocking collectives, exchange(): lax.all_to_all(blocks, 'mp', split_axis=0, concat_axis=0, axis_index_grou...  13.7 us
    ppermute x3, waiting for transfers between devices, far_blocks(): blocks[step] = lax.ppermute(moved, 'dp', pairs)  12.7 us
    all_to_all x1, waiting for transfers between devices, exchange(): lax.all_to_all(blocks, 'mp', split_axis=0, concat_axis=0, axis_index_grou...  9.89 us
    ppermute x3, starting transfers between devices, far_blocks(): blocks[step] = lax.ppermute(moved, 'dp', pairs)  9.21 us
    all_to_all x1, waiting for transfers between devices, request(): return lax.all_to_all(asked, 'dp', split_axis=0, concat_axis=0, tiled=True)  8.25 us
    all_to_all x1, starting transfers between devices, on_device(): lax.all_to_all(outgoing, 'dp', split_axis=0, concat_axis=0, tiled=True)  5.04 us
  transfers between devices with their start and end apart: 8, of which 6 were waited for; matrix products, arithmetic and copies ran while one was open for 3% of the time, Pallas kernels for 5%

profile of v15, /device:TPU:8, one launch (start us, length us, event | category | flops | bytes accessed | tf_op | source)
XLA Modules:
  0.0 150.7 jit_solution(11146124297740622505)
XLA Ops:
  6.5 0.0 copy-start
  6.5 1.7 %collective-permute-start = (bf16[256,256]{1,0:T(8,128)(2,1)}, bf16[256,256]{1,0:T(8,128)(2,1)S(1)}, u32[]{:S(2)}, u32[]{:S(2)}) collective-permute-start(bf16[256,256]{1,0:T(8,128)(2,1)} %param.10), channel_id=1, source_target_pairs={{0,0},{1,16},{2,32},{3,48},{4,4},{5,20},{6,36},{7,52},{8,8},{9,24}... | collective-permute-start | bytes 393224 | tf_op jit(solution)/shard_map/ppermute | solution.py:35
  8.2 0.8 reshape.211
  9.0 0.1 select_reduce_fusion
  9.1 0.7 broadcast_in_dim.21
  9.8 17.4 %all-to-all-start = ((s32[32,1,128]{2,1,0:T(1,128)}), s32[32,1,128]{2,1,0:T(1,128)S(1)}, u32[]{:S(2)}, u32[]{:S(2)}) async-start(s32[32,1,128]{2,1,0:T(1,128)} %broadcast_in_dim.21), calls=%async_computation | async-start | bytes 32768 | tf_op jit(solution)/shard_map/all_to_all | solution.py:128
  27.2 0.0 copy-done
  27.2 0.6 constant_dynamic-slice_fusion.blocks_ref
  27.9 8.2 %all-to-all-done = s32[32,1,128]{2,1,0:T(1,128)S(1)} async-done(((s32[32,1,128]{2,1,0:T(1,128)}), s32[32,1,128]{2,1,0:T(1,128)S(1)}, u32[]{:S(2)}, u32[]{:S(2)}) %all-to-all-start) | async-done | bytes 16416 | tf_op jit(solution)/shard_map/all_to_all | solution.py:128
  36.1 0.0 copy-start.3
  36.1 0.6 copy-done.3
  36.7 1.8 %pick.2 = bf16[1,32,8,896]{3,2,1,0:T(8,128)(2,1)} custom-call(s32[32,128]{1,0:T(8,128)} %bitcast.16, bf16[4,8,896]{2,1,0:T(8,128)(2,1)} %constant_dynamic-slice_fusion.blocks_ref), custom_call_target="tpu_custom_call" | custom-call | tf_op jit(solution)/shard_map/pick/pallas_call | solution.py:108
  38.5 0.0 collective-permute-done
  38.5 5.0 %all-to-all-start.1 = ((bf16[32,8,896]{2,1,0:T(8,128)(2,1)}), bf16[32,8,896]{2,1,0:T(8,128)(2,1)S(1)}, u32[]{:S(2)}, u32[]{:S(2)}) async-start(bf16[32,8,896]{2,1,0:T(8,128)(2,1)} %bitcast.11), calls=%async_computation.1 | async-start | bytes 917504 | tf_op jit(solution)/shard_map/all_to_all | solution.py:208
  43.5 0.0 all-gather.3.cloned.1.call-start
  43.5 2.2 %collective-permute-start.1 = (bf16[256,256]{1,0:T(8,128)(2,1)S(1)}, bf16[256,256]{1,0:T(8,128)(2,1)S(1)}, u32[]{:S(2)}, u32[]{:S(2)}) collective-permute-start(bf16[256,256]{1,0:T(8,128)(2,1)S(1)} %collective-permute-done), channel_id=1, source_target_pairs={{0,128},{16,144},{32,160},{48,176},{64,192},{80,208},{96,224},{112... | collective-permute-start | bytes 393224 | tf_op jit(solution)/shard_map/ppermute | solution.py:43
  45.8 4.6 %collective-permute-start.2 = (bf16[256,256]{1,0:T(8,128)(2,1)S(1)}, bf16[256,256]{1,0:T(8,128)(2,1)S(1)}, u32[]{:S(2)}, u32[]{:S(2)}) collective-permute-start(bf16[256,256]{1,0:T(8,128)(2,1)S(1)} %collective-permute-done), channel_id=1, source_target_pairs={{0,256},{16,272},{32,288},{48,304},{64,320},{80,336},{96,352},{112... | collective-permute-start | bytes 393224 | tf_op jit(solution)/shard_map/ppermute | solution.py:43
  50.4 2.4 %collective-permute-start.3 = (bf16[256,256]{1,0:T(8,128)(2,1)S(1)}, bf16[256,256]{1,0:T(8,128)(2,1)S(1)}, u32[]{:S(2)}, u32[]{:S(2)}) collective-permute-start(bf16[256,256]{1,0:T(8,128)(2,1)S(1)} %collective-permute-done), channel_id=1, source_target_pairs={{0,384},{16,400},{32,416},{48,432},{64,448},{80,464},{96,480},{112... | collective-permute-start | bytes 393224 | tf_op jit(solution)/shard_map/ppermute | solution.py:43
  52.8 2.8 %collective-permute-done.1 = bf16[256,256]{1,0:T(8,128)(2,1)S(1)} collective-permute-done((bf16[256,256]{1,0:T(8,128)(2,1)S(1)}, bf16[256,256]{1,0:T(8,128)(2,1)S(1)}, u32[]{:S(2)}, u32[]{:S(2)}) %collective-permute-start.1) | collective-permute-done | bytes 131104 | tf_op jit(solution)/shard_map/ppermute | solution.py:43
  55.5 5.8 %collective-permute-done.2 = bf16[256,256]{1,0:T(8,128)(2,1)S(1)} collective-permute-done((bf16[256,256]{1,0:T(8,128)(2,1)S(1)}, bf16[256,256]{1,0:T(8,128)(2,1)S(1)}, u32[]{:S(2)}, u32[]{:S(2)}) %collective-permute-start.2) | collective-permute-done | bytes 131104 | tf_op jit(solution)/shard_map/ppermute | solution.py:43
  61.4 4.1 %collective-permute-done.3 = bf16[256,256]{1,0:T(8,128)(2,1)S(1)} collective-permute-done((bf16[256,256]{1,0:T(8,128)(2,1)S(1)}, bf16[256,256]{1,0:T(8,128)(2,1)S(1)}, u32[]{:S(2)}, u32[]{:S(2)}) %collective-permute-start.3) | collective-permute-done | bytes 131104 | tf_op jit(solution)/shard_map/ppermute | solution.py:43
  65.4 0.9 pad_maximum_fusion
  66.3 0.0 all-to-all-done.1.blocks_ref
  66.3 0.0 copy-start.1
  66.3 0.0 all-gather.3.cloned.1.call-update
  66.4 0.8 reshape.216
  67.2 0.6 add_select_fusion.indices_ref
  67.8 0.0 copy-done.1
  67.8 2.0 %pick.3 = bf16[16,4,8,896]{3,2,1,0:T(8,128)(2,1)} custom-call(s32[4,1]{1,0:T(4,128)} %add_select_fusion.indices_ref, bf16[32,8,896]{2,1,0:T(8,128)(2,1)} %copy-done.1), custom_call_target="tpu_custom_call" | custom-call | tf_op jit(solution)/shard_map/pick/pallas_call | solution.py:108
  69.8 36.2 %all_to_all.28.rows_ref = bf16[16,4,8,896]{3,2,1,0:T(8,128)(2,1)} all-to-all(bf16[16,4,8,896]{3,2,1,0:T(8,128)(2,1)} %pick.3), channel_id=1, replica_groups=mesh['dp'=32,'mp'=16] {'mp'}, dimensions={0} | all-to-all | bytes 1835008 | tf_op jit(solution)/shard_map/all_to_all | solution.py:145
  106.0 4.0 %attend.1 = bf16[4,128,256]{2,1,0:T(8,128)(2,1)} custom-call(bf16[16,4,8,896]{3,2,1,0:T(8,128)(2,1)} %all_to_all.28.rows_ref, bf16[128,256]{1,0:T(8,128)(2,1)} %queries_ref.1, bf16[896,256]{1,0:T(8,128)(2,1)} %key_ref.1, bf16[896,256]{1,0:T(8,128)(2,1)} %value_ref.1), custom_call_target="tpu_custom_call" | custom-call | flops 469762048 | bytes 2097152 | tf_op jit(solution)/shard_map/attend/pallas_call | solution.py:188
  109.9 3.4 %all-to-all-start.3 = ((bf16[4,128,256]{2,1,0:T(8,128)(2,1)}), bf16[4,128,256]{2,1,0:T(8,128)(2,1)S(1)}, u32[]{:S(2)}, u32[]{:S(2)}) async-start(bf16[4,128,256]{2,1,0:T(8,128)(2,1)} %attend.1), calls=%async_computation.3 | async-start | bytes 524288 | tf_op jit(solution)/shard_map/all_to_all | solution.py:54
  113.4 9.9 %all-to-all-done.3.attended_ref = bf16[4,128,256]{2,1,0:T(8,128)(2,1)S(1)} async-done(((bf16[4,128,256]{2,1,0:T(8,128)(2,1)}), bf16[4,128,256]{2,1,0:T(8,128)(2,1)S(1)}, u32[]{:S(2)}, u32[]{:S(2)}) %all-to-all-start.3) | async-done | bytes 262176 | tf_op jit(solution)/shard_map/all_to_all | solution.py:54
  123.3 0.0 copy-start.2
  123.3 1.7 %all-gather.3.cloned.1.call-done = bf16[32,256,256]{2,1,0:T(8,128)(2,1)} async-done(((bf16[4,256,256]{2,1,0:T(8,128)(2,1)}), bf16[32,256,256]{2,1,0:T(8,128)(2,1)}) %all-gather.3.cloned.1.call-update) | async-done | bytes 4194320 | tf_op jit(solution)/shard_map/all_gather | solution.py:50
  125.0 0.0 copy-done.2
  125.0 4.5 %partial_products.1 = bf16[4,128,512]{2,1,0:T(8,128)(2,1)} custom-call(s32[1]{0:T(128)} %bitcast.far_ref, bf16[4,128,256]{2,1,0:T(8,128)(2,1)} %copy-done.2, bf16[2,4,4,256,256]{4,3,2,1,0:T(8,128)(2,1)} %bitcast.10), custom_call_target="tpu_custom_call" | custom-call | flops 536870912 | bytes 4194304 | tf_op jit(solution)/shard_map/partial_products/pallas_call | solution.py:75
  129.4 13.7 %all_to_all.29 = bf16[4,128,512]{2,1,0:T(8,128)(2,1)S(1)} all-to-all(bf16[4,128,512]{2,1,0:T(8,128)(2,1)} %partial_products.1), channel_id=1, replica_groups={{0,4,8,12},{1,5,9,13},{2,6,10,14},{3,7,11,15},{16,20,24,28},{17,21,25,2..., dimensions={0} | all-to-all | bytes 1048576 | tf_op jit(solution)/shard_map/all_to_all | solution.py:54
  143.2 0.7 reduce_sum.22
  (1 shorter events, 0.0 us)
Async XLA Ops:
  6.5 20.7 %copy-start = (bf16[512,896]{1,0:T(8,128)(2,1)S(1)}, bf16[512,896]{1,0:T(8,128)(2,1)}, u32[]{:S(2)}) copy-start(bf16[512,896]{1,0:T(8,128)(2,1)} %param.7) | copy-start | bytes 2752516
  6.5 31.9 %collective-permute-start = (bf16[256,256]{1,0:T(8,128)(2,1)}, bf16[256,256]{1,0:T(8,128)(2,1)S(1)}, u32[]{:S(2)}, u32[]{:S(2)}) collective-permute-start(bf16[256,256]{1,0:T(8,128)(2,1)} %param.10), channel_id=1, source_target_pairs={{0,0},{1,16},{2,32},{3,48},{4,4},{5,20},{6,36},{7,52},{8,8},{9,24}... | collective-permute-start | bytes 393224 | tf_op jit(solution)/shard_map/ppermute | solution.py:35
  9.8 26.3 %all-to-all-start = ((s32[32,1,128]{2,1,0:T(1,128)}), s32[32,1,128]{2,1,0:T(1,128)S(1)}, u32[]{:S(2)}, u32[]{:S(2)}) async-start(s32[32,1,128]{2,1,0:T(1,128)} %broadcast_in_dim.21), calls=%async_computation | async-start | bytes 32768 | tf_op jit(solution)/shard_map/all_to_all | solution.py:128
  36.1 0.6 copy-start.3
  38.5 27.9 %all-to-all-start.1 = ((bf16[32,8,896]{2,1,0:T(8,128)(2,1)}), bf16[32,8,896]{2,1,0:T(8,128)(2,1)S(1)}, u32[]{:S(2)}, u32[]{:S(2)}) async-start(bf16[32,8,896]{2,1,0:T(8,128)(2,1)} %bitcast.11), calls=%async_computation.1 | async-start | bytes 917504 | tf_op jit(solution)/shard_map/all_to_all | solution.py:208
  43.5 81.5 %all-gather.3.cloned.1.call-start = ((), (), s32[]{:S(2)}) async-start(), calls=%async_computation.5 | async-start | bytes 4718592 | tf_op jit(solution)/shard_map/all_gather | solution.py:50
  43.5 12.0 %collective-permute-start.1 = (bf16[256,256]{1,0:T(8,128)(2,1)S(1)}, bf16[256,256]{1,0:T(8,128)(2,1)S(1)}, u32[]{:S(2)}, u32[]{:S(2)}) collective-permute-start(bf16[256,256]{1,0:T(8,128)(2,1)S(1)} %collective-permute-done), channel_id=1, source_target_pairs={{0,128},{16,144},{32,160},{48,176},{64,192},{80,208},{96,224},{112... | collective-permute-start | bytes 393224 | tf_op jit(solution)/shard_map/ppermute | solution.py:43
  45.8 15.6 %collective-permute-start.2 = (bf16[256,256]{1,0:T(8,128)(2,1)S(1)}, bf16[256,256]{1,0:T(8,128)(2,1)S(1)}, u32[]{:S(2)}, u32[]{:S(2)}) collective-permute-start(bf16[256,256]{1,0:T(8,128)(2,1)S(1)} %collective-permute-done), channel_id=1, source_target_pairs={{0,256},{16,272},{32,288},{48,304},{64,320},{80,336},{96,352},{112... | collective-permute-start | bytes 393224 | tf_op jit(solution)/shard_map/ppermute | solution.py:43
  50.4 15.1 %collective-permute-start.3 = (bf16[256,256]{1,0:T(8,128)(2,1)S(1)}, bf16[256,256]{1,0:T(8,128)(2,1)S(1)}, u32[]{:S(2)}, u32[]{:S(2)}) collective-permute-start(bf16[256,256]{1,0:T(8,128)(2,1)S(1)} %collective-permute-done), channel_id=1, source_target_pairs={{0,384},{16,400},{32,416},{48,432},{64,448},{80,464},{96,480},{112... | collective-permute-start | bytes 393224 | tf_op jit(solution)/shard_map/ppermute | solution.py:43
  66.3 1.4 copy-start.1
  109.9 13.3 %all-to-all-start.3 = ((bf16[4,128,256]{2,1,0:T(8,128)(2,1)}), bf16[4,128,256]{2,1,0:T(8,128)(2,1)S(1)}, u32[]{:S(2)}, u32[]{:S(2)}) async-start(bf16[4,128,256]{2,1,0:T(8,128)(2,1)} %attend.1), calls=%async_computation.3 | async-start | bytes 524288 | tf_op jit(solution)/shard_map/all_to_all | solution.py:54
  123.3 1.7 %copy-start.2 = (bf16[4,128,256]{2,1,0:T(8,128)(2,1)}, bf16[4,128,256]{2,1,0:T(8,128)(2,1)S(1)}, u32[]{:S(2)}) copy-start(bf16[4,128,256]{2,1,0:T(8,128)(2,1)S(1)} %all-to-all-done.3.attended_ref) | copy-start | bytes 786436
Sparse Core Ops, SparseCore 0:
  66.5 58.4 all-gather.2
